TPU v7x, 128 devices: a whole 4x4x4 slice. The times are simulated.
128 devices in a mesh: comp: 16 (over x_lo, y, core), pair: 8 (over z, x_hi).
Axes of the slice: x: 4 (x_hi: 2, x_lo: 2; x = x_hi * 2 + x_lo), y: 4, z: 4, core: 2. Of those that a mesh axis runs over, the one named last changes fastest.
Arguments:
- densities: bfloat16 [8192, 65536], P('comp', 'pair'), may hold values from -6 to 6
- coulomb: float32 [8192], replicated, may hold values from 3.314563e-05 to 0.003314563
- pair_list: int32 [1024, 2], P(('comp', 'pair')), may hold values from 0 to 4095
- valence_energy: float32 [4096], replicated, may hold values from -20 to -0.5, as said below
- conduction_energy: float32 [4096], replicated, may hold values from 0.5 to 12, as said below
- tile_mask: int32 [512, 16], P(('pair', 'comp')), may hold values 0 or 1
Outputs:
- kernel: float32 [65536, 1024], P(('pair', 'comp'))
Inputs may be any that keep to these rules, and one draw needn't show every extreme that they name: `valence_energy`: energies in electronvolts. `conduction_energy`: energies in electronvolts.
All inputs are finite; a program needn't handle non-finite values. No bound on the sum of `tile_mask` on one device may be relied on, other than what follows from the above.
Results may differ from a plain program's by a relative error of at most 0.0025.
Values may be sent and summed in bfloat16 or wider, within the bound.
No kernel may reach another device: no remote copies, remote signals or barrier semaphores. Data moves between devices by JAX's collectives and lax.ppermute only.
A program may use at most 128 MiB of HBM per device.

v0:
```python
import jax
import jax.numpy as jnp
from jax import lax
from jax.sharding import PartitionSpec as P

TILE = 128


def per_device(densities, coulomb, pair_list, valence_energy, conduction_energy, tile_mask):
    comp_count = lax.axis_size("comp")
    pair_count = lax.axis_size("pair")
    comp_index = lax.axis_index("comp")
    pair_index = lax.axis_index("pair")
    block_len = densities.shape[0]
    pair_dev = densities.shape[1] // comp_count
    row_dev = pair_list.shape[0]
    window = row_dev * comp_count * pair_count
    weights = lax.dynamic_slice_in_dim(coulomb, comp_index * block_len, block_len)
    picked = densities.reshape(block_len, comp_count, pair_dev)[:, :, :row_dev]
    local_panel = (jnp.transpose(picked, (1, 2, 0)).astype(jnp.float32) * weights).astype(
        jnp.bfloat16
    )
    gathered = lax.all_gather(local_panel, "pair", axis=1, tiled=True)
    panel = gathered.reshape(window, block_len)
    exchange = lax.psum_scatter(
        lax.dot_general(
            densities, panel, (((0,), (1,)), ((), ())), preferred_element_type=jnp.float32
        ),
        "comp",
        scatter_dimension=0,
        tiled=True,
    )
    masked = (
        exchange.reshape(pair_dev // TILE, TILE, comp_count, window // comp_count)
        * tile_mask.astype(jnp.float32)[:, None, :, None]
    )
    masked = 2.0 * masked.reshape(pair_dev, window)
    table = jnp.arange(valence_energy.shape[0], dtype=jnp.int32)
    cond_hits = pair_list[:, 1][:, None] == table[None, :]
    val_hits = pair_list[:, 0][:, None] == table[None, :]
    energy = jnp.sum(jnp.where(cond_hits, conduction_energy[None, :], 0.0), axis=1) - jnp.sum(
        jnp.where(val_hits, valence_energy[None, :], 0.0), axis=1
    )
    diag_block = jnp.eye(row_dev, dtype=jnp.float32) * energy[None, :]
    start = (comp_index * pair_count + pair_index) * row_dev
    placed = lax.dynamic_update_slice(
        jnp.zeros((pair_dev, window), jnp.float32), diag_block, (jnp.int32(0), start)
    )
    return masked + placed


def solution(mesh):
    return jax.shard_map(
        per_device,
        mesh=mesh,
        in_specs=(
            P("comp", "pair"),
            P(),
            P(("comp", "pair"), None),
            P(),
            P(),
            P(("pair", "comp"), None),
        ),
        out_specs=P(("pair", "comp"), None),
        check_vma=False,
    )
```

profile of v0, /device:TPU:1, one launch (start us, length us, event | category | flops | bytes accessed | tf_op | source)
XLA Modules:
  0.0 278.1 jit_solution(5608610415269672751)
XLA Ops:
  6.5 0.0 all-gather.2.cloned.1.call-start
  6.5 12.0 %copy.12 = bf16[512,8192]{0,1:T(8,128)(2,1)} copy(bf16[512,8192]{1,0:T(8,128)(2,1)} %param.6) | data formatting | bytes 16777216 | tf_op args[0]
  18.5 0.8 dynamic_slice.3
  19.3 1.6 fusion.1
  20.9 0.0 all-gather.2.cloned.1.call-update
  20.9 0.0 reduce-scatter.2.cloned.1.call-start
  20.9 47.9 %all-gather.2.cloned.1.call-done = bf16[16,64,512]{2,1,0:T(8,128)(2,1)} async-done(((bf16[16,8,512]{2,1,0:T(8,128)(2,1)}), bf16[16,64,512]{2,1,0:T(8,128)(2,1)}) %all-gather.2.cloned.1.call-update) | async-done | bytes 1048592 | tf_op jit(solution)/shard_map/all_gather | solution.py:23
  68.9 17.7 %convolution_bitcast_fusion = f32[8192,1024]{0,1:T(8,128)} fusion(bf16[1024,512]{1,0:T(8,128)(2,1)} %bitcast.22, bf16[512,8192]{1,0:T(8,128)(2,1)} %param.6), kind=kOutput, calls=%fused_computation | convolution fusion | flops 8589934592 | bytes 42991616 | tf_op jit(solution)/shard_map/dot_general | solution.py:26
  86.6 0.0 copy-start.3
  86.6 0.0 copy-start.4
  86.6 0.0 copy-start.1
  86.6 0.0 copy-start.2
  86.6 0.0 reduce-scatter.2.cloned.1.call-update
  86.7 0.6 copy-done.3
  87.3 0.1 copy.13
  87.4 0.0 copy-done.4
  87.4 0.0 copy-done.1
  87.4 0.0 copy-done.2
  87.4 0.2 select_reduce_fusion
  87.7 179.2 %reduce-scatter.2.cloned.1.call-done = f32[512,1024]{0,1:T(8,128)} async-done(((f32[8192,1024]{0,1:T(8,128)}), f32[512,1024]{0,1:T(8,128)}) %reduce-scatter.2.cloned.1.call-update) | async-done | bytes 2097168 | tf_op jit(solution)/shard_map/reduce_scatter | solution.py:25
  266.9 0.0 copy-start
  266.9 0.3 mul.48
  267.2 1.2 copy-done
  268.4 0.5 fusion
  268.9 0.1 select_add_fusion
  269.0 0.5 add.18
  269.5 1.8 copy.14
  (3 shorter events, 0.0 us)
Async XLA Ops:
  6.5 62.3 %all-gather.2.cloned.1.call-start = ((), (), s32[]{:S(2)}) async-start(), calls=%async_computation.1 | async-start | bytes 1179648 | tf_op jit(solution)/shard_map/all_gather | solution.py:23
  20.9 246.0 %reduce-scatter.2.cloned.1.call-start = ((), (), s32[]{:S(2)}) async-start(), calls=%async_computation.2 | async-start | bytes 35651584 | tf_op jit(solution)/shard_map/reduce_scatter | solution.py:25
  86.6 0.7 copy-start.3
  86.6 0.8 copy-start.4
  86.6 0.8 copy-start.1
  86.6 0.8 copy-start.2
  266.9 1.6 copy-start
Sparse Core Ops, SparseCore 0:
  21.0 47.8 all-gather.1
  86.8 180.0 reduce-scatter.1
where the time goes:
time: 279 us; the launch traced here: 278 us
  waiting for transfers between devices  227 us (81%)
  matrix products  17.7 us (6%)
  local copies, waits for them, and re-layouts  17.3 us (6%)
  between operations  13.5 us (5%)
    reduce_scatter x1, waiting for transfers between devices, per_device(): lax.psum_scatter(lax.dot_general(densities, panel, (((0,), (1,)), ((), ()...  179 us
    all_gather x1, waiting for transfers between devices, per_device(): gathered = lax.all_gather(local_panel, 'pair', axis=1, tiled=True)  47.9 us
    dot_general x1, matrix products, per_device(): lax.dot_general(densities, panel, (((0,), (1,)), ((), ())), preferred_ele...  17.7 us
    unnamed x11, local copies, waits for them, and re-layouts  13.9 us
  transfers between devices with their start and end apart: 2, of which 2 were waited for; matrix products, arithmetic and copies ran while one was open for 0% of the time, Pallas kernels for 0%

commit v1 on v0

v1 whole, which is shorter than its diff:
```python
import functools

import jax
import jax.numpy as jnp
from jax import lax
from jax.experimental import pallas as pl
from jax.experimental.pallas import tpu as pltpu
from jax.sharding import PartitionSpec as P

TILE = 128
NX, NY, NC = 2, 4, 2
NZ, NH = 4, 2
N_COMP, N_PAIR = NX * NY * NC, NZ * NH
QB = 512
F32, BF16 = jnp.float32, jnp.bfloat16


def comp_at(x, y, k):
    return ((x % NX) * NY + y % NY) * NC + k % NC


def comp_perm(move):
    out = []
    for c in range(N_COMP):
        x, y, k = c // (NY * NC), (c // NC) % NY, c % NC
        out.append((c, comp_at(*move(x, y, k))))
    return out


CORE = comp_perm(lambda x, y, k: (x, y, k + 1))
XSWAP = comp_perm(lambda x, y, k: (x + 1, y, k))
XCROSS = comp_perm(lambda x, y, k: (x + 1, y, k + 1))
AHEAD = comp_perm(lambda x, y, k: (x, y + 1 - 2 * k, k))
BEHIND = comp_perm(lambda x, y, k: (x, y - 1 + 2 * k, k))
HALF = [(p, p ^ 1) for p in range(N_PAIR)]
ZSPLIT = [
    (c * N_PAIR + p, c * N_PAIR + ((p // NH + 1 - 2 * (c % NC)) % NZ) * NH + p % NH)
    for c in range(N_COMP)
    for p in range(N_PAIR)
]


def step_sign(b):
    return 1 - 2 * b[2]


def block_of(b, other_x, dy):
    x = 1 - b[0] if other_x else b[0]
    return (x * NY + ((b[1] + dy * step_sign(b) + NY) % NY)) * NC


def pick_kernel(b, *refs):
    blocks, (w_ref, o_ref) = refs[:-2], refs[-2:]
    sel = (
        lax.broadcasted_iota(jnp.int32, (8, 128), 0)
        == lax.broadcasted_iota(jnp.int32, (8, 128), 1)
    ).astype(BF16)
    for n, blk in enumerate(blocks):
        rows = lax.dot_general(
            sel, blk[...], (((1,), (1,)), ((), ())), preferred_element_type=F32
        )
        o_ref[8 * n : 8 * n + 8, :] = (rows * w_ref[0]).astype(BF16)


def pick(b, dens, coulomb):
    k = dens.shape[0]
    per = 4
    return pl.pallas_call(
        pick_kernel,
        grid_spec=pltpu.PrefetchScalarGridSpec(
            num_scalar_prefetch=1,
            grid=(N_COMP // per,),
            in_specs=[
                pl.BlockSpec((k, 128), lambda i, b, n=n: (0, (i * per + n) * (QB // 128)))
                for n in range(per)
            ]
            + [pl.BlockSpec((1, 1, k), lambda i, b: (b[3], 0, 0))],
            out_specs=pl.BlockSpec((8 * per, k), lambda i, b: (i, 0)),
        ),
        out_shape=jax.ShapeDtypeStruct((8 * N_COMP, k), BF16),
        name="pick",
    )(b, *([dens] * per), coulomb.reshape(N_COMP, 1, k))


def mm_kernel(parts, n_add, b, *refs):
    panels = refs[: 2 * parts]
    own, oth = refs[2 * parts : 2 * parts + 2]
    adds = refs[2 * parts + 2 : 2 * parts + 2 + n_add]
    o_ref = refs[-1]
    rows = panels[0].shape[0]
    for n in range(parts):
        acc = jnp.dot(panels[2 * n][...], own[...], preferred_element_type=F32)
        acc += jnp.dot(panels[2 * n + 1][...], oth[...], preferred_element_type=F32)
        at = slice(n * rows, (n + 1) * rows)
        for a in adds:
            acc += a[0, at, :].astype(F32)
        o_ref[0, at, :] = acc.astype(o_ref.dtype)


def mm(name, b, groups, dens, n, column, adds=(), dtype=BF16):
    own, oth = dens
    k = own.shape[0]
    rows = groups[0][0].shape[0]
    total = rows * len(groups)
    flat = [piece for pair in groups for piece in pair]
    return pl.pallas_call(
        functools.partial(mm_kernel, len(groups), len(adds)),
        grid_spec=pltpu.PrefetchScalarGridSpec(
            num_scalar_prefetch=1,
            grid=(n,),
            in_specs=[pl.BlockSpec((rows, k), lambda i, b: (0, 0)) for _ in flat]
            + [pl.BlockSpec((k, QB), lambda i, b: (0, column(i, b)))] * 2
            + [
                pl.BlockSpec((1, total, QB), lambda i, b, slot=slot: (slot(i, b), 0, 0))
                for _, slot in adds
            ],
            out_specs=pl.BlockSpec((1, total, QB), lambda i, b: (i, 0, 0)),
        ),
        out_shape=jax.ShapeDtypeStruct((n, total, QB), dtype),
        cost_estimate=pl.CostEstimate(
            flops=4 * n * total * k * QB,
            bytes_accessed=n * 4 * k * QB + n * total * QB * (2 + 2 * len(adds)),
            transcendentals=0,
        ),
        name=name,
    )(b, *flat, own, oth, *[a for a, _ in adds])


def final_kernel(b, mask, xo, xr, yo, yr, fo, fr, diag, o_ref, t_ref):
    z, half, core = b[4], b[5], b[2]

    def pair_at(dz, dh):
        return ((z + dz + NZ) % NZ) * NH + (half + dh) % NH

    def place(value, row, c, p):
        for t in range(QB // TILE):
            scale = (2 * mask[t, c]).astype(F32)
            at = pl.ds(pl.multiple_of((c * N_PAIR + p) * 8, 8), 8)
            t_ref[at, t * TILE : (t + 1) * TILE] = value(t) * scale

    order = (((0, 0), (-1, 0), (-1, 1), (-2, 0)), ((0, 1), (1, 1), (1, 0), (2, 1)))
    for source in range(2):
        mine = source == 0
        for g in range(4):
            spots = [pair_at(*order[s][g]) for s in range(2)]
            same = core if mine else 1 - core
            p = jnp.where(same == 0, spots[0], spots[1])
            for c in range(N_COMP):
                row = (g % 2) * 128 + c * 8
                if g < 2:
                    src = xo if mine else xr
                    value = lambda t, src=src, row=row: src[
                        0, row : row + 8, t * TILE : (t + 1) * TILE
                    ]
                else:
                    src, more = (yo, fo) if mine else (yr, fr)
                    value = lambda t, src=src, more=more, row=row: src[
                        0, row : row + 8, t * TILE : (t + 1) * TILE
                    ] + more[0, row : row + 8, t * TILE : (t + 1) * TILE].astype(F32)
                place(value, row, c, p)
    here = pl.ds(pl.multiple_of((b[3] * N_PAIR + pair_at(0, 0)) * 8, 8), 8)
    t_ref[here, 0:TILE] = t_ref[here, 0:TILE] + diag[...]
    o_ref[...] = t_ref[...].T


def final(b, mask, parts, diag):
    window = 8 * N_COMP * N_PAIR
    full = lambda a: pl.BlockSpec(a.shape, lambda i, b, m: (0,) * a.ndim)
    return pl.pallas_call(
        final_kernel,
        grid_spec=pltpu.PrefetchScalarGridSpec(
            num_scalar_prefetch=2,
            grid=(1,),
            in_specs=[full(a) for a in parts] + [full(diag)],
            out_specs=pl.BlockSpec((QB, window), lambda i, b, m: (0, 0)),
            scratch_shapes=[pltpu.VMEM((window, QB), F32)],
        ),
        out_shape=jax.ShapeDtypeStruct((QB, window), F32),
        name="final",
    )(b, mask, *parts, diag)


def energy_tile(pair_list, valence_energy, conduction_energy):
    table = jnp.arange(valence_energy.shape[0], dtype=jnp.int32)
    cond_hits = pair_list[:, 1][:, None] == table[None, :]
    val_hits = pair_list[:, 0][:, None] == table[None, :]
    energy = jnp.sum(jnp.where(cond_hits, conduction_energy[None, :], 0.0), axis=1) - jnp.sum(
        jnp.where(val_hits, valence_energy[None, :], 0.0), axis=1
    )
    return jnp.eye(8, TILE, dtype=F32) * energy[:, None]


def per_device(densities, coulomb, pair_list, valence_energy, conduction_energy, tile_mask):
    comp = lax.axis_index("comp")
    pair = lax.axis_index("pair")
    core = comp % NC
    pos = jnp.arange(8, dtype=jnp.int32)
    facts = (comp // (NY * NC), (comp // NC) % NY, core, comp, pair // NH, pair % NH)
    b = jnp.zeros((8,), jnp.int32)
    for n, fact in enumerate(facts):
        b = jnp.where(pos == n, fact, b)

    swap = lambda a: lax.ppermute(a, "comp", CORE)
    dens = (densities, swap(densities))

    with jax.named_scope("panel"):
        v = pick(b, densities, coulomb)
        hv = lax.ppermute(v, "pair", HALF)
        mine = jnp.stack([v, hv])
        theirs = swap(mine)
        mine = jnp.where(core == 0, mine, mine[::-1])
        theirs = jnp.where(core == 0, theirs, theirs[::-1])
        first = jnp.stack([mine[0], theirs[0]])
        second = jnp.stack([mine[1], theirs[1]])
        zmove = lambda a: lax.ppermute(a, ("comp", "pair"), ZSPLIT)
        near = zmove(first)
        near2 = zmove(second)
        far = zmove(near)
    rows_x = [(first[0], first[1]), (near[0], near[1])]
    rows_y = [(near2[0], near2[1]), (far[0], far[1])]

    def dests(*pairs):
        def column(i, b):
            out = block_of(b, *pairs[-1])
            for n in range(len(pairs) - 2, -1, -1):
                out = jnp.where(i // NC == n, block_of(b, *pairs[n]), out)
            return out + i % NC

        return column

    same = lambda i, b: i
    ahead = lambda a: lax.ppermute(a, "comp", AHEAD)
    behind = lambda a: lax.ppermute(a, "comp", BEHIND)

    with jax.named_scope("x_then_y_send"):
        x1 = mm("x1", b, rows_x, dens, 4, dests((True, 2), (True, -1)))
        x1r = lax.ppermute(x1, "comp", XSWAP)
        x2 = mm("x2", b, rows_x, dens, 4, dests((True, 1), (True, 0)))
        x2r = lax.ppermute(x2, "comp", XSWAP)
    with jax.named_scope("y_then_x"):
        m1y = ahead(mm("m1y", b, rows_y, dens, 4, dests((True, 2), (False, 2))))
        m2y = behind(mm("m2y", b, rows_y, dens, 4, dests((True, -1), (False, -1))))
        m3y = ahead(
            mm("m3y", b, rows_y, dens, 4, dests((True, 1), (False, 1)), [(m1y, same)])
        )
    with jax.named_scope("x_then_y"):
        m1x = ahead(mm("m1x", b, rows_x, dens, 2, dests((False, 2)), [(x1r, same)]))
        m2x = behind(
            mm("m2x", b, rows_x, dens, 2, dests((False, -1)), [(x1r, lambda i, b: i + 2)])
        )
        m3x = ahead(
            mm("m3x", b, rows_x, dens, 2, dests((False, 1)), [(x2r, same), (m1x, same)])
        )

    mine_at = lambda i, b: b[2]
    other_at = lambda i, b: 1 - b[2]

    def at(core_of, base):
        return lambda i, b: base + core_of(i, b)

    def last_x(name, core_of):
        return mm(
            name, b, rows_x, dens, 1,
            lambda i, b: block_of(b, False, 0) + core_of(i, b),
            [(x2r, at(core_of, 2)), (m3x, at(core_of, 0)), (m2x, at(core_of, 0))],
            F32,
        )

    def last_y(name, core_of, other_x, dtype):
        base = 0 if other_x else 2
        return mm(
            name, b, rows_y, dens, 1,
            lambda i, b: block_of(b, other_x, 0) + core_of(i, b),
            [(m3y, at(core_of, base)), (m2y, at(core_of, base))],
            dtype,
        )

    with jax.named_scope("last"):
        fo = lax.ppermute(last_y("yf", mine_at, True, BF16), "comp", XSWAP)
        fr = lax.ppermute(last_y("yg", other_at, True, BF16), "comp", XCROSS)
        yr = swap(last_y("ys", other_at, False, F32))
        yo = last_y("yo", mine_at, False, F32)
        xr = swap(last_x("xs", other_at))
        xo = last_x("xo", mine_at)
        diag = energy_tile(pair_list, valence_energy, conduction_energy)
        return final(b, tile_mask, (xo, xr, yo, yr, fo, fr), diag)


def solution(mesh):
    return jax.shard_map(
        per_device,
        mesh=mesh,
        in_specs=(
            P("comp", "pair"),
            P(),
            P(("comp", "pair"), None),
            P(),
            P(),
            P(("pair", "comp"), None),
        ),
        out_specs=P(("pair", "comp"), None),
        check_vma=False,
    )
```

time: 279 us -> 134 us (0.48)
  waiting for transfers between devices: 227 us -> 21.2 us
  Pallas kernels: 0 us -> 71.2 us
  starting transfers between devices: 0.04 us -> 28.4 us
  matrix products: 17.7 us -> 0 us
  between operations: 13.5 us -> 0.09 us
  local copies, waits for them, and re-layouts: 17.3 us -> 9 us
    reduce_scatter x1 -> x0, waiting for transfers between devices: 179 us -> none  [per_device(): lax.psum_scatter(lax.dot_general(densities, panel, (((0,), (1,)), ((), ()...]
    pallas_call x0 -> x16, Pallas kernels: none -> 71.2 us  [the longest x14 61.7 us: mm(): pl.pallas_call(functools.partial(mm_kernel, len(groups), len(adds)), grid...]
    all_gather x1 -> x0, waiting for transfers between devices: 47.9 us -> none  [per_device(): gathered = lax.all_gather(local_panel, 'pair', axis=1, tiled=True)]
    ppermute x0 -> x18, starting transfers between devices: none -> 28.4 us  [the longest x4 8.77 us: per_device(): ahead = lambda a: lax.ppermute(a, 'comp', AHEAD)]
    ppermute x0 -> x18, waiting for transfers between devices: none -> 21.2 us  [the longest x4 6.83 us: per_device(): ahead = lambda a: lax.ppermute(a, 'comp', AHEAD)]
    dot_general x1 -> x0, matrix products: 17.7 us -> none  [per_device(): lax.dot_general(densities, panel, (((0,), (1,)), ((), ())), preferred_ele...]
    unnamed x11 -> x24, local copies, waits for them, and re-layouts: 13.9 us -> 5.48 us
  transfers between devices with their start and end apart: 2 -> 18, of which waited for: 2 -> 8; matrix products, arithmetic and copies ran while one was open for 0% -> 5% of each run, Pallas kernels for 0% -> 46%
where the time goes in v1:
time: 134 us; the launch traced here: 133 us
  Pallas kernels  71.2 us (53%)
  starting transfers between devices  28.4 us (21%)
  waiting for transfers between devices  21.2 us (16%)
  local copies, waits for them, and re-layouts  9 us (7%)
  other arithmetic  2.53 us (2%)
    pallas_call x14, Pallas kernels, mm(): pl.pallas_call(functools.partial(mm_kernel, len(groups), len(adds)), grid...  61.7 us
    ppermute x4, starting transfers between devices, per_device(): ahead = lambda a: lax.ppermute(a, 'comp', AHEAD)  8.77 us
    ppermute x3, starting transfers between devices, per_device(): zmove = lambda a: lax.ppermute(a, ('comp', 'pair'), ZSPLIT)  7.22 us
    ppermute x4, waiting for transfers between devices, per_device(): ahead = lambda a: lax.ppermute(a, 'comp', AHEAD)  6.83 us
    ppermute x4, starting transfers between devices, per_device(): swap = lambda a: lax.ppermute(a, 'comp', CORE)  5.79 us
    unnamed x24, local copies, waits for them, and re-layouts  5.48 us
    ppermute x3, waiting for transfers between devices, per_device(): zmove = lambda a: lax.ppermute(a, ('comp', 'pair'), ZSPLIT)  4.95 us
    pallas_call x1, Pallas kernels, final(): pl.pallas_call(final_kernel, grid_spec=pltpu.PrefetchScalarGridSpec(num_s...  4.85 us
  transfers between devices with their start and end apart: 18, of which 8 were waited for; matrix products, arithmetic and copies ran while one was open for 5% of the time, Pallas kernels for 46%

profile of v1, /device:TPU:1, one launch (start us, length us, event | category | flops | bytes accessed | tf_op | source)
XLA Modules:
  0.0 132.5 jit_solution(11238822964495149409)
XLA Ops:
  0.0 1.4 %collective-permute-start.3 = (bf16[512,8192]{1,0:T(8,128)(2,1)}, bf16[512,8192]{1,0:T(8,128)(2,1)}, u32[]{:S(2)}, u32[]{:S(2)}) collective-permute-start(bf16[512,8192]{1,0:T(8,128)(2,1)} %refs_4_.27), channel_id=1, source_target_pairs={{0,8},{8,0},{16,24},{24,16},{32,40},{40,32},{48,56},{56,48},{64,72... | collective-permute-start | bytes 25165832 | tf_op jit(solution)/shard_map/ppermute | solution.py:203
  2.0 4.6 %pick.1 = bf16[128,512]{1,0:T(8,128)(2,1)} custom-call(s32[8]{0:T(128)} %compare_select_fusion.5.b, bf16[512,8192]{1,0:T(8,128)(2,1)} %refs_4_.27, bf16[512,8192]{1,0:T(8,128)(2,1)} %refs_4_.27, bf16[512,8192]{1,0:T(8,128)(2,1)} %refs_4_.27, bf16[512,8192]{1,0:T(8,128)(2,1)} %refs_4_.27, f32[16,1,512]{2,1,0:T(1,128)} %bitcast.25), custom_call_target="tpu_custom_call" | custom-call | tf_op jit(solution)/shard_map/panel/pick/pallas_call | solution.py:68
  6.6 2.8 %collective-permute-start = (bf16[128,512]{1,0:T(8,128)(2,1)}, bf16[128,512]{1,0:T(8,128)(2,1)S(1)}, u32[]{:S(2)}, u32[]{:S(2)}) collective-permute-start(bf16[128,512]{1,0:T(8,128)(2,1)} %pick.1), channel_id=1, source_target_pairs={{0,1},{1,0},{2,3},{3,2},{4,5},{5,4},{6,7},{7,6},{8,9},{9,8},{10,11... | collective-permute-start | bytes 393224 | tf_op jit(solution)/shard_map/panel/ppermute | solution.py:208
  9.4 4.0 %collective-permute-done = bf16[128,512]{1,0:T(8,128)(2,1)S(1)} collective-permute-done((bf16[128,512]{1,0:T(8,128)(2,1)}, bf16[128,512]{1,0:T(8,128)(2,1)S(1)}, u32[]{:S(2)}, u32[]{:S(2)}) %collective-permute-start) | collective-permute-done | bytes 131104 | tf_op jit(solution)/shard_map/panel/ppermute | solution.py:208
  17.1 3.9 %collective-permute-start.2 = (bf16[2,128,512]{2,1,0:T(8,128)(2,1)S(1)}, bf16[2,128,512]{2,1,0:T(8,128)(2,1)S(1)}, u32[]{:S(2)}, u32[]{:S(2)}) collective-permute-start(bf16[2,128,512]{2,1,0:T(8,128)(2,1)S(1)} %pad_maximum_fusion.1), channel_id=1, source_target_pairs={{0,2},{1,3},{2,4},{3,5},{4,6},{5,7},{6,0},{7,1},{8,14},{9,15},{10,... | collective-permute-start | bytes 786440 | tf_op jit(solution)/shard_map/panel/ppermute | solution.py:215
  21.3 3.1 %collective-permute-done.2 = bf16[2,128,512]{2,1,0:T(8,128)(2,1)S(1)} collective-permute-done((bf16[2,128,512]{2,1,0:T(8,128)(2,1)S(1)}, bf16[2,128,512]{2,1,0:T(8,128)(2,1)S(1)}, u32[]{:S(2)}, u32[]{:S(2)}) %collective-permute-start.2) | collective-permute-done | bytes 262176 | tf_op jit(solution)/shard_map/panel/ppermute | solution.py:215
  24.4 3.1 %collective-permute-start.11 = (bf16[2,128,512]{2,1,0:T(8,128)(2,1)S(1)}, bf16[2,128,512]{2,1,0:T(8,128)(2,1)S(1)}, u32[]{:S(2)}, u32[]{:S(2)}) collective-permute-start(bf16[2,128,512]{2,1,0:T(8,128)(2,1)S(1)} %collective-permute-done.2), channel_id=1, source_target_pairs={{0,2},{1,3},{2,4},{3,5},{4,6},{5,7},{6,0},{7,1},{8,14},{9,15},{10,... | collective-permute-start | bytes 786440 | tf_op jit(solution)/shard_map/panel/ppermute | solution.py:215
  29.0 1.9 %collective-permute-done.11 = bf16[2,128,512]{2,1,0:T(8,128)(2,1)S(1)} collective-permute-done((bf16[2,128,512]{2,1,0:T(8,128)(2,1)S(1)}, bf16[2,128,512]{2,1,0:T(8,128)(2,1)S(1)}, u32[]{:S(2)}, u32[]{:S(2)}) %collective-permute-start.11) | collective-permute-done | bytes 262176 | tf_op jit(solution)/shard_map/panel/ppermute | solution.py:215
  31.5 5.6 %x1.1 = bf16[4,256,512]{2,1,0:T(8,128)(2,1)} custom-call(s32[8]{0:T(128)} %compare_select_fusion.5.b, bf16[128,512]{1,0:T(8,128)(2,1)} %get-tuple-element.10.refs_0_, bf16[128,512]{1,0:T(8,128)(2,1)} %get-tuple-element.13.refs_1_, bf16[128,512]{1,0:T(8,128)(2,1)} %get-tuple-element.16.refs_2_, bf16[128,512]{1,0:T(8,128)(2,1)} %get-tuple-element.15.refs_3_, ...), custom_call_target="tpu_custom_call" | custom-call | flops 1073741824 | bytes 5242880 | tf_op jit(solution)/shard_map/x_then_y_send/x1/pallas_call | solution.py:106
  37.2 1.2 collective-permute-start.5
  38.4 5.7 %m1y.1 = bf16[4,256,512]{2,1,0:T(8,128)(2,1)} custom-call(s32[8]{0:T(128)} %compare_select_fusion.5.b, bf16[128,512]{1,0:T(8,128)(2,1)} %get-tuple-element.8.refs_0_, bf16[128,512]{1,0:T(8,128)(2,1)} %get-tuple-element.7.refs_1_, bf16[128,512]{1,0:T(8,128)(2,1)} %get-tuple-element.6.refs_2_, bf16[128,512]{1,0:T(8,128)(2,1)} %get-tuple-element.5.refs_3_, ...), custom_call_target="tpu_custom_call" | custom-call | flops 1073741824 | bytes 5242880 | tf_op jit(solution)/shard_map/y_then_x/m1y/pallas_call | solution.py:106
  44.0 2.7 %collective-permute-start.12 = (bf16[4,256,512]{2,1,0:T(8,128)(2,1)}, bf16[4,256,512]{2,1,0:T(8,128)(2,1)}, u32[]{:S(2)}, u32[]{:S(2)}) collective-permute-start(bf16[4,256,512]{2,1,0:T(8,128)(2,1)} %m1y.1), channel_id=1, source_target_pairs={{0,16},{8,56},{16,32},{24,8},{32,48},{40,24},{48,0},{56,40},{64,80... | collective-permute-start | bytes 3145736 | tf_op jit(solution)/shard_map/y_then_x/ppermute | solution.py:232
  46.8 5.6 %x2.1 = bf16[4,256,512]{2,1,0:T(8,128)(2,1)} custom-call(s32[8]{0:T(128)} %compare_select_fusion.5.b, bf16[128,512]{1,0:T(8,128)(2,1)} %get-tuple-element.10.refs_0_, bf16[128,512]{1,0:T(8,128)(2,1)} %get-tuple-element.13.refs_1_, bf16[128,512]{1,0:T(8,128)(2,1)} %get-tuple-element.16.refs_2_, bf16[128,512]{1,0:T(8,128)(2,1)} %get-tuple-element.15.refs_3_, ...), custom_call_target="tpu_custom_call" | custom-call | flops 1073741824 | bytes 5242880 | tf_op jit(solution)/shard_map/x_then_y_send/x2/pallas_call | solution.py:106
  52.7 5.7 %m2y.1 = bf16[4,256,512]{2,1,0:T(8,128)(2,1)} custom-call(s32[8]{0:T(128)} %compare_select_fusion.5.b, bf16[128,512]{1,0:T(8,128)(2,1)} %get-tuple-element.8.refs_0_, bf16[128,512]{1,0:T(8,128)(2,1)} %get-tuple-element.7.refs_1_, bf16[128,512]{1,0:T(8,128)(2,1)} %get-tuple-element.6.refs_2_, bf16[128,512]{1,0:T(8,128)(2,1)} %get-tuple-element.5.refs_3_, ...), custom_call_target="tpu_custom_call" | custom-call | flops 1073741824 | bytes 5242880 | tf_op jit(solution)/shard_map/y_then_x/m2y/pallas_call | solution.py:106
  60.3 4.0 %m1x.1 = bf16[2,256,512]{2,1,0:T(8,128)(2,1)} custom-call(s32[8]{0:T(128)} %compare_select_fusion.5.b, bf16[128,512]{1,0:T(8,128)(2,1)} %get-tuple-element.10.refs_0_, bf16[128,512]{1,0:T(8,128)(2,1)} %get-tuple-element.13.refs_1_, bf16[128,512]{1,0:T(8,128)(2,1)} %get-tuple-element.16.refs_2_, bf16[128,512]{1,0:T(8,128)(2,1)} %get-tuple-element.15.refs_3_, ...), custom_call_target="tpu_custom_call" | custom-call | flops 536870912 | bytes 3145728 | tf_op jit(solution)/shard_map/x_then_y/m1x/pallas_call | solution.py:106
  64.2 2.7 %collective-permute-start.6 = (bf16[2,256,512]{2,1,0:T(8,128)(2,1)}, bf16[2,256,512]{2,1,0:T(8,128)(2,1)}, u32[]{:S(2)}, u32[]{:S(2)}) collective-permute-start(bf16[2,256,512]{2,1,0:T(8,128)(2,1)} %m1x.1), channel_id=1, source_target_pairs={{0,16},{8,56},{16,32},{24,8},{32,48},{40,24},{48,0},{56,40},{64,80... | collective-permute-start | bytes 1572872 | tf_op jit(solution)/shard_map/x_then_y/ppermute | solution.py:232
  67.0 6.0 %m3y.1 = bf16[4,256,512]{2,1,0:T(8,128)(2,1)} custom-call(s32[8]{0:T(128)} %compare_select_fusion.5.b, bf16[128,512]{1,0:T(8,128)(2,1)} %get-tuple-element.8.refs_0_, bf16[128,512]{1,0:T(8,128)(2,1)} %get-tuple-element.7.refs_1_, bf16[128,512]{1,0:T(8,128)(2,1)} %get-tuple-element.6.refs_2_, bf16[128,512]{1,0:T(8,128)(2,1)} %get-tuple-element.5.refs_3_, ...), custom_call_target="tpu_custom_call" | custom-call | flops 1073741824 | bytes 6291456 | tf_op jit(solution)/shard_map/y_then_x/m3y/pallas_call | solution.py:106
  73.4 4.0 %m2x.1 = bf16[2,256,512]{2,1,0:T(8,128)(2,1)} custom-call(s32[8]{0:T(128)} %compare_select_fusion.5.b, bf16[128,512]{1,0:T(8,128)(2,1)} %get-tuple-element.10.refs_0_, bf16[128,512]{1,0:T(8,128)(2,1)} %get-tuple-element.13.refs_1_, bf16[128,512]{1,0:T(8,128)(2,1)} %get-tuple-element.16.refs_2_, bf16[128,512]{1,0:T(8,128)(2,1)} %get-tuple-element.15.refs_3_, ...), custom_call_target="tpu_custom_call" | custom-call | flops 536870912 | bytes 3145728 | tf_op jit(solution)/shard_map/x_then_y/m2x/pallas_call | solution.py:106
  78.4 3.3 %collective-permute-done.4.refs_6_ = bf16[4,256,512]{2,1,0:T(8,128)(2,1)S(1)} collective-permute-done((bf16[4,256,512]{2,1,0:T(8,128)(2,1)}, bf16[4,256,512]{2,1,0:T(8,128)(2,1)S(1)}, u32[]{:S(2)}, u32[]{:S(2)}) %collective-permute-start.4) | collective-permute-done | bytes 1048608 | tf_op jit(solution)/shard_map/x_then_y_send/ppermute | solution.py:239
  82.6 4.1 %m3x.1 = bf16[2,256,512]{2,1,0:T(8,128)(2,1)} custom-call(s32[8]{0:T(128)} %compare_select_fusion.5.b, bf16[128,512]{1,0:T(8,128)(2,1)} %get-tuple-element.10.refs_0_, bf16[128,512]{1,0:T(8,128)(2,1)} %get-tuple-element.13.refs_1_, bf16[128,512]{1,0:T(8,128)(2,1)} %get-tuple-element.16.refs_2_, bf16[128,512]{1,0:T(8,128)(2,1)} %get-tuple-element.15.refs_3_, ...), custom_call_target="tpu_custom_call" | custom-call | flops 536870912 | bytes 3670016 | tf_op jit(solution)/shard_map/x_then_y/m3x/pallas_call | solution.py:106
  86.7 2.8 %collective-permute-start.7 = (bf16[2,256,512]{2,1,0:T(8,128)(2,1)}, bf16[2,256,512]{2,1,0:T(8,128)(2,1)S(1)}, u32[]{:S(2)}, u32[]{:S(2)}) collective-permute-start(bf16[2,256,512]{2,1,0:T(8,128)(2,1)} %m3x.1), channel_id=1, source_target_pairs={{0,16},{8,56},{16,32},{24,8},{32,48},{40,24},{48,0},{56,40},{64,80... | collective-permute-start | bytes 1572872 | tf_op jit(solution)/shard_map/x_then_y/ppermute | solution.py:232
  89.5 6.8 %collective-permute-done.13.refs_6_ = bf16[4,256,512]{2,1,0:T(8,128)(2,1)S(1)} collective-permute-done((bf16[4,256,512]{2,1,0:T(8,128)(2,1)}, bf16[4,256,512]{2,1,0:T(8,128)(2,1)S(1)}, u32[]{:S(2)}, u32[]{:S(2)}) %collective-permute-start.13) | collective-permute-done | bytes 1048608 | tf_op jit(solution)/shard_map/y_then_x/ppermute | solution.py:232
  96.3 1.0 copy-done.1
  97.4 3.5 %ys.1 = f32[1,256,512]{2,1,0:T(8,128)} custom-call(s32[8]{0:T(128)} %compare_select_fusion.5.b, bf16[128,512]{1,0:T(8,128)(2,1)} %get-tuple-element.8.refs_0_, bf16[128,512]{1,0:T(8,128)(2,1)} %get-tuple-element.7.refs_1_, bf16[128,512]{1,0:T(8,128)(2,1)} %get-tuple-element.6.refs_2_, bf16[128,512]{1,0:T(8,128)(2,1)} %get-tuple-element.5.refs_3_, ...), custom_call_target="tpu_custom_call" | custom-call | flops 268435456 | bytes 1835008 | tf_op jit(solution)/shard_map/last/ys/pallas_call | solution.py:106
  100.9 2.5 %collective-permute-start.15 = (f32[1,256,512]{2,1,0:T(8,128)}, f32[1,256,512]{2,1,0:T(8,128)S(1)}, u32[]{:S(2)}, u32[]{:S(2)}) collective-permute-start(f32[1,256,512]{2,1,0:T(8,128)} %ys.1), channel_id=1, source_target_pairs={{0,8},{8,0},{16,24},{24,16},{32,40},{40,32},{48,56},{56,48},{64,72... | collective-permute-start | bytes 1572872 | tf_op jit(solution)/shard_map/last/ppermute | solution.py:203
  104.2 3.6 %xs.1 = f32[1,256,512]{2,1,0:T(8,128)} custom-call(s32[8]{0:T(128)} %compare_select_fusion.5.b, bf16[128,512]{1,0:T(8,128)(2,1)} %get-tuple-element.10.refs_0_, bf16[128,512]{1,0:T(8,128)(2,1)} %get-tuple-element.13.refs_1_, bf16[128,512]{1,0:T(8,128)(2,1)} %get-tuple-element.16.refs_2_, bf16[128,512]{1,0:T(8,128)(2,1)} %get-tuple-element.15.refs_3_, ...), custom_call_target="tpu_custom_call" | custom-call | flops 268435456 | bytes 2097152 | tf_op jit(solution)/shard_map/last/xs/pallas_call | solution.py:106
  109.1 3.4 %yg.1 = bf16[1,256,512]{2,1,0:T(8,128)(2,1)} custom-call(s32[8]{0:T(128)} %compare_select_fusion.5.b, bf16[128,512]{1,0:T(8,128)(2,1)} %get-tuple-element.8.refs_0_, bf16[128,512]{1,0:T(8,128)(2,1)} %get-tuple-element.7.refs_1_, bf16[128,512]{1,0:T(8,128)(2,1)} %get-tuple-element.6.refs_2_, bf16[128,512]{1,0:T(8,128)(2,1)} %get-tuple-element.5.refs_3_, ...), custom_call_target="tpu_custom_call" | custom-call | flops 268435456 | bytes 1835008 | tf_op jit(solution)/shard_map/last/yg/pallas_call | solution.py:106
  112.6 1.1 collective-permute-start.17
  113.7 3.4 %yf.1 = bf16[1,256,512]{2,1,0:T(8,128)(2,1)} custom-call(s32[8]{0:T(128)} %compare_select_fusion.5.b, bf16[128,512]{1,0:T(8,128)(2,1)} %get-tuple-element.8.refs_0_, bf16[128,512]{1,0:T(8,128)(2,1)} %get-tuple-element.7.refs_1_, bf16[128,512]{1,0:T(8,128)(2,1)} %get-tuple-element.6.refs_2_, bf16[128,512]{1,0:T(8,128)(2,1)} %get-tuple-element.5.refs_3_, ...), custom_call_target="tpu_custom_call" | custom-call | flops 268435456 | bytes 1835008 | tf_op jit(solution)/shard_map/last/yf/pallas_call | solution.py:106
  118.0 3.6 %yo.1 = f32[1,256,512]{2,1,0:T(8,128)} custom-call(s32[8]{0:T(128)} %compare_select_fusion.5.b, bf16[128,512]{1,0:T(8,128)(2,1)} %get-tuple-element.8.refs_0_, bf16[128,512]{1,0:T(8,128)(2,1)} %get-tuple-element.7.refs_1_, bf16[128,512]{1,0:T(8,128)(2,1)} %get-tuple-element.6.refs_2_, bf16[128,512]{1,0:T(8,128)(2,1)} %get-tuple-element.5.refs_3_, ...), custom_call_target="tpu_custom_call" | custom-call | flops 268435456 | bytes 1835008 | tf_op jit(solution)/shard_map/last/yo/pallas_call | solution.py:106
  121.6 3.7 %xo.1 = f32[1,256,512]{2,1,0:T(8,128)} custom-call(s32[8]{0:T(128)} %compare_select_fusion.5.b, bf16[128,512]{1,0:T(8,128)(2,1)} %get-tuple-element.10.refs_0_, bf16[128,512]{1,0:T(8,128)(2,1)} %get-tuple-element.13.refs_1_, bf16[128,512]{1,0:T(8,128)(2,1)} %get-tuple-element.16.refs_2_, bf16[128,512]{1,0:T(8,128)(2,1)} %get-tuple-element.15.refs_3_, ...), custom_call_target="tpu_custom_call" | custom-call | flops 268435456 | bytes 2097152 | tf_op jit(solution)/shard_map/last/xo/pallas_call | solution.py:106
  127.7 4.8 %final.1 = f32[512,1024]{1,0:T(8,128)} custom-call(s32[8]{0:T(128)} %compare_select_fusion.5.b, s32[4,16]{1,0:T(4,128)} %mask.1, f32[1,256,512]{2,1,0:T(8,128)} %xo.1, f32[1,256,512]{2,1,0:T(8,128)} %copy-done.6, f32[1,256,512]{2,1,0:T(8,128)} %yo.1, f32[1,256,512]{2,1,0:T(8,128)} %copy-done.5, bf16[1,256,512]{2,1,0:T(8,128)(2,1)} %copy-done.8, ...), custom_call_target="tpu_custom_call" | custom-call | tf_op jit(solution)/shard_map/last/final/pallas_call | solution.py:169
  (59 shorter events, 16.7 us)
Async XLA Ops:
  0.0 31.5 %collective-permute-start.3 = (bf16[512,8192]{1,0:T(8,128)(2,1)}, bf16[512,8192]{1,0:T(8,128)(2,1)}, u32[]{:S(2)}, u32[]{:S(2)}) collective-permute-start(bf16[512,8192]{1,0:T(8,128)(2,1)} %refs_4_.27), channel_id=1, source_target_pairs={{0,8},{8,0},{16,24},{24,16},{32,40},{40,32},{48,56},{56,48},{64,72... | collective-permute-start | bytes 25165832 | tf_op jit(solution)/shard_map/ppermute | solution.py:203
  6.6 6.8 %collective-permute-start = (bf16[128,512]{1,0:T(8,128)(2,1)}, bf16[128,512]{1,0:T(8,128)(2,1)S(1)}, u32[]{:S(2)}, u32[]{:S(2)}) collective-permute-start(bf16[128,512]{1,0:T(8,128)(2,1)} %pick.1), channel_id=1, source_target_pairs={{0,1},{1,0},{2,3},{3,2},{4,5},{5,4},{6,7},{7,6},{8,9},{9,8},{10,11... | collective-permute-start | bytes 393224 | tf_op jit(solution)/shard_map/panel/ppermute | solution.py:208
  14.4 2.0 %collective-permute-start.1 = (bf16[2,128,512]{2,1,0:T(8,128)(2,1)S(1)}, bf16[2,128,512]{2,1,0:T(8,128)(2,1)S(1)}, u32[]{:S(2)}, u32[]{:S(2)}) collective-permute-start(bf16[2,128,512]{2,1,0:T(8,128)(2,1)S(1)} %pad_maximum_fusion), channel_id=1, source_target_pairs={{0,8},{8,0},{16,24},{24,16},{32,40},{40,32},{48,56},{56,48},{64,72... | collective-permute-start | bytes 786440 | tf_op jit(solution)/shard_map/panel/ppermute | solution.py:203
  17.1 7.2 %collective-permute-start.2 = (bf16[2,128,512]{2,1,0:T(8,128)(2,1)S(1)}, bf16[2,128,512]{2,1,0:T(8,128)(2,1)S(1)}, u32[]{:S(2)}, u32[]{:S(2)}) collective-permute-start(bf16[2,128,512]{2,1,0:T(8,128)(2,1)S(1)} %pad_maximum_fusion.1), channel_id=1, source_target_pairs={{0,2},{1,3},{2,4},{3,5},{4,6},{5,7},{6,0},{7,1},{8,14},{9,15},{10,... | collective-permute-start | bytes 786440 | tf_op jit(solution)/shard_map/panel/ppermute | solution.py:215
  21.1 7.1 %collective-permute-start.10 = (bf16[2,128,512]{2,1,0:T(8,128)(2,1)S(1)}, bf16[2,128,512]{2,1,0:T(8,128)(2,1)S(1)}, u32[]{:S(2)}, u32[]{:S(2)}) collective-permute-start(bf16[2,128,512]{2,1,0:T(8,128)(2,1)S(1)} %pad_maximum_fusion.2), channel_id=1, source_target_pairs={{0,2},{1,3},{2,4},{3,5},{4,6},{5,7},{6,0},{7,1},{8,14},{9,15},{10,... | collective-permute-start | bytes 786440 | tf_op jit(solution)/shard_map/panel/ppermute | solution.py:215
  24.4 6.4 %collective-permute-start.11 = (bf16[2,128,512]{2,1,0:T(8,128)(2,1)S(1)}, bf16[2,128,512]{2,1,0:T(8,128)(2,1)S(1)}, u32[]{:S(2)}, u32[]{:S(2)}) collective-permute-start(bf16[2,128,512]{2,1,0:T(8,128)(2,1)S(1)} %collective-permute-done.2), channel_id=1, source_target_pairs={{0,2},{1,3},{2,4},{3,5},{4,6},{5,7},{6,0},{7,1},{8,14},{9,15},{10,... | collective-permute-start | bytes 786440 | tf_op jit(solution)/shard_map/panel/ppermute | solution.py:215
  37.2 22.1 %collective-permute-start.5 = (bf16[4,256,512]{2,1,0:T(8,128)(2,1)}, bf16[4,256,512]{2,1,0:T(8,128)(2,1)S(1)}, u32[]{:S(2)}, u32[]{:S(2)}) collective-permute-start(bf16[4,256,512]{2,1,0:T(8,128)(2,1)} %x1.1), channel_id=1, source_target_pairs={{0,64},{8,72},{16,80},{24,88},{32,96},{40,104},{48,112},{56,120},{... | collective-permute-start | bytes 3145736 | tf_op jit(solution)/shard_map/x_then_y_send/ppermute | solution.py:237
  44.0 22.9 %collective-permute-start.12 = (bf16[4,256,512]{2,1,0:T(8,128)(2,1)}, bf16[4,256,512]{2,1,0:T(8,128)(2,1)}, u32[]{:S(2)}, u32[]{:S(2)}) collective-permute-start(bf16[4,256,512]{2,1,0:T(8,128)(2,1)} %m1y.1), channel_id=1, source_target_pairs={{0,16},{8,56},{16,32},{24,8},{32,48},{40,24},{48,0},{56,40},{64,80... | collective-permute-start | bytes 3145736 | tf_op jit(solution)/shard_map/y_then_x/ppermute | solution.py:232
  52.4 29.2 %collective-permute-start.4 = (bf16[4,256,512]{2,1,0:T(8,128)(2,1)}, bf16[4,256,512]{2,1,0:T(8,128)(2,1)S(1)}, u32[]{:S(2)}, u32[]{:S(2)}) collective-permute-start(bf16[4,256,512]{2,1,0:T(8,128)(2,1)} %x2.1), channel_id=1, source_target_pairs={{0,64},{8,72},{16,80},{24,88},{32,96},{40,104},{48,112},{56,120},{... | collective-permute-start | bytes 3145736 | tf_op jit(solution)/shard_map/x_then_y_send/ppermute | solution.py:239
  58.3 31.2 %collective-permute-start.14 = (bf16[4,256,512]{2,1,0:T(8,128)(2,1)}, bf16[4,256,512]{2,1,0:T(8,128)(2,1)S(1)}, u32[]{:S(2)}, u32[]{:S(2)}) collective-permute-start(bf16[4,256,512]{2,1,0:T(8,128)(2,1)} %m2y.1), channel_id=1, source_target_pairs={{0,48},{8,24},{16,0},{24,40},{32,16},{40,56},{48,32},{56,8},{64,11... | collective-permute-start | bytes 3145736 | tf_op jit(solution)/shard_map/y_then_x/ppermute | solution.py:233
  59.3 1.0 copy-start.3
  64.2 17.4 %collective-permute-start.6 = (bf16[2,256,512]{2,1,0:T(8,128)(2,1)}, bf16[2,256,512]{2,1,0:T(8,128)(2,1)}, u32[]{:S(2)}, u32[]{:S(2)}) collective-permute-start(bf16[2,256,512]{2,1,0:T(8,128)(2,1)} %m1x.1), channel_id=1, source_target_pairs={{0,16},{8,56},{16,32},{24,8},{32,48},{40,24},{48,0},{56,40},{64,80... | collective-permute-start | bytes 1572872 | tf_op jit(solution)/shard_map/x_then_y/ppermute | solution.py:232
  73.0 23.4 %collective-permute-start.13 = (bf16[4,256,512]{2,1,0:T(8,128)(2,1)}, bf16[4,256,512]{2,1,0:T(8,128)(2,1)S(1)}, u32[]{:S(2)}, u32[]{:S(2)}) collective-permute-start(bf16[4,256,512]{2,1,0:T(8,128)(2,1)} %m3y.1), channel_id=1, source_target_pairs={{0,16},{8,56},{16,32},{24,8},{32,48},{40,24},{48,0},{56,40},{64,80... | collective-permute-start | bytes 3145736 | tf_op jit(solution)/shard_map/y_then_x/ppermute | solution.py:232
  77.4 26.0 %collective-permute-start.8 = (bf16[2,256,512]{2,1,0:T(8,128)(2,1)}, bf16[2,256,512]{2,1,0:T(8,128)(2,1)}, u32[]{:S(2)}, u32[]{:S(2)}) collective-permute-start(bf16[2,256,512]{2,1,0:T(8,128)(2,1)} %m2x.1), channel_id=1, source_target_pairs={{0,48},{8,24},{16,0},{24,40},{32,16},{40,56},{48,32},{56,8},{64,11... | collective-permute-start | bytes 1572872 | tf_op jit(solution)/shard_map/x_then_y/ppermute | solution.py:233
  81.7 1.0 copy-start.2
  86.7 16.7 %collective-permute-start.7 = (bf16[2,256,512]{2,1,0:T(8,128)(2,1)}, bf16[2,256,512]{2,1,0:T(8,128)(2,1)S(1)}, u32[]{:S(2)}, u32[]{:S(2)}) collective-permute-start(bf16[2,256,512]{2,1,0:T(8,128)(2,1)} %m3x.1), channel_id=1, source_target_pairs={{0,16},{8,56},{16,32},{24,8},{32,48},{40,24},{48,0},{56,40},{64,80... | collective-permute-start | bytes 1572872 | tf_op jit(solution)/shard_map/x_then_y/ppermute | solution.py:232
  89.5 6.8 %copy-start = (bf16[4,256,512]{2,1,0:T(8,128)(2,1)}, bf16[4,256,512]{2,1,0:T(8,128)(2,1)S(1)}, u32[]{:S(2)}) copy-start(bf16[4,256,512]{2,1,0:T(8,128)(2,1)S(1)} %collective-permute-done.14.refs_7_) | copy-start | bytes 3145732
  96.3 1.0 copy-start.1
  100.9 8.0 %copy-start.11 = (s32[8,2]{0,1:T(2,128)S(1)}, s32[8,2]{0,1:T(2,128)}, u32[]{:S(2)}) copy-start(s32[8,2]{0,1:T(2,128)} %param.8) | copy-start | bytes 196
  100.9 8.0 %copy-start.9 = (f32[4096]{0:T(1024)S(1)}, f32[4096]{0:T(1024)}, u32[]{:S(2)}) copy-start(f32[4096]{0:T(1024)} %param.9) | copy-start | bytes 49156
  100.9 8.0 %copy-start.10 = (f32[4096]{0:T(1024)S(1)}, f32[4096]{0:T(1024)}, u32[]{:S(2)}) copy-start(f32[4096]{0:T(1024)} %param.10) | copy-start | bytes 49156
  100.9 25.1 %collective-permute-start.15 = (f32[1,256,512]{2,1,0:T(8,128)}, f32[1,256,512]{2,1,0:T(8,128)S(1)}, u32[]{:S(2)}, u32[]{:S(2)}) collective-permute-start(f32[1,256,512]{2,1,0:T(8,128)} %ys.1), channel_id=1, source_target_pairs={{0,8},{8,0},{16,24},{24,16},{32,40},{40,32},{48,56},{56,48},{64,72... | collective-permute-start | bytes 1572872 | tf_op jit(solution)/shard_map/last/ppermute | solution.py:203
  103.4 0.8 copy-start.4
  107.9 18.2 %collective-permute-start.9 = (f32[1,256,512]{2,1,0:T(8,128)}, f32[1,256,512]{2,1,0:T(8,128)S(1)}, u32[]{:S(2)}, u32[]{:S(2)}) collective-permute-start(f32[1,256,512]{2,1,0:T(8,128)} %xs.1), channel_id=1, source_target_pairs={{0,8},{8,0},{16,24},{24,16},{32,40},{40,32},{48,56},{56,48},{64,72... | collective-permute-start | bytes 1572872 | tf_op jit(solution)/shard_map/last/ppermute | solution.py:203
  112.6 12.7 %collective-permute-start.17 = (bf16[1,256,512]{2,1,0:T(8,128)(2,1)}, bf16[1,256,512]{2,1,0:T(8,128)(2,1)S(1)}, u32[]{:S(2)}, u32[]{:S(2)}) collective-permute-start(bf16[1,256,512]{2,1,0:T(8,128)(2,1)} %yg.1), channel_id=1, source_target_pairs={{0,72},{8,64},{16,88},{24,80},{32,104},{40,96},{48,120},{56,112},{... | collective-permute-start | bytes 786440 | tf_op jit(solution)/shard_map/last/ppermute | solution.py:280
  117.1 8.9 %collective-permute-start.16 = (bf16[1,256,512]{2,1,0:T(8,128)(2,1)}, bf16[1,256,512]{2,1,0:T(8,128)(2,1)S(1)}, u32[]{:S(2)}, u32[]{:S(2)}) collective-permute-start(bf16[1,256,512]{2,1,0:T(8,128)(2,1)} %yf.1), channel_id=1, source_target_pairs={{0,64},{8,72},{16,80},{24,88},{32,96},{40,104},{48,112},{56,120},{... | collective-permute-start | bytes 786440 | tf_op jit(solution)/shard_map/last/ppermute | solution.py:279
  125.2 0.8 copy-start.7
  126.0 0.7 copy-start.8
  126.0 0.9 copy-start.5
  126.9 0.8 copy-start.6

commit v2 on v0

v2 whole, which is shorter than its diff:
```python
import functools

import jax
import jax.numpy as jnp
from jax import lax
from jax.experimental import pallas as pl
from jax.experimental.pallas import tpu as pltpu
from jax.sharding import PartitionSpec as P

TILE = 128
NX, NY, NC = 2, 4, 2
NZ, NH = 4, 2
N_COMP, N_PAIR = NX * NY * NC, NZ * NH
QB = 512
F32, BF16 = jnp.float32, jnp.bfloat16


def comp_at(x, y, k):
    return ((x % NX) * NY + y % NY) * NC + k % NC


def comp_perm(move):
    out = []
    for c in range(N_COMP):
        x, y, k = c // (NY * NC), (c // NC) % NY, c % NC
        out.append((c, comp_at(*move(x, y, k))))
    return out


CORE = comp_perm(lambda x, y, k: (x, y, k + 1))
XSWAP = comp_perm(lambda x, y, k: (x + 1, y, k))
XCROSS = comp_perm(lambda x, y, k: (x + 1, y, k + 1))
AHEAD = comp_perm(lambda x, y, k: (x, y + 1 - 2 * k, k))
BEHIND = comp_perm(lambda x, y, k: (x, y - 1 + 2 * k, k))
HALF = [(p, p ^ 1) for p in range(N_PAIR)]
ZSPLIT = [
    (c * N_PAIR + p, c * N_PAIR + ((p // NH + 1 - 2 * (c % NC)) % NZ) * NH + p % NH)
    for c in range(N_COMP)
    for p in range(N_PAIR)
]


def place_facts():
    comp, pair = lax.axis_index("comp"), lax.axis_index("pair")
    return [comp // (NY * NC), (comp // NC) % NY, comp % NC, comp, pair // NH, pair % NH]


def step_sign(b):
    return 1 - 2 * b[2]


def block_of(b, other_x, dy):
    x = 1 - b[0] if other_x else b[0]
    return (x * NY + ((b[1] + dy * step_sign(b) + NY) % NY)) * NC


VMEM = pl.BlockSpec(memory_space=pltpu.VMEM)
ANY = pl.BlockSpec(memory_space=pl.ANY)
HBM = pl.BlockSpec(memory_space=pltpu.HBM)
LIMIT = 20 << 20
NO_ROOM = 58 << 20


def pick_kernel(dens, w_ref, o_ref, buf, sems):
    def load(n):
        return pltpu.make_async_copy(
            dens.at[:, n * QB : n * QB + TILE], buf.at[:, n * TILE : (n + 1) * TILE], sems.at[n]
        )

    for n in range(N_COMP):
        load(n).start()
    k, wide = buf.shape
    at = lax.broadcasted_iota(jnp.int32, (wide, TILE), 0)
    to = lax.broadcasted_iota(jnp.int32, (wide, TILE), 1)
    spots = (at == (to // 8) * TILE + to % 8).astype(BF16)
    per = k // TILE
    comp = lax.axis_index("comp")
    w = [w_ref[pl.ds(comp * per + n, 1), :] for n in range(per)]
    for n in range(N_COMP):
        load(n).wait()
    rows = jnp.dot(buf[...], spots, preferred_element_type=F32)
    o_ref[0] = (rows.T * jnp.concatenate(w, axis=1)).astype(BF16)


def pick(dens, coulomb):
    k = dens.shape[0]
    return pl.pallas_call(
        pick_kernel,
        in_specs=[HBM, VMEM],
        out_specs=VMEM,
        out_shape=jax.ShapeDtypeStruct((1, 8 * N_COMP, k), BF16),
        scratch_shapes=[
            pltpu.VMEM((k, N_COMP * TILE), BF16),
            pltpu.SemaphoreType.DMA((N_COMP,)),
        ],
        compiler_params=pltpu.CompilerParams(vmem_limit_bytes=NO_ROOM),
        name="pick",
    )(dens, coulomb.reshape(coulomb.shape[0] // TILE, TILE))


def pair_kernel(a_ref, b_ref, o_ref, same_ref):
    for out in (o_ref, same_ref):
        out[0:1] = a_ref[...]
        out[1:2] = b_ref[...]


def pair_up(a, b):
    return pl.pallas_call(
        pair_kernel,
        in_specs=[VMEM, VMEM],
        out_specs=[VMEM, VMEM],
        out_shape=[jax.ShapeDtypeStruct((2, *a.shape[1:]), a.dtype)] * 2,
        compiler_params=pltpu.CompilerParams(vmem_limit_bytes=LIMIT),
        name="pair_up",
    )(a, b)


def choose_kernel(zero, one, after, o_ref):
    o_ref[...] = jnp.where(place_facts()[2] == 0, zero[...], one[...])


def choose(zero, one, after):
    return pl.pallas_call(
        choose_kernel,
        in_specs=[VMEM, VMEM, ANY],
        out_specs=VMEM,
        out_shape=jax.ShapeDtypeStruct(zero.shape, zero.dtype),
        compiler_params=pltpu.CompilerParams(vmem_limit_bytes=LIMIT),
        name="choose",
    )(zero, one, after)


def mm_kernel(work, sizes, n_add, n_out, *refs):
    n_panel = sum(sizes)
    panels, (own, oth), refs = refs[:n_panel], refs[n_panel : n_panel + 2], refs[n_panel + 2 :]
    adds, outs = refs[:n_add], refs[n_add : n_add + n_out]
    own_buf, oth_buf, sems = refs[-3:]
    b = place_facts()

    def loads(n):
        at = pl.ds(pl.multiple_of(work[n][2](b) * QB, QB), QB)
        return [
            pltpu.make_async_copy(src.at[:, at], buf.at[n], sems.at[s, n])
            for s, (src, buf) in enumerate(((own, own_buf), (oth, oth_buf)))
        ]

    for n in range(len(work)):
        for copy in loads(n):
            copy.start()
    sides = ([], [])
    for size in sizes:
        group, panels = panels[:size], panels[size:]
        for n, side in enumerate(sides):
            if size == 1:
                side.append(group[0][n])
            else:
                side.append(jnp.where(b[2] == 0, group[0][n], group[1][n]))
    left, right = [jnp.concatenate(side) if len(side) > 1 else side[0] for side in sides]
    rows = left.shape[0]
    part = rows // len(sizes)
    for n, (out, slot, _, terms) in enumerate(work):
        for copy in loads(n):
            copy.wait()
        acc = jnp.dot(left, own_buf[n], preferred_element_type=F32)
        acc += jnp.dot(right, oth_buf[n], preferred_element_type=F32)
        for g in range(len(sizes)):
            piece = acc[g * part : (g + 1) * part]
            for a, where in terms:
                if isinstance(a, tuple):
                    piece += adds[a[g]][where(b)].astype(F32)
                else:
                    piece += adds[a][where(b), g * part : (g + 1) * part].astype(F32)
            if isinstance(out, tuple):
                step = rows // len(out)
                for m in range(g * part // step, (g + 1) * part // step):
                    outs[out[m]][slot] = piece[m * step - g * part : (m + 1) * step - g * part]
            else:
                outs[out][slot, g * part : (g + 1) * part] = piece.astype(outs[out].dtype)


def mm(name, groups, dens, work, outs, adds=(), after=(), limit=LIMIT):
    k = dens[0].shape[0]
    rows = 128 * len(groups)
    n = len(work)
    panels = [piece for group in groups for piece in group]

    def body(*refs):
        n_in = len(panels) + 2 + len(adds)
        mm_kernel(
            work, [len(g) for g in groups], len(adds), len(outs), *refs[:n_in], *refs[n_in + len(after) :]
        )

    return pl.pallas_call(
        body,
        in_specs=[VMEM] * len(panels) + [HBM] * 2 + [VMEM] * len(adds) + [ANY] * len(after),
        out_specs=[VMEM] * len(outs),
        out_shape=[jax.ShapeDtypeStruct((m, out_rows or rows, QB), dtype) for m, dtype, out_rows in outs],
        scratch_shapes=[pltpu.VMEM((n, k, QB), BF16)] * 2 + [pltpu.SemaphoreType.DMA((2, n))],
        cost_estimate=pl.CostEstimate(
            flops=4 * n * rows * k * QB, bytes_accessed=4 * n * k * QB, transcendentals=0
        ),
        compiler_params=pltpu.CompilerParams(vmem_limit_bytes=limit),
        name=name,
    )(*panels, *dens, *adds, *after)


def final_kernel(mask, *refs):
    b = place_facts()
    z, half, core = b[4], b[5], b[2]
    (xo, *xr), (yo, *yr), (fo, fr, diag, o_ref, t_ref) = refs[:5], refs[5:10], refs[10:]

    def pair_at(dz, dh):
        return ((z + dz + NZ) % NZ) * NH + (half + dh) % NH

    def place(value, c, p):
        for t in range(QB // TILE):
            scale = (2 * mask[t, c]).astype(F32)
            at = pl.ds(pl.multiple_of((c * N_PAIR + p) * 8, 8), 8)
            t_ref[at, t * TILE : (t + 1) * TILE] = value(t) * scale

    order = (((-1, 1), (-2, 0), (0, 0), (-1, 0)), ((1, 1), (2, 1), (0, 1), (1, 0)))
    for source in range(2):
        mine = source == 0
        for g in range(4):
            spots = [pair_at(*order[s][g]) for s in range(2)]
            same = core if mine else 1 - core
            p = jnp.where(same == 0, spots[0], spots[1])
            for c in range(N_COMP):
                row = (g % 2) * 128 + c * 8
                own, swapped, more = (xo, xr, None) if g < 2 else (yo, yr, fo if mine else fr)
                if mine:
                    src, at = own, row
                else:
                    src, at = swapped[row // 64], row % 64

                def value(t, src=src, at=at, more=more, row=row):
                    lanes = slice(t * TILE, (t + 1) * TILE)
                    out = src[0, at : at + 8, lanes]
                    if more is not None:
                        out = out + more[0, row : row + 8, lanes].astype(F32)
                    return out

                place(value, c, p)
    here = pl.ds(pl.multiple_of((b[3] * N_PAIR + pair_at(0, 0)) * 8, 8), 8)
    t_ref[here, 0:TILE] = t_ref[here, 0:TILE] + diag[...]
    o_ref[...] = t_ref[...].T


def final(mask, parts, diag):
    window = 8 * N_COMP * N_PAIR
    return pl.pallas_call(
        final_kernel,
        in_specs=[pl.BlockSpec(memory_space=pltpu.SMEM)] + [VMEM] * (len(parts) + 1),
        out_specs=VMEM,
        out_shape=jax.ShapeDtypeStruct((QB, window), F32),
        scratch_shapes=[pltpu.VMEM((window, QB), F32)],
        compiler_params=pltpu.CompilerParams(vmem_limit_bytes=LIMIT),
        name="final",
    )(mask, *parts, diag)


def energy_tile(pair_list, valence_energy, conduction_energy):
    table = jnp.arange(valence_energy.shape[0], dtype=jnp.int32)
    cond_hits = pair_list[:, 1][:, None] == table[None, :]
    val_hits = pair_list[:, 0][:, None] == table[None, :]
    energy = jnp.sum(jnp.where(cond_hits, conduction_energy[None, :], 0.0), axis=1) - jnp.sum(
        jnp.where(val_hits, valence_energy[None, :], 0.0), axis=1
    )
    return jnp.eye(8, TILE, dtype=F32) * energy[:, None]


def per_device(densities, coulomb, pair_list, valence_energy, conduction_energy, tile_mask):
    swap = lambda a: lax.ppermute(a, "comp", CORE)
    zmove = lambda a: lax.ppermute(a, ("comp", "pair"), ZSPLIT)
    with jax.named_scope("panel"):
        v = pick(densities, coulomb)
        w = swap(v)
        held, w = lax.optimization_barrier((densities, w))
        dens = (densities, swap(held))
        vw, vw_again = pair_up(v, w)
        hvw = lax.ppermute(vw_again, "pair", HALF)
        near = zmove(vw)
        near2 = zmove(hvw)
    early = (vw, hvw)

    ahead = lambda a: lax.ppermute(a, "comp", AHEAD)
    behind = lambda a: lax.ppermute(a, "comp", BEHIND)
    across = lambda a: lax.ppermute(a, "comp", XSWAP)

    def both(out, start, other_x, dy, terms=()):
        return [
            (
                out, start + n,
                lambda b, n=n: block_of(b, other_x, dy) + n,
                tuple((a, lambda b, t=t, n=n: t + n) for a, t in terms),
            )
            for n in range(NC)
        ]

    def each(out_mine, out_other, other_x, terms):
        mine, other = lambda b: b[2], lambda b: 1 - b[2]
        return [
            (
                out, 0,
                lambda b, core=core: block_of(b, other_x, 0) + core(b),
                tuple((a, lambda b, t=t, core=core: t + core(b)) for a, t in terms),
            )
            for out, core in ((out_mine, mine), (out_other, other))
        ]

    def mmx(name, *rest, **more):
        return mm(name, [(near2,), (far,)], dens, *rest, **more)

    def mmy(name, *rest, **more):
        return mm(name, [early, (near,)], dens, *rest, **more)

    def through_y(other_x, **more):
        dest = lambda out, start, dy: both(out, start, other_x, dy)
        m1, m2 = mmy("m12y", dest(0, 0, 2) + dest(1, 0, -1), [(2, BF16, 0)] * 2, **more)
        return m1, ahead(m1), behind(m2)

    def through_y_2(other_x, m1r, after):
        m3, = mmy("m3y", both(0, 0, other_x, 1, [(0, 0)]), [(2, BF16, 0)], [m1r], after=after)
        return m3, ahead(m3)

    near_dests = both(0, 0, True, 2) + both(0, 2, True, -1)
    with jax.named_scope("y_then_x"):
        m1o, m1or, m2or = through_y(True)
    with jax.named_scope("x_then_y_send"):
        far = zmove(choose(near, near2, m1o))
        xe, = mm("xe", [(near2,)], dens, near_dests, [(4, BF16, 0)], after=(m1o,))
        xer = across(xe)
    with jax.named_scope("y_then_x"):
        m1w, m1wr, m2wr = through_y(False, after=(xe,))
    with jax.named_scope("x_then_y_send"):
        xl, = mm("xl", [(far,)], dens, near_dests, [(4, BF16, 0)], after=(m1w,))
        xlr = across(xl)
        x2, = mmx("x2", both(0, 0, True, 1) + both(0, 2, True, 0), [(4, BF16, 0)], after=(xl,))
        x2r = across(x2)
    with jax.named_scope("y_then_x"):
        m3o, m3or = through_y_2(True, m1or, (x2, xer))
        m3w, m3wr = through_y_2(False, m1wr, (m3o,))
        yf, yg = mmy(
            "yfg", each(0, 1, True, [(0, 0), (1, 0)]), [(1, BF16, 0)] * 2, [m3or, m2or], after=(m3w, xlr)
        )
        fo, fr = across(yf), lax.ppermute(yg, "comp", XCROSS)
    with jax.named_scope("x_then_y"):
        m1x, m2x = mmx(
            "m12x", both(0, 0, False, 2, [((0, 1), 0)]) + both(1, 0, False, -1, [((0, 1), 2)]),
            [(2, BF16, 0)] * 2, [xer, xlr], after=(yf,),
        )
        m1xr, m2xr = ahead(m1x), behind(m2x)
        m3x, = mmx(
            "m3x", both(0, 0, False, 1, [(0, 0), (1, 0)]), [(2, BF16, 0)], [x2r, m1xr], after=(m1x,)
        )
        m3xr = ahead(m3x)

    split = [(1, F32, 0)] + [(1, F32, 64)] * 4
    with jax.named_scope("last"):
        yo, *ys = mmy(
            "yos", each(0, (1, 2, 3, 4), False, [(0, 0), (1, 0)]), split, [m3wr, m2wr], after=(m3x,)
        )
        yr = [swap(a) for a in ys]
        xo, *xs = mmx(
            "xos", each(0, (1, 2, 3, 4), False, [(0, 2), (1, 0), (2, 0)]), split, [x2r, m3xr, m2xr],
            after=(yo,),
        )
        xr = [swap(a) for a in xs]
        diag = energy_tile(pair_list, valence_energy, conduction_energy)
        return final(tile_mask, (xo, *xr, yo, *yr, fo, fr), diag)


def solution(mesh):
    return jax.shard_map(
        per_device,
        mesh=mesh,
        in_specs=(
            P("comp", "pair"),
            P(),
            P(("comp", "pair"), None),
            P(),
            P(),
            P(("pair", "comp"), None),
        ),
        out_specs=P(("pair", "comp"), None),
        check_vma=False,
    )
```

time: 279 us -> 102 us (0.37)
  waiting for transfers between devices: 227 us -> 31.2 us
  starting transfers between devices: 0.04 us -> 36.8 us
  Pallas kernels: 0 us -> 29.1 us
  matrix products: 17.7 us -> 0 us
  between operations: 13.5 us -> 0.23 us
  local copies, waits for them, and re-layouts: 17.3 us -> 4.31 us
    reduce_scatter x1 -> x0, waiting for transfers between devices: 179 us -> none  [per_device(): lax.psum_scatter(lax.dot_general(densities, panel, (((0,), (1,)), ((), ()...]
    all_gather x1 -> x0, waiting for transfers between devices: 47.9 us -> none  [per_device(): gathered = lax.all_gather(local_panel, 'pair', axis=1, tiled=True)]
    ppermute x0 -> x28, starting transfers between devices: none -> 36.8 us  [the longest x6 11.4 us: per_device(): ahead = lambda a: lax.ppermute(a, 'comp', AHEAD)]
    ppermute x0 -> x28, waiting for transfers between devices: none -> 31.2 us  [the longest x4 14.1 us: per_device(): across = lambda a: lax.ppermute(a, 'comp', XSWAP)]
    pallas_call x0 -> x16, Pallas kernels: none -> 29.1 us  [the longest x12 22 us: mm(): pl.pallas_call(body, in_specs=[VMEM] * len(panels) + [HBM] * 2 + [VMEM] *...]
    dot_general x1 -> x0, matrix products: 17.7 us -> none  [per_device(): lax.dot_general(densities, panel, (((0,), (1,)), ((), ())), preferred_ele...]
    unnamed x11 -> x12, local copies, waits for them, and re-layouts: 13.9 us -> 4.3 us
  transfers between devices with their start and end apart: 2 -> 28, of which waited for: 2 -> 14; matrix products, arithmetic and copies ran while one was open for 0% -> 0% of each run, Pallas kernels for 0% -> 20%
where the time goes in v2:
time: 102 us
  starting transfers between devices  36.8 us (36%)
  waiting for transfers between devices  31.2 us (31%)
  Pallas kernels  29.1 us (29%)
  local copies, waits for them, and re-layouts  4.31 us (4%)
    pallas_call x12, Pallas kernels, mm(): pl.pallas_call(body, in_specs=[VMEM] * len(panels) + [HBM] * 2 + [VMEM] *...  22 us
    ppermute x4, waiting for transfers between devices, per_device(): across = lambda a: lax.ppermute(a, 'comp', XSWAP)  14.1 us
    ppermute x6, starting transfers between devices, per_device(): ahead = lambda a: lax.ppermute(a, 'comp', AHEAD)  11.4 us
    ppermute x6, waiting for transfers between devices, per_device(): ahead = lambda a: lax.ppermute(a, 'comp', AHEAD)  11.3 us
    ppermute x3, starting transfers between devices, per_device(): zmove = lambda a: lax.ppermute(a, ('comp', 'pair'), ZSPLIT)  10.4 us
    ppermute x10, starting transfers between devices, per_device(): swap = lambda a: lax.ppermute(a, 'comp', CORE)  7.37 us
    unnamed x12, local copies, waits for them, and re-layouts  4.3 us
    pallas_call x1, Pallas kernels, pick(): pl.pallas_call(pick_kernel, in_specs=[HBM, VMEM], out_specs=VMEM, out_sha...  3.98 us
  transfers between devices with their start and end apart: 28, of which 14 were waited for; matrix products, arithmetic and copies ran while one was open for 0% of the time, Pallas kernels for 20%

profile of v2, /device:TPU:1, one launch (start us, length us, event | category | flops | bytes accessed | tf_op | source)
XLA Modules:
  0.0 101.9 jit_solution(7079891036175809177)
XLA Ops:
  0.0 4.0 %pick.1.a_ref = bf16[1,128,512]{2,1,0:T(8,128)(2,1)} custom-call(bf16[512,8192]{1,0:T(8,128)(2,1)} %refs_2_.7, f32[64,128]{1,0:T(8,128)} %bitcast.5), custom_call_target="tpu_custom_call" | custom-call | tf_op jit(solution)/shard_map/panel/pick/pallas_call | solution.py:87
  4.0 1.5 %collective-permute-start = (bf16[1,128,512]{2,1,0:T(8,128)(2,1)}, bf16[1,128,512]{2,1,0:T(8,128)(2,1)S(1)}, u32[]{:S(2)}, u32[]{:S(2)}) collective-permute-start(bf16[1,128,512]{2,1,0:T(8,128)(2,1)} %pick.1.a_ref), channel_id=1, source_target_pairs={{0,8},{8,0},{16,24},{24,16},{32,40},{40,32},{48,56},{56,48},{64,72... | collective-permute-start | bytes 393224 | tf_op jit(solution)/shard_map/panel/ppermute | solution.py:273
  8.0 2.9 %collective-permute-start.1 = (bf16[2,128,512]{2,1,0:T(8,128)(2,1)S(1)}, bf16[2,128,512]{2,1,0:T(8,128)(2,1)S(1)}, u32[]{:S(2)}, u32[]{:S(2)}) collective-permute-start(bf16[2,128,512]{2,1,0:T(8,128)(2,1)S(1)} %get-tuple-element.28), channel_id=1, source_target_pairs={{0,1},{1,0},{2,3},{3,2},{4,5},{5,4},{6,7},{7,6},{8,9},{9,8},{10,11... | collective-permute-start | bytes 786440 | tf_op jit(solution)/shard_map/panel/ppermute | solution.py:281
  10.9 3.8 %collective-permute-start.3 = (bf16[2,128,512]{2,1,0:T(8,128)(2,1)S(1)}, bf16[2,128,512]{2,1,0:T(8,128)(2,1)S(1)}, u32[]{:S(2)}, u32[]{:S(2)}) collective-permute-start(bf16[2,128,512]{2,1,0:T(8,128)(2,1)S(1)} %get-tuple-element.29.refs_0_), channel_id=1, source_target_pairs={{0,2},{1,3},{2,4},{3,5},{4,6},{5,7},{6,0},{7,1},{8,14},{9,15},{10,... | collective-permute-start | bytes 786440 | tf_op jit(solution)/shard_map/panel/ppermute | solution.py:274
  14.7 2.7 %collective-permute-done.1.refs_1_ = bf16[2,128,512]{2,1,0:T(8,128)(2,1)S(1)} collective-permute-done((bf16[2,128,512]{2,1,0:T(8,128)(2,1)S(1)}, bf16[2,128,512]{2,1,0:T(8,128)(2,1)S(1)}, u32[]{:S(2)}, u32[]{:S(2)}) %collective-permute-start.1) | collective-permute-done | bytes 262176 | tf_op jit(solution)/shard_map/panel/ppermute | solution.py:281
  17.3 3.8 %collective-permute-start.2 = (bf16[2,128,512]{2,1,0:T(8,128)(2,1)S(1)}, bf16[2,128,512]{2,1,0:T(8,128)(2,1)S(1)}, u32[]{:S(2)}, u32[]{:S(2)}) collective-permute-start(bf16[2,128,512]{2,1,0:T(8,128)(2,1)S(1)} %collective-permute-done.1.refs_1_), channel_id=1, source_target_pairs={{0,2},{1,3},{2,4},{3,5},{4,6},{5,7},{6,0},{7,1},{8,14},{9,15},{10,... | collective-permute-start | bytes 786440 | tf_op jit(solution)/shard_map/panel/ppermute | solution.py:274
  21.2 3.4 %copy-done = bf16[512,8192]{1,0:T(8,128)(2,1)S(1)} copy-done((bf16[512,8192]{1,0:T(8,128)(2,1)S(1)}, bf16[512,8192]{1,0:T(8,128)(2,1)}, u32[]{:S(2)}) %copy-start) | copy-done | bytes 8388632
  24.6 2.5 %m12y.2 = (bf16[2,256,512]{2,1,0:T(8,128)(2,1)S(1)}, bf16[2,256,512]{2,1,0:T(8,128)(2,1)S(1)}) custom-call(bf16[2,128,512]{2,1,0:T(8,128)(2,1)S(1)} %get-tuple-element.29.refs_0_, bf16[2,128,512]{2,1,0:T(8,128)(2,1)S(1)} %collective-permute-done.1.refs_1_, bf16[2,128,512]{2,1,0:T(8,128)(2,1)S(1)} %collective-permute-done.3.refs_2_.zero, ...), custom_call_target="tpu_custom_call" | custom-call | flops 1073741824 | bytes 4194304 | tf_op jit(solution)/shard_map/y_then_x/m12y/pallas_call | solution.py:193
  27.1 2.0 %xe.1.refs_5_ = bf16[4,128,512]{2,1,0:T(8,128)(2,1)S(1)} custom-call(bf16[2,128,512]{2,1,0:T(8,128)(2,1)S(1)} %collective-permute-done.2.one.refs_0_, bf16[512,8192]{1,0:T(8,128)(2,1)S(1)} %copy-done, bf16[512,8192]{1,0:T(8,128)(2,1)S(1)} %collective-permute-done.4.refs_4_.refs_2_.refs_3_, bf16[2,256,512]{2,1,0:T(8,128)(2,1)S(1)} %get-tuple-element.31.after.refs_3_), custom_call_target="tpu_custom_call" | custom-call | flops 536870912 | bytes 4194304 | tf_op jit(solution)/shard_map/x_then_y_send/xe/pallas_call | solution.py:193
  30.4 2.7 %collective-permute-start.9 = (bf16[2,256,512]{2,1,0:T(8,128)(2,1)S(1)}, bf16[2,256,512]{2,1,0:T(8,128)(2,1)S(1)}, u32[]{:S(2)}, u32[]{:S(2)}) collective-permute-start(bf16[2,256,512]{2,1,0:T(8,128)(2,1)S(1)} %get-tuple-element.31.after.refs_3_), channel_id=1, source_target_pairs={{0,16},{8,56},{16,32},{24,8},{32,48},{40,24},{48,0},{56,40},{64,80... | collective-permute-start | bytes 1572872 | tf_op jit(solution)/shard_map/y_then_x/ppermute | solution.py:286
  33.2 2.8 %collective-permute-start.5 = (bf16[2,128,512]{2,1,0:T(8,128)(2,1)S(1)}, bf16[2,128,512]{2,1,0:T(8,128)(2,1)S(1)}, u32[]{:S(2)}, u32[]{:S(2)}) collective-permute-start(bf16[2,128,512]{2,1,0:T(8,128)(2,1)S(1)} %choose.1), channel_id=1, source_target_pairs={{0,2},{1,3},{2,4},{3,5},{4,6},{5,7},{6,0},{7,1},{8,14},{9,15},{10,... | collective-permute-start | bytes 786440 | tf_op jit(solution)/shard_map/x_then_y_send/ppermute | solution.py:274
  36.0 2.5 %m12y.3 = (bf16[2,256,512]{2,1,0:T(8,128)(2,1)S(1)}, bf16[2,256,512]{2,1,0:T(8,128)(2,1)S(1)}) custom-call(bf16[2,128,512]{2,1,0:T(8,128)(2,1)S(1)} %get-tuple-element.29.refs_0_, bf16[2,128,512]{2,1,0:T(8,128)(2,1)S(1)} %collective-permute-done.1.refs_1_, bf16[2,128,512]{2,1,0:T(8,128)(2,1)S(1)} %collective-permute-done.3.refs_2_.zero, ...), custom_call_target="tpu_custom_call" | custom-call | flops 1073741824 | bytes 4194304 | tf_op jit(solution)/shard_map/y_then_x/m12y/pallas_call | solution.py:193
  40.0 2.0 %xl.1.refs_4_ = bf16[4,128,512]{2,1,0:T(8,128)(2,1)S(1)} custom-call(bf16[2,128,512]{2,1,0:T(8,128)(2,1)S(1)} %collective-permute-done.5.refs_0_.refs_1_, bf16[512,8192]{1,0:T(8,128)(2,1)S(1)} %copy-done, bf16[512,8192]{1,0:T(8,128)(2,1)S(1)} %collective-permute-done.4.refs_4_.refs_2_.refs_3_, bf16[2,256,512]{2,1,0:T(8,128)(2,1)S(1)} %get-tuple-element.32.refs_3_), custom_call_target="tpu_custom_call" | custom-call | flops 536870912 | bytes 4194304 | tf_op jit(solution)/shard_map/x_then_y_send/xl/pallas_call | solution.py:193
  42.3 2.5 %x2.1.refs_6_ = bf16[4,256,512]{2,1,0:T(8,128)(2,1)S(1)} custom-call(bf16[2,128,512]{2,1,0:T(8,128)(2,1)S(1)} %collective-permute-done.2.one.refs_0_, bf16[2,128,512]{2,1,0:T(8,128)(2,1)S(1)} %collective-permute-done.5.refs_0_.refs_1_, bf16[512,8192]{1,0:T(8,128)(2,1)S(1)} %copy-done, bf16[512,8192]{1,0:T(8,128)(2,1)S(1)} %collective-permute-done.4.refs_4_.refs_2_.refs_3_, ...), custom_call_target="tpu_custom_call" | custom-call | flops 1073741824 | bytes 4194304 | tf_op jit(solution)/shard_map/x_then_y_send/x2/pallas_call | solution.py:193
  44.9 1.3 %m3y.2.refs_6_ = bf16[2,256,512]{2,1,0:T(8,128)(2,1)S(1)} custom-call(bf16[2,128,512]{2,1,0:T(8,128)(2,1)S(1)} %get-tuple-element.29.refs_0_, bf16[2,128,512]{2,1,0:T(8,128)(2,1)S(1)} %collective-permute-done.1.refs_1_, bf16[2,128,512]{2,1,0:T(8,128)(2,1)S(1)} %collective-permute-done.3.refs_2_.zero, bf16[512,8192]{1,0:T(8,128)(2,1)S(1)} %copy-done, ...), custom_call_target="tpu_custom_call" | custom-call | flops 536870912 | bytes 2097152 | tf_op jit(solution)/shard_map/y_then_x/m3y/pallas_call | solution.py:193
  46.2 1.7 %collective-permute-start.10 = (bf16[2,256,512]{2,1,0:T(8,128)(2,1)S(1)}, bf16[2,256,512]{2,1,0:T(8,128)(2,1)S(1)}, u32[]{:S(2)}, u32[]{:S(2)}) collective-permute-start(bf16[2,256,512]{2,1,0:T(8,128)(2,1)S(1)} %m3y.2.refs_6_), channel_id=1, source_target_pairs={{0,16},{8,56},{16,32},{24,8},{32,48},{40,24},{48,0},{56,40},{64,80... | collective-permute-start | bytes 1572872 | tf_op jit(solution)/shard_map/y_then_x/ppermute | solution.py:286
  49.2 3.0 %collective-permute-done.12.refs_5_ = bf16[2,256,512]{2,1,0:T(8,128)(2,1)S(1)} collective-permute-done((bf16[2,256,512]{2,1,0:T(8,128)(2,1)S(1)}, bf16[2,256,512]{2,1,0:T(8,128)(2,1)S(1)}, u32[]{:S(2)}, u32[]{:S(2)}) %collective-permute-start.12) | collective-permute-done | bytes 524320 | tf_op jit(solution)/shard_map/y_then_x/ppermute | solution.py:286
  53.5 2.1 %collective-permute-done.8.refs_8_.refs_5_ = bf16[4,128,512]{2,1,0:T(8,128)(2,1)S(1)} collective-permute-done((bf16[4,128,512]{2,1,0:T(8,128)(2,1)S(1)}, bf16[4,128,512]{2,1,0:T(8,128)(2,1)S(1)}, u32[]{:S(2)}, u32[]{:S(2)}) %collective-permute-start.8) | collective-permute-done | bytes 524320 | tf_op jit(solution)/shard_map/x_then_y_send/ppermute | solution.py:288
  55.6 2.2 %collective-permute-done.10.refs_5_ = bf16[2,256,512]{2,1,0:T(8,128)(2,1)S(1)} collective-permute-done((bf16[2,256,512]{2,1,0:T(8,128)(2,1)S(1)}, bf16[2,256,512]{2,1,0:T(8,128)(2,1)S(1)}, u32[]{:S(2)}, u32[]{:S(2)}) %collective-permute-start.10) | collective-permute-done | bytes 524320 | tf_op jit(solution)/shard_map/y_then_x/ppermute | solution.py:286
  57.8 1.3 %yfg.1 = (bf16[1,256,512]{2,1,0:T(8,128)(2,1)S(1)}, bf16[1,256,512]{2,1,0:T(8,128)(2,1)S(1)}) custom-call(bf16[2,128,512]{2,1,0:T(8,128)(2,1)S(1)} %get-tuple-element.29.refs_0_, bf16[2,128,512]{2,1,0:T(8,128)(2,1)S(1)} %collective-permute-done.1.refs_1_, bf16[2,128,512]{2,1,0:T(8,128)(2,1)S(1)} %collective-permute-done.3.refs_2_.zero, ...), custom_call_target="tpu_custom_call" | custom-call | flops 536870912 | bytes 2097152 | tf_op jit(solution)/shard_map/y_then_x/yfg/pallas_call | solution.py:193
  59.1 2.5 %m12x.1 = (bf16[2,256,512]{2,1,0:T(8,128)(2,1)S(1)}, bf16[2,256,512]{2,1,0:T(8,128)(2,1)S(1)}) custom-call(bf16[2,128,512]{2,1,0:T(8,128)(2,1)S(1)} %collective-permute-done.2.one.refs_0_, bf16[2,128,512]{2,1,0:T(8,128)(2,1)S(1)} %collective-permute-done.5.refs_0_.refs_1_, bf16[512,8192]{1,0:T(8,128)(2,1)S(1)} %copy-done, ...), custom_call_target="tpu_custom_call" | custom-call | flops 1073741824 | bytes 4194304 | tf_op jit(solution)/shard_map/x_then_y/m12x/pallas_call | solution.py:193
  61.7 1.8 %collective-permute-start.13 = (bf16[2,256,512]{2,1,0:T(8,128)(2,1)S(1)}, bf16[2,256,512]{2,1,0:T(8,128)(2,1)S(1)}, u32[]{:S(2)}, u32[]{:S(2)}) collective-permute-start(bf16[2,256,512]{2,1,0:T(8,128)(2,1)S(1)} %get-tuple-element.35.refs_6_), channel_id=1, source_target_pairs={{0,16},{8,56},{16,32},{24,8},{32,48},{40,24},{48,0},{56,40},{64,80... | collective-permute-start | bytes 1572872 | tf_op jit(solution)/shard_map/x_then_y/ppermute | solution.py:286
  63.4 2.7 %collective-permute-start.16 = (bf16[2,256,512]{2,1,0:T(8,128)(2,1)S(1)}, bf16[2,256,512]{2,1,0:T(8,128)(2,1)S(1)}, u32[]{:S(2)}, u32[]{:S(2)}) collective-permute-start(bf16[2,256,512]{2,1,0:T(8,128)(2,1)S(1)} %m3y.3.refs_7_), channel_id=1, source_target_pairs={{0,16},{8,56},{16,32},{24,8},{32,48},{40,24},{48,0},{56,40},{64,80... | collective-permute-start | bytes 1572872 | tf_op jit(solution)/shard_map/y_then_x/ppermute | solution.py:286
  66.1 11.9 %collective-permute-done.6.refs_4_ = bf16[4,256,512]{2,1,0:T(8,128)(2,1)S(1)} collective-permute-done((bf16[4,256,512]{2,1,0:T(8,128)(2,1)S(1)}, bf16[4,256,512]{2,1,0:T(8,128)(2,1)S(1)}, u32[]{:S(2)}, u32[]{:S(2)}) %collective-permute-start.6) | collective-permute-done | bytes 1048608 | tf_op jit(solution)/shard_map/x_then_y_send/ppermute | solution.py:288
  78.1 1.3 %m3x.1.refs_7_ = bf16[2,256,512]{2,1,0:T(8,128)(2,1)S(1)} custom-call(bf16[2,128,512]{2,1,0:T(8,128)(2,1)S(1)} %collective-permute-done.2.one.refs_0_, bf16[2,128,512]{2,1,0:T(8,128)(2,1)S(1)} %collective-permute-done.5.refs_0_.refs_1_, bf16[512,8192]{1,0:T(8,128)(2,1)S(1)} %copy-done, bf16[512,8192]{1,0:T(8,128)(2,1)S(1)} %collective-permute-done.4.refs_4_.refs_2_.refs_3_, ...), custom_call_target="tpu_custom_call" | custom-call | flops 536870912 | bytes 2097152 | tf_op jit(solution)/shard_map/x_then_y/m3x/pallas_call | solution.py:193
  79.4 2.0 %collective-permute-start.14 = (bf16[2,256,512]{2,1,0:T(8,128)(2,1)S(1)}, bf16[2,256,512]{2,1,0:T(8,128)(2,1)S(1)}, u32[]{:S(2)}, u32[]{:S(2)}) collective-permute-start(bf16[2,256,512]{2,1,0:T(8,128)(2,1)S(1)} %m3x.1.refs_7_), channel_id=1, source_target_pairs={{0,16},{8,56},{16,32},{24,8},{32,48},{40,24},{48,0},{56,40},{64,80... | collective-permute-start | bytes 1572872 | tf_op jit(solution)/shard_map/x_then_y/ppermute | solution.py:286
  82.2 3.4 %collective-permute-done.16.refs_5_ = bf16[2,256,512]{2,1,0:T(8,128)(2,1)S(1)} collective-permute-done((bf16[2,256,512]{2,1,0:T(8,128)(2,1)S(1)}, bf16[2,256,512]{2,1,0:T(8,128)(2,1)S(1)}, u32[]{:S(2)}, u32[]{:S(2)}) %collective-permute-start.16) | collective-permute-done | bytes 524320 | tf_op jit(solution)/shard_map/y_then_x/ppermute | solution.py:286
  86.9 2.2 %collective-permute-start.22 = (f32[1,64,512]{2,1,0:T(8,128)S(1)}, f32[1,64,512]{2,1,0:T(8,128)S(1)}, u32[]{:S(2)}, u32[]{:S(2)}) collective-permute-start(f32[1,64,512]{2,1,0:T(8,128)S(1)} %get-tuple-element.44), channel_id=1, source_target_pairs={{0,8},{8,0},{16,24},{24,16},{32,40},{40,32},{48,56},{56,48},{64,72... | collective-permute-start | bytes 393224 | tf_op jit(solution)/shard_map/last/ppermute | solution.py:273
  89.9 2.7 %collective-permute-done.14.refs_5_ = bf16[2,256,512]{2,1,0:T(8,128)(2,1)S(1)} collective-permute-done((bf16[2,256,512]{2,1,0:T(8,128)(2,1)S(1)}, bf16[2,256,512]{2,1,0:T(8,128)(2,1)S(1)}, u32[]{:S(2)}, u32[]{:S(2)}) %collective-permute-start.14) | collective-permute-done | bytes 524320 | tf_op jit(solution)/shard_map/x_then_y/ppermute | solution.py:286
  92.5 2.1 %collective-permute-start.24 = (f32[1,64,512]{2,1,0:T(8,128)S(1)}, f32[1,64,512]{2,1,0:T(8,128)S(1)}, u32[]{:S(2)}, u32[]{:S(2)}) collective-permute-start(f32[1,64,512]{2,1,0:T(8,128)S(1)} %get-tuple-element.46), channel_id=1, source_target_pairs={{0,8},{8,0},{16,24},{24,16},{32,40},{40,32},{48,56},{56,48},{64,72... | collective-permute-start | bytes 393224 | tf_op jit(solution)/shard_map/last/ppermute | solution.py:273
  94.9 1.4 %xos.1 = (f32[1,256,512]{2,1,0:T(8,128)S(1)}, f32[1,64,512]{2,1,0:T(8,128)S(1)}, f32[1,64,512]{2,1,0:T(8,128)S(1)}, f32[1,64,512]{2,1,0:T(8,128)S(1)}, f32[1,64,512]{2,1,0:T(8,128)S(1)}) custom-call(bf16[2,128,512]{2,1,0:T(8,128)(2,1)S(1)} %collective-permute-done.2.one.refs_0_, bf16[2,128,512]{2,1,0:T(8,128)(2,1)S(1)} %collective-permute-done.5.refs_0_.refs_1_, ...), custom_call_target="tpu_custom_call" | custom-call | flops 536870912 | bytes 2097152 | tf_op jit(solution)/shard_map/last/xos/pallas_call | solution.py:193
  98.8 3.1 %final.1 = f32[512,1024]{1,0:T(8,128)} custom-call(s32[4,16]{1,0:T(4,128)S(1)} %copy-done.2, f32[1,256,512]{2,1,0:T(8,128)S(1)} %get-tuple-element.39.refs_0_, f32[1,64,512]{2,1,0:T(8,128)S(1)} %collective-permute-done.18.refs_1_, f32[1,64,512]{2,1,0:T(8,128)S(1)} %collective-permute-done.19.refs_2_, f32[1,64,512]{2,1,0:T(8,128)S(1)} %collective-permute-done.20.refs_3_, ...), custom_call_target="tpu_custom_call" | custom-call | tf_op jit(solution)/shard_map/last/final/pallas_call | solution.py:251
  (56 shorter events, 13.8 us)
Async XLA Ops:
  4.0 2.7 %collective-permute-start = (bf16[1,128,512]{2,1,0:T(8,128)(2,1)}, bf16[1,128,512]{2,1,0:T(8,128)(2,1)S(1)}, u32[]{:S(2)}, u32[]{:S(2)}) collective-permute-start(bf16[1,128,512]{2,1,0:T(8,128)(2,1)} %pick.1.a_ref), channel_id=1, source_target_pairs={{0,8},{8,0},{16,24},{24,16},{32,40},{40,32},{48,56},{56,48},{64,72... | collective-permute-start | bytes 393224 | tf_op jit(solution)/shard_map/panel/ppermute | solution.py:273
  6.7 14.5 %collective-permute-start.4 = (bf16[512,8192]{1,0:T(8,128)(2,1)}, bf16[512,8192]{1,0:T(8,128)(2,1)S(1)}, u32[]{:S(2)}, u32[]{:S(2)}) collective-permute-start(bf16[512,8192]{1,0:T(8,128)(2,1)} %refs_2_.7), channel_id=1, source_target_pairs={{0,8},{8,0},{16,24},{24,16},{32,40},{40,32},{48,56},{56,48},{64,72... | collective-permute-start | bytes 25165832 | tf_op jit(solution)/shard_map/panel/ppermute | solution.py:273
  8.0 9.3 %collective-permute-start.1 = (bf16[2,128,512]{2,1,0:T(8,128)(2,1)S(1)}, bf16[2,128,512]{2,1,0:T(8,128)(2,1)S(1)}, u32[]{:S(2)}, u32[]{:S(2)}) collective-permute-start(bf16[2,128,512]{2,1,0:T(8,128)(2,1)S(1)} %get-tuple-element.28), channel_id=1, source_target_pairs={{0,1},{1,0},{2,3},{3,2},{4,5},{5,4},{6,7},{7,6},{8,9},{9,8},{10,11... | collective-permute-start | bytes 786440 | tf_op jit(solution)/shard_map/panel/ppermute | solution.py:281
  10.9 10.3 %collective-permute-start.3 = (bf16[2,128,512]{2,1,0:T(8,128)(2,1)S(1)}, bf16[2,128,512]{2,1,0:T(8,128)(2,1)S(1)}, u32[]{:S(2)}, u32[]{:S(2)}) collective-permute-start(bf16[2,128,512]{2,1,0:T(8,128)(2,1)S(1)} %get-tuple-element.29.refs_0_), channel_id=1, source_target_pairs={{0,2},{1,3},{2,4},{3,5},{4,6},{5,7},{6,0},{7,1},{8,14},{9,15},{10,... | collective-permute-start | bytes 786440 | tf_op jit(solution)/shard_map/panel/ppermute | solution.py:274
  17.3 9.8 %collective-permute-start.2 = (bf16[2,128,512]{2,1,0:T(8,128)(2,1)S(1)}, bf16[2,128,512]{2,1,0:T(8,128)(2,1)S(1)}, u32[]{:S(2)}, u32[]{:S(2)}) collective-permute-start(bf16[2,128,512]{2,1,0:T(8,128)(2,1)S(1)} %collective-permute-done.1.refs_1_), channel_id=1, source_target_pairs={{0,2},{1,3},{2,4},{3,5},{4,6},{5,7},{6,0},{7,1},{8,14},{9,15},{10,... | collective-permute-start | bytes 786440 | tf_op jit(solution)/shard_map/panel/ppermute | solution.py:274
  29.1 15.7 %collective-permute-start.7 = (bf16[4,128,512]{2,1,0:T(8,128)(2,1)S(1)}, bf16[4,128,512]{2,1,0:T(8,128)(2,1)S(1)}, u32[]{:S(2)}, u32[]{:S(2)}) collective-permute-start(bf16[4,128,512]{2,1,0:T(8,128)(2,1)S(1)} %xe.1.refs_5_), channel_id=1, source_target_pairs={{0,64},{8,72},{16,80},{24,88},{32,96},{40,104},{48,112},{56,120},{... | collective-permute-start | bytes 1572872 | tf_op jit(solution)/shard_map/x_then_y_send/ppermute | solution.py:288
  30.4 14.5 %collective-permute-start.9 = (bf16[2,256,512]{2,1,0:T(8,128)(2,1)S(1)}, bf16[2,256,512]{2,1,0:T(8,128)(2,1)S(1)}, u32[]{:S(2)}, u32[]{:S(2)}) collective-permute-start(bf16[2,256,512]{2,1,0:T(8,128)(2,1)S(1)} %get-tuple-element.31.after.refs_3_), channel_id=1, source_target_pairs={{0,16},{8,56},{16,32},{24,8},{32,48},{40,24},{48,0},{56,40},{64,80... | collective-permute-start | bytes 1572872 | tf_op jit(solution)/shard_map/y_then_x/ppermute | solution.py:286
  33.2 6.9 %collective-permute-start.5 = (bf16[2,128,512]{2,1,0:T(8,128)(2,1)S(1)}, bf16[2,128,512]{2,1,0:T(8,128)(2,1)S(1)}, u32[]{:S(2)}, u32[]{:S(2)}) collective-permute-start(bf16[2,128,512]{2,1,0:T(8,128)(2,1)S(1)} %choose.1), channel_id=1, source_target_pairs={{0,2},{1,3},{2,4},{3,5},{4,6},{5,7},{6,0},{7,1},{8,14},{9,15},{10,... | collective-permute-start | bytes 786440 | tf_op jit(solution)/shard_map/x_then_y_send/ppermute | solution.py:274
  38.5 13.7 %collective-permute-start.12 = (bf16[2,256,512]{2,1,0:T(8,128)(2,1)S(1)}, bf16[2,256,512]{2,1,0:T(8,128)(2,1)S(1)}, u32[]{:S(2)}, u32[]{:S(2)}) collective-permute-start(bf16[2,256,512]{2,1,0:T(8,128)(2,1)S(1)} %get-tuple-element.32.refs_3_), channel_id=1, source_target_pairs={{0,16},{8,56},{16,32},{24,8},{32,48},{40,24},{48,0},{56,40},{64,80... | collective-permute-start | bytes 1572872 | tf_op jit(solution)/shard_map/y_then_x/ppermute | solution.py:286
  39.0 14.5 %collective-permute-start.11 = (bf16[2,256,512]{2,1,0:T(8,128)(2,1)S(1)}, bf16[2,256,512]{2,1,0:T(8,128)(2,1)S(1)}, u32[]{:S(2)}, u32[]{:S(2)}) collective-permute-start(bf16[2,256,512]{2,1,0:T(8,128)(2,1)S(1)} %get-tuple-element.33), channel_id=1, source_target_pairs={{0,48},{8,24},{16,0},{24,40},{32,16},{40,56},{48,32},{56,8},{64,11... | collective-permute-start | bytes 1572872 | tf_op jit(solution)/shard_map/y_then_x/ppermute | solution.py:287
  42.0 13.6 %collective-permute-start.8 = (bf16[4,128,512]{2,1,0:T(8,128)(2,1)S(1)}, bf16[4,128,512]{2,1,0:T(8,128)(2,1)S(1)}, u32[]{:S(2)}, u32[]{:S(2)}) collective-permute-start(bf16[4,128,512]{2,1,0:T(8,128)(2,1)S(1)} %xl.1.refs_4_), channel_id=1, source_target_pairs={{0,64},{8,72},{16,80},{24,88},{32,96},{40,104},{48,112},{56,120},{... | collective-permute-start | bytes 1572872 | tf_op jit(solution)/shard_map/x_then_y_send/ppermute | solution.py:288
  46.2 11.6 %collective-permute-start.10 = (bf16[2,256,512]{2,1,0:T(8,128)(2,1)S(1)}, bf16[2,256,512]{2,1,0:T(8,128)(2,1)S(1)}, u32[]{:S(2)}, u32[]{:S(2)}) collective-permute-start(bf16[2,256,512]{2,1,0:T(8,128)(2,1)S(1)} %m3y.2.refs_6_), channel_id=1, source_target_pairs={{0,16},{8,56},{16,32},{24,8},{32,48},{40,24},{48,0},{56,40},{64,80... | collective-permute-start | bytes 1572872 | tf_op jit(solution)/shard_map/y_then_x/ppermute | solution.py:286
  47.9 30.1 %collective-permute-start.6 = (bf16[4,256,512]{2,1,0:T(8,128)(2,1)S(1)}, bf16[4,256,512]{2,1,0:T(8,128)(2,1)S(1)}, u32[]{:S(2)}, u32[]{:S(2)}) collective-permute-start(bf16[4,256,512]{2,1,0:T(8,128)(2,1)S(1)} %x2.1.refs_6_), channel_id=1, source_target_pairs={{0,64},{8,72},{16,80},{24,88},{32,96},{40,104},{48,112},{56,120},{... | collective-permute-start | bytes 3145736 | tf_op jit(solution)/shard_map/x_then_y_send/ppermute | solution.py:288
  61.7 16.4 %collective-permute-start.13 = (bf16[2,256,512]{2,1,0:T(8,128)(2,1)S(1)}, bf16[2,256,512]{2,1,0:T(8,128)(2,1)S(1)}, u32[]{:S(2)}, u32[]{:S(2)}) collective-permute-start(bf16[2,256,512]{2,1,0:T(8,128)(2,1)S(1)} %get-tuple-element.35.refs_6_), channel_id=1, source_target_pairs={{0,16},{8,56},{16,32},{24,8},{32,48},{40,24},{48,0},{56,40},{64,80... | collective-permute-start | bytes 1572872 | tf_op jit(solution)/shard_map/x_then_y/ppermute | solution.py:286
  63.4 18.6 %collective-permute-start.17 = (bf16[2,256,512]{2,1,0:T(8,128)(2,1)S(1)}, bf16[2,256,512]{2,1,0:T(8,128)(2,1)S(1)}, u32[]{:S(2)}, u32[]{:S(2)}) collective-permute-start(bf16[2,256,512]{2,1,0:T(8,128)(2,1)S(1)} %get-tuple-element.37), channel_id=1, source_target_pairs={{0,48},{8,24},{16,0},{24,40},{32,16},{40,56},{48,32},{56,8},{64,11... | collective-permute-start | bytes 1572872 | tf_op jit(solution)/shard_map/y_then_x/ppermute | solution.py:287
  63.4 22.2 %collective-permute-start.16 = (bf16[2,256,512]{2,1,0:T(8,128)(2,1)S(1)}, bf16[2,256,512]{2,1,0:T(8,128)(2,1)S(1)}, u32[]{:S(2)}, u32[]{:S(2)}) collective-permute-start(bf16[2,256,512]{2,1,0:T(8,128)(2,1)S(1)} %m3y.3.refs_7_), channel_id=1, source_target_pairs={{0,16},{8,56},{16,32},{24,8},{32,48},{40,24},{48,0},{56,40},{64,80... | collective-permute-start | bytes 1572872 | tf_op jit(solution)/shard_map/y_then_x/ppermute | solution.py:286
  66.1 16.1 %copy-start.5 = (s32[8,2]{0,1:T(2,128)S(1)}, s32[8,2]{0,1:T(2,128)}, u32[]{:S(2)}) copy-start(s32[8,2]{0,1:T(2,128)} %param.8) | copy-start | bytes 196
  66.1 23.7 %collective-permute-start.15 = (bf16[2,256,512]{2,1,0:T(8,128)(2,1)S(1)}, bf16[2,256,512]{2,1,0:T(8,128)(2,1)S(1)}, u32[]{:S(2)}, u32[]{:S(2)}) collective-permute-start(bf16[2,256,512]{2,1,0:T(8,128)(2,1)S(1)} %get-tuple-element.36), channel_id=1, source_target_pairs={{0,48},{8,24},{16,0},{24,40},{32,16},{40,56},{48,32},{56,8},{64,11... | collective-permute-start | bytes 1572872 | tf_op jit(solution)/shard_map/x_then_y/ppermute | solution.py:287
  79.4 13.2 %collective-permute-start.14 = (bf16[2,256,512]{2,1,0:T(8,128)(2,1)S(1)}, bf16[2,256,512]{2,1,0:T(8,128)(2,1)S(1)}, u32[]{:S(2)}, u32[]{:S(2)}) collective-permute-start(bf16[2,256,512]{2,1,0:T(8,128)(2,1)S(1)} %m3x.1.refs_7_), channel_id=1, source_target_pairs={{0,16},{8,56},{16,32},{24,8},{32,48},{40,24},{48,0},{56,40},{64,80... | collective-permute-start | bytes 1572872 | tf_op jit(solution)/shard_map/x_then_y/ppermute | solution.py:286
  81.3 15.0 %collective-permute-start.26 = (bf16[1,256,512]{2,1,0:T(8,128)(2,1)S(1)}, bf16[1,256,512]{2,1,0:T(8,128)(2,1)S(1)}, u32[]{:S(2)}, u32[]{:S(2)}) collective-permute-start(bf16[1,256,512]{2,1,0:T(8,128)(2,1)S(1)} %get-tuple-element.34.refs_6_), channel_id=1, source_target_pairs={{0,64},{8,72},{16,80},{24,88},{32,96},{40,104},{48,112},{56,120},{... | collective-permute-start | bytes 786440 | tf_op jit(solution)/shard_map/y_then_x/ppermute | solution.py:288
  82.1 14.4 %collective-permute-start.27 = (bf16[1,256,512]{2,1,0:T(8,128)(2,1)S(1)}, bf16[1,256,512]{2,1,0:T(8,128)(2,1)S(1)}, u32[]{:S(2)}, u32[]{:S(2)}) collective-permute-start(bf16[1,256,512]{2,1,0:T(8,128)(2,1)S(1)} %get-tuple-element.48), channel_id=1, source_target_pairs={{0,72},{8,64},{16,88},{24,80},{32,104},{40,96},{48,120},{56,112},{... | collective-permute-start | bytes 786440 | tf_op jit(solution)/shard_map/y_then_x/ppermute | solution.py:346
  82.2 12.4 %copy-start.3 = (f32[4096]{0:T(1024)S(1)}, f32[4096]{0:T(1024)}, u32[]{:S(2)}) copy-start(f32[4096]{0:T(1024)} %param.9) | copy-start | bytes 49156
  82.2 12.4 %copy-start.4 = (f32[4096]{0:T(1024)S(1)}, f32[4096]{0:T(1024)}, u32[]{:S(2)}) copy-start(f32[4096]{0:T(1024)} %param.10) | copy-start | bytes 49156
  86.9 10.0 %collective-permute-start.22 = (f32[1,64,512]{2,1,0:T(8,128)S(1)}, f32[1,64,512]{2,1,0:T(8,128)S(1)}, u32[]{:S(2)}, u32[]{:S(2)}) collective-permute-start(f32[1,64,512]{2,1,0:T(8,128)S(1)} %get-tuple-element.44), channel_id=1, source_target_pairs={{0,8},{8,0},{16,24},{24,16},{32,40},{40,32},{48,56},{56,48},{64,72... | collective-permute-start | bytes 393224 | tf_op jit(solution)/shard_map/last/ppermute | solution.py:273
  89.9 7.2 %collective-permute-start.23 = (f32[1,64,512]{2,1,0:T(8,128)S(1)}, f32[1,64,512]{2,1,0:T(8,128)S(1)}, u32[]{:S(2)}, u32[]{:S(2)}) collective-permute-start(f32[1,64,512]{2,1,0:T(8,128)S(1)} %get-tuple-element.45), channel_id=1, source_target_pairs={{0,8},{8,0},{16,24},{24,16},{32,40},{40,32},{48,56},{56,48},{64,72... | collective-permute-start | bytes 393224 | tf_op jit(solution)/shard_map/last/ppermute | solution.py:273
  92.5 4.9 %collective-permute-start.24 = (f32[1,64,512]{2,1,0:T(8,128)S(1)}, f32[1,64,512]{2,1,0:T(8,128)S(1)}, u32[]{:S(2)}, u32[]{:S(2)}) collective-permute-start(f32[1,64,512]{2,1,0:T(8,128)S(1)} %get-tuple-element.46), channel_id=1, source_target_pairs={{0,8},{8,0},{16,24},{24,16},{32,40},{40,32},{48,56},{56,48},{64,72... | collective-permute-start | bytes 393224 | tf_op jit(solution)/shard_map/last/ppermute | solution.py:273
  94.9 3.9 %copy-start.2 = (s32[4,16]{1,0:T(4,128)S(1)}, s32[4,16]{1,0:T(4,128)}, u32[]{:S(2)}) copy-start(s32[4,16]{1,0:T(4,128)} %mask.1) | copy-start | bytes 772
  96.3 1.4 %collective-permute-start.25 = (f32[1,64,512]{2,1,0:T(8,128)S(1)}, f32[1,64,512]{2,1,0:T(8,128)S(1)}, u32[]{:S(2)}, u32[]{:S(2)}) collective-permute-start(f32[1,64,512]{2,1,0:T(8,128)S(1)} %get-tuple-element.47), channel_id=1, source_target_pairs={{0,8},{8,0},{16,24},{24,16},{32,40},{40,32},{48,56},{56,48},{64,72... | collective-permute-start | bytes 393224 | tf_op jit(solution)/shard_map/last/ppermute | solution.py:273
  96.4 1.5 %collective-permute-start.18 = (f32[1,64,512]{2,1,0:T(8,128)S(1)}, f32[1,64,512]{2,1,0:T(8,128)S(1)}, u32[]{:S(2)}, u32[]{:S(2)}) collective-permute-start(f32[1,64,512]{2,1,0:T(8,128)S(1)} %get-tuple-element.40), channel_id=1, source_target_pairs={{0,8},{8,0},{16,24},{24,16},{32,40},{40,32},{48,56},{56,48},{64,72... | collective-permute-start | bytes 393224 | tf_op jit(solution)/shard_map/last/ppermute | solution.py:273
  96.9 1.3 %collective-permute-start.19 = (f32[1,64,512]{2,1,0:T(8,128)S(1)}, f32[1,64,512]{2,1,0:T(8,128)S(1)}, u32[]{:S(2)}, u32[]{:S(2)}) collective-permute-start(f32[1,64,512]{2,1,0:T(8,128)S(1)} %get-tuple-element.41), channel_id=1, source_target_pairs={{0,8},{8,0},{16,24},{24,16},{32,40},{40,32},{48,56},{56,48},{64,72... | collective-permute-start | bytes 393224 | tf_op jit(solution)/shard_map/last/ppermute | solution.py:273
  97.0 1.4 %collective-permute-start.20 = (f32[1,64,512]{2,1,0:T(8,128)S(1)}, f32[1,64,512]{2,1,0:T(8,128)S(1)}, u32[]{:S(2)}, u32[]{:S(2)}) collective-permute-start(f32[1,64,512]{2,1,0:T(8,128)S(1)} %get-tuple-element.42), channel_id=1, source_target_pairs={{0,8},{8,0},{16,24},{24,16},{32,40},{40,32},{48,56},{56,48},{64,72... | collective-permute-start | bytes 393224 | tf_op jit(solution)/shard_map/last/ppermute | solution.py:273
  97.4 1.3 %collective-permute-start.21 = (f32[1,64,512]{2,1,0:T(8,128)S(1)}, f32[1,64,512]{2,1,0:T(8,128)S(1)}, u32[]{:S(2)}, u32[]{:S(2)}) collective-permute-start(f32[1,64,512]{2,1,0:T(8,128)S(1)} %get-tuple-element.43), channel_id=1, source_target_pairs={{0,8},{8,0},{16,24},{24,16},{32,40},{40,32},{48,56},{56,48},{64,72... | collective-permute-start | bytes 393224 | tf_op jit(solution)/shard_map/last/ppermute | solution.py:273
  (2 other events, 4.3 us)

commit v3 on v2

--- a/solution.py
+++ b/solution.py
@@ -93,7 +93,7 @@
             pltpu.VMEM((k, N_COMP * TILE), BF16),
             pltpu.SemaphoreType.DMA((N_COMP,)),
         ],
-        compiler_params=pltpu.CompilerParams(vmem_limit_bytes=NO_ROOM),
+        compiler_params=pltpu.CompilerParams(vmem_limit_bytes=LIMIT),
         name="pick",
     )(dens, coulomb.reshape(coulomb.shape[0] // TILE, TILE))
 
@@ -167,18 +167,21 @@
             piece = acc[g * part : (g + 1) * part]
             for a, where in terms:
                 if isinstance(a, tuple):
-                    piece += adds[a[g]][where(b)].astype(F32)
+                    piece += adds[a[g]][where(b, g)].astype(F32)
                 else:
                     piece += adds[a][where(b), g * part : (g + 1) * part].astype(F32)
             if isinstance(out, tuple):
                 step = rows // len(out)
                 for m in range(g * part // step, (g + 1) * part // step):
                     outs[out[m]][slot] = piece[m * step - g * part : (m + 1) * step - g * part]
+            elif isinstance(slot, tuple):
+                if slot[g] is not None:
+                    outs[out][slot[g]] = piece.astype(outs[out].dtype)
             else:
                 outs[out][slot, g * part : (g + 1) * part] = piece.astype(outs[out].dtype)
 
 
-def mm(name, groups, dens, work, outs, adds=(), after=(), limit=LIMIT):
+def mm(name, groups, dens, work, outs, adds=(), after=(), limit=LIMIT, weight=1):
     k = dens[0].shape[0]
     rows = 128 * len(groups)
     n = len(work)
@@ -197,66 +200,78 @@
         out_shape=[jax.ShapeDtypeStruct((m, out_rows or rows, QB), dtype) for m, dtype, out_rows in outs],
         scratch_shapes=[pltpu.VMEM((n, k, QB), BF16)] * 2 + [pltpu.SemaphoreType.DMA((2, n))],
         cost_estimate=pl.CostEstimate(
-            flops=4 * n * rows * k * QB, bytes_accessed=4 * n * k * QB, transcendentals=0
+            flops=4 * n * rows * k * QB * weight, bytes_accessed=4 * n * k * QB, transcendentals=0
         ),
         compiler_params=pltpu.CompilerParams(vmem_limit_bytes=limit),
         name=name,
     )(*panels, *dens, *adds, *after)
 
 
-def final_kernel(mask, *refs):
-    b = place_facts()
-    z, half, core = b[4], b[5], b[2]
-    (xo, *xr), (yo, *yr), (fo, fr, diag, o_ref, t_ref) = refs[:5], refs[5:10], refs[10:]
-
-    def pair_at(dz, dh):
-        return ((z + dz + NZ) % NZ) * NH + (half + dh) % NH
-
-    def place(value, c, p):
-        for t in range(QB // TILE):
-            scale = (2 * mask[t, c]).astype(F32)
-            at = pl.ds(pl.multiple_of((c * N_PAIR + p) * 8, 8), 8)
-            t_ref[at, t * TILE : (t + 1) * TILE] = value(t) * scale
-
-    order = (((-1, 1), (-2, 0), (0, 0), (-1, 0)), ((1, 1), (2, 1), (0, 1), (1, 0)))
-    for source in range(2):
-        mine = source == 0
-        for g in range(4):
-            spots = [pair_at(*order[s][g]) for s in range(2)]
-            same = core if mine else 1 - core
+ORDER = (((-1, 1), (-2, 0), (0, 0), (-1, 0)), ((1, 1), (2, 1), (0, 1), (1, 0)))
+
+
+def place_rows(b, mask, t_ref, groups, sources):
+    for source, rows_at in enumerate(sources):
+        for n, g in enumerate(groups):
+            spots = [
+                ((b[4] + ORDER[s][g][0] + NZ) % NZ) * NH + (b[5] + ORDER[s][g][1]) % NH
+                for s in range(2)
+            ]
+            same = b[2] if source == 0 else 1 - b[2]
             p = jnp.where(same == 0, spots[0], spots[1])
             for c in range(N_COMP):
-                row = (g % 2) * 128 + c * 8
-                own, swapped, more = (xo, xr, None) if g < 2 else (yo, yr, fo if mine else fr)
-                if mine:
-                    src, at = own, row
-                else:
-                    src, at = swapped[row // 64], row % 64
-
-                def value(t, src=src, at=at, more=more, row=row):
+                at = pl.ds(pl.multiple_of((c * N_PAIR + p) * 8, 8), 8)
+                for t in range(QB // TILE):
                     lanes = slice(t * TILE, (t + 1) * TILE)
-                    out = src[0, at : at + 8, lanes]
-                    if more is not None:
-                        out = out + more[0, row : row + 8, lanes].astype(F32)
-                    return out
-
-                place(value, c, p)
-    here = pl.ds(pl.multiple_of((b[3] * N_PAIR + pair_at(0, 0)) * 8, 8), 8)
+                    scale = (2 * mask[t, c]).astype(F32)
+                    t_ref[at, lanes] = rows_at(n, c * 8, lanes) * scale
+
+
+def gather_y_kernel(mask, yo, ya, yb, fo, fr, t_ref):
+    def mine(n, at, lanes):
+        row = slice(n * 128 + at, n * 128 + at + 8)
+        return yo[0, row, lanes] + fo[0, row, lanes].astype(F32)
+
+    def others(n, at, lanes):
+        row = slice(n * 128 + at, n * 128 + at + 8)
+        return (ya, yb)[n][0, at : at + 8, lanes] + fr[0, row, lanes].astype(F32)
+
+    place_rows(place_facts(), mask, t_ref, (2, 3), (mine, others))
+
+
+def final_kernel(mask, y_rows, xo, xa, xb, diag, o_ref, t_ref):
+    b = place_facts()
+    t_ref[...] = y_rows[...]
+
+    def mine(n, at, lanes):
+        return xo[0, n * 128 + at : n * 128 + at + 8, lanes]
+
+    def others(n, at, lanes):
+        return (xa, xb)[n][0, at : at + 8, lanes]
+
+    place_rows(b, mask, t_ref, (0, 1), (mine, others))
+    here = pl.ds(pl.multiple_of((b[3] * N_PAIR + b[4] * NH + b[5]) * 8, 8), 8)
     t_ref[here, 0:TILE] = t_ref[here, 0:TILE] + diag[...]
     o_ref[...] = t_ref[...].T
 
 
-def final(mask, parts, diag):
-    window = 8 * N_COMP * N_PAIR
+def assemble(name, kernel, mask, parts, out_shape, scratch, weight=1, after=()):
+    def body(*refs):
+        n_in = 1 + len(parts)
+        kernel(*refs[:n_in], *refs[n_in + len(after) :])
+
     return pl.pallas_call(
-        final_kernel,
-        in_specs=[pl.BlockSpec(memory_space=pltpu.SMEM)] + [VMEM] * (len(parts) + 1),
+        body,
+        in_specs=[pl.BlockSpec(memory_space=pltpu.SMEM)] + [VMEM] * len(parts) + [ANY] * len(after),
         out_specs=VMEM,
-        out_shape=jax.ShapeDtypeStruct((QB, window), F32),
-        scratch_shapes=[pltpu.VMEM((window, QB), F32)],
+        out_shape=jax.ShapeDtypeStruct(out_shape, F32),
+        scratch_shapes=[pltpu.VMEM(shape, F32) for shape in scratch],
+        cost_estimate=pl.CostEstimate(
+            flops=1000000000 * weight, bytes_accessed=4 * QB * 1024, transcendentals=0
+        ),
         compiler_params=pltpu.CompilerParams(vmem_limit_bytes=LIMIT),
-        name="final",
-    )(mask, *parts, diag)
+        name=name,
+    )(mask, *parts, *after)
 
 
 def energy_tile(pair_list, valence_energy, conduction_energy):
@@ -290,9 +305,9 @@
     def both(out, start, other_x, dy, terms=()):
         return [
             (
-                out, start + n,
+                out, start + n if isinstance(start, int) else tuple(s if s is None else s + n for s in start),
                 lambda b, n=n: block_of(b, other_x, dy) + n,
-                tuple((a, lambda b, t=t, n=n: t + n) for a, t in terms),
+                tuple((a, lambda b, g=0, t=t, n=n: (t[g] if isinstance(t, tuple) else t) + n) for a, t in terms),
             )
             for n in range(NC)
         ]
@@ -303,7 +318,10 @@
             (
                 out, 0,
                 lambda b, core=core: block_of(b, other_x, 0) + core(b),
-                tuple((a, lambda b, t=t, core=core: t + core(b)) for a, t in terms),
+                tuple(
+                    (a, lambda b, g=0, t=t, core=core: (t[g] if isinstance(t, tuple) else t) + core(b))
+                    for a, t in terms
+                ),
             )
             for out, core in ((out_mine, mine), (out_other, other))
         ]
@@ -327,47 +345,57 @@
     with jax.named_scope("y_then_x"):
         m1o, m1or, m2or = through_y(True)
     with jax.named_scope("x_then_y_send"):
-        far = zmove(choose(near, near2, m1o))
-        xe, = mm("xe", [(near2,)], dens, near_dests, [(4, BF16, 0)], after=(m1o,))
+        chosen = choose(near, near2, m1o)
+        far = zmove(chosen)
+        xe, = mm(
+            "xe", [(near2,)], dens, near_dests + both(0, 4, True, 1), [(6, BF16, 0)], after=(chosen,)
+        )
         xer = across(xe)
     with jax.named_scope("y_then_x"):
         m1w, m1wr, m2wr = through_y(False, after=(xe,))
     with jax.named_scope("x_then_y_send"):
-        xl, = mm("xl", [(far,)], dens, near_dests, [(4, BF16, 0)], after=(m1w,))
+        xl, = mm("xl", [(far,)], dens, near_dests, [(4, BF16, 0)], after=(m1w, m1or, m2or), weight=100)
         xlr = across(xl)
-        x2, = mmx("x2", both(0, 0, True, 1) + both(0, 2, True, 0), [(4, BF16, 0)], after=(xl,))
-        x2r = across(x2)
     with jax.named_scope("y_then_x"):
-        m3o, m3or = through_y_2(True, m1or, (x2, xer))
-        m3w, m3wr = through_y_2(False, m1wr, (m3o,))
-        yf, yg = mmy(
-            "yfg", each(0, 1, True, [(0, 0), (1, 0)]), [(1, BF16, 0)] * 2, [m3or, m2or], after=(m3w, xlr)
-        )
-        fo, fr = across(yf), lax.ppermute(yg, "comp", XCROSS)
+        m3o, m3or = through_y_2(True, m1or, (xl, m2or))
+        x3, = mmx(
+            "x3", both(0, (None, 0), True, 1) + both(0, (2, 4), True, 0), [(6, BF16, 128)], after=(m3o,)
+        )
+        x3r = across(x3)
+        m3w, m3wr = through_y_2(False, m1wr, (x3, m2wr))
     with jax.named_scope("x_then_y"):
         m1x, m2x = mmx(
             "m12x", both(0, 0, False, 2, [((0, 1), 0)]) + both(1, 0, False, -1, [((0, 1), 2)]),
-            [(2, BF16, 0)] * 2, [xer, xlr], after=(yf,),
+            [(2, BF16, 0)] * 2, [xer, xlr], after=(m3w,),
         )
         m1xr, m2xr = ahead(m1x), behind(m2x)
-        m3x, = mmx(
-            "m3x", both(0, 0, False, 1, [(0, 0), (1, 0)]), [(2, BF16, 0)], [x2r, m1xr], after=(m1x,)
-        )
-        m3xr = ahead(m3x)
-
-    split = [(1, F32, 0)] + [(1, F32, 64)] * 4
+        yf, yg = mmy(
+            "yfg", each(0, 1, True, [(0, 0), (1, 0)]), [(1, BF16, 0)] * 2, [m3or, m2or], after=(m1x, m2wr)
+        )
+        fo, fr = across(yf), lax.ppermute(yg, "comp", XCROSS)
+    split = [(1, F32, 0)] + [(1, F32, 128)] * 2
     with jax.named_scope("last"):
         yo, *ys = mmy(
-            "yos", each(0, (1, 2, 3, 4), False, [(0, 0), (1, 0)]), split, [m3wr, m2wr], after=(m3x,)
+            "yos", each(0, (1, 2), False, [(0, 0), (1, 0)]), split, [m3wr, m2wr], after=(yf,)
         )
         yr = [swap(a) for a in ys]
+        m3x, = mmx(
+            "m3x", both(0, 0, False, 1, [((0, 1), (4, 0)), (2, 0)]), [(2, BF16, 0)], [xer, x3r, m1xr], after=(yo, *yr)
+        )
+        m3xr = ahead(m3x)
+        window = 8 * N_COMP * N_PAIR
         xo, *xs = mmx(
-            "xos", each(0, (1, 2, 3, 4), False, [(0, 2), (1, 0), (2, 0)]), split, [x2r, m3xr, m2xr],
-            after=(yo,),
+            "xos", each(0, (1, 2), False, [((0, 0), (2, 4)), (1, 0), (2, 0)]), split, [x3r, m3xr, m2xr],
+            after=(yo, m3x),
         )
         xr = [swap(a) for a in xs]
+        y_rows = assemble(
+            "gather_y", gather_y_kernel, tile_mask, (yo, *yr, fo, fr), (window, QB), (), 1, (xo,)
+        )
         diag = energy_tile(pair_list, valence_energy, conduction_energy)
-        return final(tile_mask, (xo, *xr, yo, *yr, fo, fr), diag)
+        return assemble(
+            "final", final_kernel, tile_mask, (y_rows, xo, *xr, diag), (QB, window), [(window, QB)]
+        )
 
 
 def solution(mesh):

time: 102 us -> 100 us (0.980)
  Pallas kernels: 29.1 us -> 35.2 us
  local copies, waits for them, and re-layouts: 4.31 us -> 0.78 us
  waiting for transfers between devices: 31.2 us -> 28 us
  starting transfers between devices: 36.8 us -> 35 us
    pallas_call x12, Pallas kernels: 22 us -> 28.8 us  [mm(): pl.pallas_call(body, in_specs=[VMEM] * len(panels) + [HBM] * 2 + [VMEM] *...]
    ppermute x6, waiting for transfers between devices: 11.3 us -> 6.61 us  [per_device(): ahead = lambda a: lax.ppermute(a, 'comp', AHEAD)]
    unnamed x12 -> x10, local copies, waits for them, and re-layouts: 4.3 us -> 0.77 us
    ppermute x4, waiting for transfers between devices: 14.1 us -> 11 us  [per_device(): across = lambda a: lax.ppermute(a, 'comp', XSWAP)]
    ppermute x10 -> x6, starting transfers between devices: 7.37 us -> 4.62 us  [per_device(): swap = lambda a: lax.ppermute(a, 'comp', CORE)]
    ppermute x3, waiting for transfers between devices: 0.71 us -> 3.43 us  [per_device(): behind = lambda a: lax.ppermute(a, 'comp', BEHIND)]
    ppermute x1, waiting for transfers between devices: 0.01 us -> 1.93 us  [per_device(): fo, fr = (across(yf), lax.ppermute(yg, 'comp', XCROSS))]
    ppermute x6, starting transfers between devices: 11.4 us -> 12.9 us  [per_device(): ahead = lambda a: lax.ppermute(a, 'comp', AHEAD)]
  transfers between devices with their start and end apart: 28 -> 24, of which waited for: 14 -> 10; matrix products, arithmetic and copies ran while one was open for 0% -> 0% of each run, Pallas kernels for 20% -> 30%
where the time goes in v3:
time: 100 us; the launch traced here: 99.5 us
  Pallas kernels  35.2 us (35%)
  starting transfers between devices  35 us (35%)
  waiting for transfers between devices  28 us (28%)
    pallas_call x12, Pallas kernels, mm(): pl.pallas_call(body, in_specs=[VMEM] * len(panels) + [HBM] * 2 + [VMEM] *...  28.8 us
    ppermute x6, starting transfers between devices, per_device(): ahead = lambda a: lax.ppermute(a, 'comp', AHEAD)  12.9 us
    ppermute x3, starting transfers between devices, per_device(): zmove = lambda a: lax.ppermute(a, ('comp', 'pair'), ZSPLIT)  11.3 us
    ppermute x4, waiting for transfers between devices, per_device(): across = lambda a: lax.ppermute(a, 'comp', XSWAP)  11 us
    ppermute x6, waiting for transfers between devices, per_device(): ahead = lambda a: lax.ppermute(a, 'comp', AHEAD)  6.61 us
    ppermute x6, starting transfers between devices, per_device(): swap = lambda a: lax.ppermute(a, 'comp', CORE)  4.62 us
    pallas_call x2, Pallas kernels, assemble(): pl.pallas_call(body, in_specs=[pl.BlockSpec(memory_space=pltpu.SMEM)] + [...  3.77 us
    ppermute x3, waiting for transfers between devices, per_device(): behind = lambda a: lax.ppermute(a, 'comp', BEHIND)  3.43 us
  transfers between devices with their start and end apart: 24, of which 10 were waited for; matrix products, arithmetic and copies ran while one was open for 0% of the time, Pallas kernels for 30%

profile of v3, /device:TPU:1, one launch (start us, length us, event | category | flops | bytes accessed | tf_op | source)
XLA Modules:
  0.0 99.5 jit_solution(13179280888872931701)
XLA Ops:
  0.8 2.6 %pick.1.a_ref = bf16[1,128,512]{2,1,0:T(8,128)(2,1)S(1)} custom-call(bf16[512,8192]{1,0:T(8,128)(2,1)} %refs_2_.7, f32[64,128]{1,0:T(8,128)S(1)} %bitcast.5), custom_call_target="tpu_custom_call" | custom-call | tf_op jit(solution)/shard_map/panel/pick/pallas_call | solution.py:87
  3.3 1.5 %collective-permute-start = (bf16[1,128,512]{2,1,0:T(8,128)(2,1)S(1)}, bf16[1,128,512]{2,1,0:T(8,128)(2,1)S(1)}, u32[]{:S(2)}, u32[]{:S(2)}) collective-permute-start(bf16[1,128,512]{2,1,0:T(8,128)(2,1)S(1)} %pick.1.a_ref), channel_id=1, source_target_pairs={{0,8},{8,0},{16,24},{24,16},{32,40},{40,32},{48,56},{56,48},{64,72... | collective-permute-start | bytes 393224 | tf_op jit(solution)/shard_map/panel/ppermute | solution.py:288
  6.2 2.9 %collective-permute-start.1 = (bf16[2,128,512]{2,1,0:T(8,128)(2,1)S(1)}, bf16[2,128,512]{2,1,0:T(8,128)(2,1)S(1)}, u32[]{:S(2)}, u32[]{:S(2)}) collective-permute-start(bf16[2,128,512]{2,1,0:T(8,128)(2,1)S(1)} %get-tuple-element.25), channel_id=1, source_target_pairs={{0,1},{1,0},{2,3},{3,2},{4,5},{5,4},{6,7},{7,6},{8,9},{9,8},{10,11... | collective-permute-start | bytes 786440 | tf_op jit(solution)/shard_map/panel/ppermute | solution.py:296
  9.1 3.8 %collective-permute-start.2 = (bf16[2,128,512]{2,1,0:T(8,128)(2,1)S(1)}, bf16[2,128,512]{2,1,0:T(8,128)(2,1)S(1)}, u32[]{:S(2)}, u32[]{:S(2)}) collective-permute-start(bf16[2,128,512]{2,1,0:T(8,128)(2,1)S(1)} %get-tuple-element.24.refs_0_), channel_id=1, source_target_pairs={{0,2},{1,3},{2,4},{3,5},{4,6},{5,7},{6,0},{7,1},{8,14},{9,15},{10,... | collective-permute-start | bytes 786440 | tf_op jit(solution)/shard_map/panel/ppermute | solution.py:289
  12.9 2.7 %collective-permute-done.1.refs_1_ = bf16[2,128,512]{2,1,0:T(8,128)(2,1)S(1)} collective-permute-done((bf16[2,128,512]{2,1,0:T(8,128)(2,1)S(1)}, bf16[2,128,512]{2,1,0:T(8,128)(2,1)S(1)}, u32[]{:S(2)}, u32[]{:S(2)}) %collective-permute-start.1) | collective-permute-done | bytes 262176 | tf_op jit(solution)/shard_map/panel/ppermute | solution.py:296
  15.6 3.8 %collective-permute-start.4 = (bf16[2,128,512]{2,1,0:T(8,128)(2,1)S(1)}, bf16[2,128,512]{2,1,0:T(8,128)(2,1)S(1)}, u32[]{:S(2)}, u32[]{:S(2)}) collective-permute-start(bf16[2,128,512]{2,1,0:T(8,128)(2,1)S(1)} %collective-permute-done.1.refs_1_), channel_id=1, source_target_pairs={{0,2},{1,3},{2,4},{3,5},{4,6},{5,7},{6,0},{7,1},{8,14},{9,15},{10,... | collective-permute-start | bytes 786440 | tf_op jit(solution)/shard_map/panel/ppermute | solution.py:289
  19.4 2.9 %m12y.2 = (bf16[2,256,512]{2,1,0:T(8,128)(2,1)S(1)}, bf16[2,256,512]{2,1,0:T(8,128)(2,1)S(1)}) custom-call(bf16[2,128,512]{2,1,0:T(8,128)(2,1)S(1)} %get-tuple-element.24.refs_0_, bf16[2,128,512]{2,1,0:T(8,128)(2,1)S(1)} %collective-permute-done.1.refs_1_, bf16[2,128,512]{2,1,0:T(8,128)(2,1)S(1)} %collective-permute-done.2.refs_2_.zero, ...), custom_call_target="tpu_custom_call" | custom-call | flops 1073741824 | bytes 4194304 | tf_op jit(solution)/shard_map/y_then_x/m12y/pallas_call | solution.py:196
  22.3 2.8 %collective-permute-start.7 = (bf16[2,256,512]{2,1,0:T(8,128)(2,1)S(1)}, bf16[2,256,512]{2,1,0:T(8,128)(2,1)S(1)}, u32[]{:S(2)}, u32[]{:S(2)}) collective-permute-start(bf16[2,256,512]{2,1,0:T(8,128)(2,1)S(1)} %get-tuple-element.27.after), channel_id=1, source_target_pairs={{0,16},{8,56},{16,32},{24,8},{32,48},{40,24},{48,0},{56,40},{64,80... | collective-permute-start | bytes 1572872 | tf_op jit(solution)/shard_map/y_then_x/ppermute | solution.py:301
  25.1 3.7 %collective-permute-start.6 = (bf16[2,128,512]{2,1,0:T(8,128)(2,1)S(1)}, bf16[2,128,512]{2,1,0:T(8,128)(2,1)S(1)}, u32[]{:S(2)}, u32[]{:S(2)}) collective-permute-start(bf16[2,128,512]{2,1,0:T(8,128)(2,1)S(1)} %choose.1.refs_3_), channel_id=1, source_target_pairs={{0,2},{1,3},{2,4},{3,5},{4,6},{5,7},{6,0},{7,1},{8,14},{9,15},{10,... | collective-permute-start | bytes 786440 | tf_op jit(solution)/shard_map/x_then_y_send/ppermute | solution.py:289
  28.8 3.0 %xe.1.refs_5_ = bf16[6,128,512]{2,1,0:T(8,128)(2,1)S(1)} custom-call(bf16[2,128,512]{2,1,0:T(8,128)(2,1)S(1)} %collective-permute-done.4.one.refs_0_, bf16[512,8192]{1,0:T(8,128)(2,1)} %refs_2_.7, bf16[512,8192]{1,0:T(8,128)(2,1)S(1)} %collective-permute-done.3.refs_4_.refs_2_.refs_3_, bf16[2,128,512]{2,1,0:T(8,128)(2,1)S(1)} %choose.1.refs_3_), custom_call_target="tpu_custom_call" | custom-call | flops 805306368 | bytes 6291456 | tf_op jit(solution)/shard_map/x_then_y_send/xe/pallas_call | solution.py:196
  33.1 2.9 %m12y.3 = (bf16[2,256,512]{2,1,0:T(8,128)(2,1)S(1)}, bf16[2,256,512]{2,1,0:T(8,128)(2,1)S(1)}) custom-call(bf16[2,128,512]{2,1,0:T(8,128)(2,1)S(1)} %get-tuple-element.24.refs_0_, bf16[2,128,512]{2,1,0:T(8,128)(2,1)S(1)} %collective-permute-done.1.refs_1_, bf16[2,128,512]{2,1,0:T(8,128)(2,1)S(1)} %collective-permute-done.2.refs_2_.zero, ...), custom_call_target="tpu_custom_call" | custom-call | flops 1073741824 | bytes 4194304 | tf_op jit(solution)/shard_map/y_then_x/m12y/pallas_call | solution.py:196
  36.0 2.7 %collective-permute-start.5 = (bf16[2,256,512]{2,1,0:T(8,128)(2,1)S(1)}, bf16[2,256,512]{2,1,0:T(8,128)(2,1)S(1)}, u32[]{:S(2)}, u32[]{:S(2)}) collective-permute-start(bf16[2,256,512]{2,1,0:T(8,128)(2,1)S(1)} %get-tuple-element.28.refs_3_), channel_id=1, source_target_pairs={{0,16},{8,56},{16,32},{24,8},{32,48},{40,24},{48,0},{56,40},{64,80... | collective-permute-start | bytes 1572872 | tf_op jit(solution)/shard_map/y_then_x/ppermute | solution.py:301
  38.8 2.4 %xl.1.refs_6_ = bf16[4,128,512]{2,1,0:T(8,128)(2,1)S(1)} custom-call(bf16[2,128,512]{2,1,0:T(8,128)(2,1)S(1)} %collective-permute-done.6.refs_0_.refs_1_, bf16[512,8192]{1,0:T(8,128)(2,1)} %refs_2_.7, bf16[512,8192]{1,0:T(8,128)(2,1)S(1)} %collective-permute-done.3.refs_4_.refs_2_.refs_3_, bf16[2,256,512]{2,1,0:T(8,128)(2,1)S(1)} %get-tuple-element.28.refs_3_, ...), custom_call_target="tpu_custom_call" | custom-call | flops 53687091200 | bytes 4194304 | tf_op jit(solution)/shard_map/x_then_y_send/xl/pallas_call | solution.py:196
  41.6 2.0 %m3y.2.refs_4_ = bf16[2,256,512]{2,1,0:T(8,128)(2,1)S(1)} custom-call(bf16[2,128,512]{2,1,0:T(8,128)(2,1)S(1)} %get-tuple-element.24.refs_0_, bf16[2,128,512]{2,1,0:T(8,128)(2,1)S(1)} %collective-permute-done.1.refs_1_, bf16[2,128,512]{2,1,0:T(8,128)(2,1)S(1)} %collective-permute-done.2.refs_2_.zero, bf16[512,8192]{1,0:T(8,128)(2,1)} %refs_2_.7, ...), custom_call_target="tpu_custom_call" | custom-call | flops 536870912 | bytes 2097152 | tf_op jit(solution)/shard_map/y_then_x/m3y/pallas_call | solution.py:196
  43.5 2.7 %collective-permute-start.11 = (bf16[2,256,512]{2,1,0:T(8,128)(2,1)S(1)}, bf16[2,256,512]{2,1,0:T(8,128)(2,1)S(1)}, u32[]{:S(2)}, u32[]{:S(2)}) collective-permute-start(bf16[2,256,512]{2,1,0:T(8,128)(2,1)S(1)} %m3y.2.refs_4_), channel_id=1, source_target_pairs={{0,16},{8,56},{16,32},{24,8},{32,48},{40,24},{48,0},{56,40},{64,80... | collective-permute-start | bytes 1572872 | tf_op jit(solution)/shard_map/y_then_x/ppermute | solution.py:301
  46.2 2.9 %x3.1.refs_6_ = bf16[6,128,512]{2,1,0:T(8,128)(2,1)S(1)} custom-call(bf16[2,128,512]{2,1,0:T(8,128)(2,1)S(1)} %collective-permute-done.4.one.refs_0_, bf16[2,128,512]{2,1,0:T(8,128)(2,1)S(1)} %collective-permute-done.6.refs_0_.refs_1_, bf16[512,8192]{1,0:T(8,128)(2,1)} %refs_2_.7, bf16[512,8192]{1,0:T(8,128)(2,1)S(1)} %collective-permute-done.3.refs_4_.refs_2_.refs_3_, ...), custom_call_target="tpu_custom_call" | custom-call | flops 1073741824 | bytes 4194304 | tf_op jit(solution)/shard_map/y_then_x/x3/pallas_call | solution.py:196
  49.1 1.4 %collective-permute-done.5.refs_5_ = bf16[2,256,512]{2,1,0:T(8,128)(2,1)S(1)} collective-permute-done((bf16[2,256,512]{2,1,0:T(8,128)(2,1)S(1)}, bf16[2,256,512]{2,1,0:T(8,128)(2,1)S(1)}, u32[]{:S(2)}, u32[]{:S(2)}) %collective-permute-start.5) | collective-permute-done | bytes 524320 | tf_op jit(solution)/shard_map/y_then_x/ppermute | solution.py:301
  50.5 3.4 %collective-permute-done.9.refs_7_.refs_8_.refs_6_ = bf16[2,256,512]{2,1,0:T(8,128)(2,1)S(1)} collective-permute-done((bf16[2,256,512]{2,1,0:T(8,128)(2,1)S(1)}, bf16[2,256,512]{2,1,0:T(8,128)(2,1)S(1)}, u32[]{:S(2)}, u32[]{:S(2)}) %collective-permute-start.9) | collective-permute-done | bytes 524320 | tf_op jit(solution)/shard_map/y_then_x/ppermute | solution.py:302
  53.9 2.0 %m3y.3.refs_6_ = bf16[2,256,512]{2,1,0:T(8,128)(2,1)S(1)} custom-call(bf16[2,128,512]{2,1,0:T(8,128)(2,1)S(1)} %get-tuple-element.24.refs_0_, bf16[2,128,512]{2,1,0:T(8,128)(2,1)S(1)} %collective-permute-done.1.refs_1_, bf16[2,128,512]{2,1,0:T(8,128)(2,1)S(1)} %collective-permute-done.2.refs_2_.zero, bf16[512,8192]{1,0:T(8,128)(2,1)} %refs_2_.7, ...), custom_call_target="tpu_custom_call" | custom-call | flops 536870912 | bytes 2097152 | tf_op jit(solution)/shard_map/y_then_x/m3y/pallas_call | solution.py:196
  56.3 6.3 %collective-permute-done.13.refs_5_ = bf16[4,128,512]{2,1,0:T(8,128)(2,1)S(1)} collective-permute-done((bf16[4,128,512]{2,1,0:T(8,128)(2,1)S(1)}, bf16[4,128,512]{2,1,0:T(8,128)(2,1)S(1)}, u32[]{:S(2)}, u32[]{:S(2)}) %collective-permute-start.13) | collective-permute-done | bytes 524320 | tf_op jit(solution)/shard_map/x_then_y_send/ppermute | solution.py:303
  62.7 2.9 %m12x.1 = (bf16[2,256,512]{2,1,0:T(8,128)(2,1)S(1)}, bf16[2,256,512]{2,1,0:T(8,128)(2,1)S(1)}) custom-call(bf16[2,128,512]{2,1,0:T(8,128)(2,1)S(1)} %collective-permute-done.4.one.refs_0_, bf16[2,128,512]{2,1,0:T(8,128)(2,1)S(1)} %collective-permute-done.6.refs_0_.refs_1_, bf16[512,8192]{1,0:T(8,128)(2,1)} %refs_2_.7, ...), custom_call_target="tpu_custom_call" | custom-call | flops 1073741824 | bytes 4194304 | tf_op jit(solution)/shard_map/x_then_y/m12x/pallas_call | solution.py:196
  65.5 2.9 %collective-permute-start.19 = (bf16[2,256,512]{2,1,0:T(8,128)(2,1)S(1)}, bf16[2,256,512]{2,1,0:T(8,128)(2,1)S(1)}, u32[]{:S(2)}, u32[]{:S(2)}) collective-permute-start(bf16[2,256,512]{2,1,0:T(8,128)(2,1)S(1)} %get-tuple-element.31.refs_7_), channel_id=1, source_target_pairs={{0,16},{8,56},{16,32},{24,8},{32,48},{40,24},{48,0},{56,40},{64,80... | collective-permute-start | bytes 1572872 | tf_op jit(solution)/shard_map/x_then_y/ppermute | solution.py:301
  68.4 2.0 %yfg.1 = (bf16[1,256,512]{2,1,0:T(8,128)(2,1)S(1)}, bf16[1,256,512]{2,1,0:T(8,128)(2,1)S(1)}) custom-call(bf16[2,128,512]{2,1,0:T(8,128)(2,1)S(1)} %get-tuple-element.24.refs_0_, bf16[2,128,512]{2,1,0:T(8,128)(2,1)S(1)} %collective-permute-done.1.refs_1_, bf16[2,128,512]{2,1,0:T(8,128)(2,1)S(1)} %collective-permute-done.2.refs_2_.zero, ...), custom_call_target="tpu_custom_call" | custom-call | flops 536870912 | bytes 2097152 | tf_op jit(solution)/shard_map/x_then_y/yfg/pallas_call | solution.py:196
  70.4 2.0 %yos.1 = (f32[1,256,512]{2,1,0:T(8,128)S(1)}, f32[1,128,512]{2,1,0:T(8,128)S(1)}, f32[1,128,512]{2,1,0:T(8,128)S(1)}) custom-call(bf16[2,128,512]{2,1,0:T(8,128)(2,1)S(1)} %get-tuple-element.24.refs_0_, bf16[2,128,512]{2,1,0:T(8,128)(2,1)S(1)} %collective-permute-done.1.refs_1_, bf16[2,128,512]{2,1,0:T(8,128)(2,1)S(1)} %collective-permute-done.2.refs_2_.zero, ...), custom_call_target="tpu_custom_call" | custom-call | flops 536870912 | bytes 2097152 | tf_op jit(solution)/shard_map/last/yos/pallas_call | solution.py:196
  74.4 4.7 %collective-permute-done.18.refs_5_.refs_4_ = bf16[6,128,512]{2,1,0:T(8,128)(2,1)S(1)} collective-permute-done((bf16[6,128,512]{2,1,0:T(8,128)(2,1)S(1)}, bf16[6,128,512]{2,1,0:T(8,128)(2,1)S(1)}, u32[]{:S(2)}, u32[]{:S(2)}) %collective-permute-start.18) | collective-permute-done | bytes 786464 | tf_op jit(solution)/shard_map/y_then_x/ppermute | solution.py:303
  79.1 2.0 %m3x.1.refs_8_ = bf16[2,256,512]{2,1,0:T(8,128)(2,1)S(1)} custom-call(bf16[2,128,512]{2,1,0:T(8,128)(2,1)S(1)} %collective-permute-done.4.one.refs_0_, bf16[2,128,512]{2,1,0:T(8,128)(2,1)S(1)} %collective-permute-done.6.refs_0_.refs_1_, bf16[512,8192]{1,0:T(8,128)(2,1)} %refs_2_.7, bf16[512,8192]{1,0:T(8,128)(2,1)S(1)} %collective-permute-done.3.refs_4_.refs_2_.refs_3_, ...), custom_call_target="tpu_custom_call" | custom-call | flops 536870912 | bytes 2097152 | tf_op jit(solution)/shard_map/last/m3x/pallas_call | solution.py:196
  81.1 1.6 %collective-permute-start.20 = (bf16[2,256,512]{2,1,0:T(8,128)(2,1)S(1)}, bf16[2,256,512]{2,1,0:T(8,128)(2,1)S(1)}, u32[]{:S(2)}, u32[]{:S(2)}) collective-permute-start(bf16[2,256,512]{2,1,0:T(8,128)(2,1)S(1)} %m3x.1.refs_8_), channel_id=1, source_target_pairs={{0,16},{8,56},{16,32},{24,8},{32,48},{40,24},{48,0},{56,40},{64,80... | collective-permute-start | bytes 1572872 | tf_op jit(solution)/shard_map/last/ppermute | solution.py:301
  84.3 5.2 %collective-permute-done.20.refs_5_ = bf16[2,256,512]{2,1,0:T(8,128)(2,1)S(1)} collective-permute-done((bf16[2,256,512]{2,1,0:T(8,128)(2,1)S(1)}, bf16[2,256,512]{2,1,0:T(8,128)(2,1)S(1)}, u32[]{:S(2)}, u32[]{:S(2)}) %collective-permute-start.20) | collective-permute-done | bytes 524320 | tf_op jit(solution)/shard_map/last/ppermute | solution.py:301
  89.5 2.0 %xos.1 = (f32[1,256,512]{2,1,0:T(8,128)S(1)}, f32[1,128,512]{2,1,0:T(8,128)S(1)}, f32[1,128,512]{2,1,0:T(8,128)S(1)}) custom-call(bf16[2,128,512]{2,1,0:T(8,128)(2,1)S(1)} %collective-permute-done.4.one.refs_0_, bf16[2,128,512]{2,1,0:T(8,128)(2,1)S(1)} %collective-permute-done.6.refs_0_.refs_1_, bf16[512,8192]{1,0:T(8,128)(2,1)} %refs_2_.7, ...), custom_call_target="tpu_custom_call" | custom-call | flops 536870912 | bytes 2097152 | tf_op jit(solution)/shard_map/last/xos/pallas_call | solution.py:196
  91.5 2.1 %collective-permute-start.22 = (f32[1,128,512]{2,1,0:T(8,128)S(1)}, f32[1,128,512]{2,1,0:T(8,128)S(1)}, u32[]{:S(2)}, u32[]{:S(2)}) collective-permute-start(f32[1,128,512]{2,1,0:T(8,128)S(1)} %get-tuple-element.39), channel_id=1, source_target_pairs={{0,8},{8,0},{16,24},{24,16},{32,40},{40,32},{48,56},{56,48},{64,72... | collective-permute-start | bytes 786440 | tf_op jit(solution)/shard_map/last/ppermute | solution.py:288
  93.8 1.9 %collective-permute-done.17.refs_5_ = bf16[1,256,512]{2,1,0:T(8,128)(2,1)S(1)} collective-permute-done((bf16[1,256,512]{2,1,0:T(8,128)(2,1)S(1)}, bf16[1,256,512]{2,1,0:T(8,128)(2,1)S(1)}, u32[]{:S(2)}, u32[]{:S(2)}) %collective-permute-start.17) | collective-permute-done | bytes 262176 | tf_op jit(solution)/shard_map/x_then_y/ppermute | solution.py:375
  96.7 2.9 %final.1 = f32[512,1024]{1,0:T(8,128)} custom-call(s32[4,16]{1,0:T(4,128)S(1)} %copy-done.1, f32[1024,512]{1,0:T(8,128)S(1)} %gather_y.1.refs_1_, f32[1,256,512]{2,1,0:T(8,128)S(1)} %get-tuple-element.38.refs_6_.refs_2_, f32[1,128,512]{2,1,0:T(8,128)S(1)} %collective-permute-done.22.refs_3_, f32[1,128,512]{2,1,0:T(8,128)S(1)} %collective-permute-done.23.refs_4_, ...), custom_call_target="tpu_custom_call" | custom-call | flops 1000000000 | bytes 2097152 | tf_op jit(solution)/shard_map/last/final/pallas_call | solution.py:263
  (47 shorter events, 9.0 us)
Async XLA Ops:
  0.0 0.8 copy-start
  3.3 2.5 %collective-permute-start = (bf16[1,128,512]{2,1,0:T(8,128)(2,1)S(1)}, bf16[1,128,512]{2,1,0:T(8,128)(2,1)S(1)}, u32[]{:S(2)}, u32[]{:S(2)}) collective-permute-start(bf16[1,128,512]{2,1,0:T(8,128)(2,1)S(1)} %pick.1.a_ref), channel_id=1, source_target_pairs={{0,8},{8,0},{16,24},{24,16},{32,40},{40,32},{48,56},{56,48},{64,72... | collective-permute-start | bytes 393224 | tf_op jit(solution)/shard_map/panel/ppermute | solution.py:288
  5.8 13.6 %collective-permute-start.3 = (bf16[512,8192]{1,0:T(8,128)(2,1)}, bf16[512,8192]{1,0:T(8,128)(2,1)S(1)}, u32[]{:S(2)}, u32[]{:S(2)}) collective-permute-start(bf16[512,8192]{1,0:T(8,128)(2,1)} %refs_2_.7), channel_id=1, source_target_pairs={{0,8},{8,0},{16,24},{24,16},{32,40},{40,32},{48,56},{56,48},{64,72... | collective-permute-start | bytes 25165832 | tf_op jit(solution)/shard_map/panel/ppermute | solution.py:288
  6.2 9.3 %collective-permute-start.1 = (bf16[2,128,512]{2,1,0:T(8,128)(2,1)S(1)}, bf16[2,128,512]{2,1,0:T(8,128)(2,1)S(1)}, u32[]{:S(2)}, u32[]{:S(2)}) collective-permute-start(bf16[2,128,512]{2,1,0:T(8,128)(2,1)S(1)} %get-tuple-element.25), channel_id=1, source_target_pairs={{0,1},{1,0},{2,3},{3,2},{4,5},{5,4},{6,7},{7,6},{8,9},{9,8},{10,11... | collective-permute-start | bytes 786440 | tf_op jit(solution)/shard_map/panel/ppermute | solution.py:296
  9.1 10.3 %collective-permute-start.2 = (bf16[2,128,512]{2,1,0:T(8,128)(2,1)S(1)}, bf16[2,128,512]{2,1,0:T(8,128)(2,1)S(1)}, u32[]{:S(2)}, u32[]{:S(2)}) collective-permute-start(bf16[2,128,512]{2,1,0:T(8,128)(2,1)S(1)} %get-tuple-element.24.refs_0_), channel_id=1, source_target_pairs={{0,2},{1,3},{2,4},{3,5},{4,6},{5,7},{6,0},{7,1},{8,14},{9,15},{10,... | collective-permute-start | bytes 786440 | tf_op jit(solution)/shard_map/panel/ppermute | solution.py:289
  15.6 9.5 %collective-permute-start.4 = (bf16[2,128,512]{2,1,0:T(8,128)(2,1)S(1)}, bf16[2,128,512]{2,1,0:T(8,128)(2,1)S(1)}, u32[]{:S(2)}, u32[]{:S(2)}) collective-permute-start(bf16[2,128,512]{2,1,0:T(8,128)(2,1)S(1)} %collective-permute-done.1.refs_1_), channel_id=1, source_target_pairs={{0,2},{1,3},{2,4},{3,5},{4,6},{5,7},{6,0},{7,1},{8,14},{9,15},{10,... | collective-permute-start | bytes 786440 | tf_op jit(solution)/shard_map/panel/ppermute | solution.py:289
  22.3 16.5 %collective-permute-start.7 = (bf16[2,256,512]{2,1,0:T(8,128)(2,1)S(1)}, bf16[2,256,512]{2,1,0:T(8,128)(2,1)S(1)}, u32[]{:S(2)}, u32[]{:S(2)}) collective-permute-start(bf16[2,256,512]{2,1,0:T(8,128)(2,1)S(1)} %get-tuple-element.27.after), channel_id=1, source_target_pairs={{0,16},{8,56},{16,32},{24,8},{32,48},{40,24},{48,0},{56,40},{64,80... | collective-permute-start | bytes 1572872 | tf_op jit(solution)/shard_map/y_then_x/ppermute | solution.py:301
  25.1 13.7 %collective-permute-start.8 = (bf16[2,256,512]{2,1,0:T(8,128)(2,1)S(1)}, bf16[2,256,512]{2,1,0:T(8,128)(2,1)S(1)}, u32[]{:S(2)}, u32[]{:S(2)}) collective-permute-start(bf16[2,256,512]{2,1,0:T(8,128)(2,1)S(1)} %get-tuple-element.29), channel_id=1, source_target_pairs={{0,48},{8,24},{16,0},{24,40},{32,16},{40,56},{48,32},{56,8},{64,11... | collective-permute-start | bytes 1572872 | tf_op jit(solution)/shard_map/y_then_x/ppermute | solution.py:302
  25.1 13.6 %collective-permute-start.6 = (bf16[2,128,512]{2,1,0:T(8,128)(2,1)S(1)}, bf16[2,128,512]{2,1,0:T(8,128)(2,1)S(1)}, u32[]{:S(2)}, u32[]{:S(2)}) collective-permute-start(bf16[2,128,512]{2,1,0:T(8,128)(2,1)S(1)} %choose.1.refs_3_), channel_id=1, source_target_pairs={{0,2},{1,3},{2,4},{3,5},{4,6},{5,7},{6,0},{7,1},{8,14},{9,15},{10,... | collective-permute-start | bytes 786440 | tf_op jit(solution)/shard_map/x_then_y_send/ppermute | solution.py:289
  31.9 24.5 %collective-permute-start.12 = (bf16[6,128,512]{2,1,0:T(8,128)(2,1)S(1)}, bf16[6,128,512]{2,1,0:T(8,128)(2,1)S(1)}, u32[]{:S(2)}, u32[]{:S(2)}) collective-permute-start(bf16[6,128,512]{2,1,0:T(8,128)(2,1)S(1)} %xe.1.refs_5_), channel_id=1, source_target_pairs={{0,64},{8,72},{16,80},{24,88},{32,96},{40,104},{48,112},{56,120},{... | collective-permute-start | bytes 2359304 | tf_op jit(solution)/shard_map/x_then_y_send/ppermute | solution.py:303
  36.0 14.4 %collective-permute-start.5 = (bf16[2,256,512]{2,1,0:T(8,128)(2,1)S(1)}, bf16[2,256,512]{2,1,0:T(8,128)(2,1)S(1)}, u32[]{:S(2)}, u32[]{:S(2)}) collective-permute-start(bf16[2,256,512]{2,1,0:T(8,128)(2,1)S(1)} %get-tuple-element.28.refs_3_), channel_id=1, source_target_pairs={{0,16},{8,56},{16,32},{24,8},{32,48},{40,24},{48,0},{56,40},{64,80... | collective-permute-start | bytes 1572872 | tf_op jit(solution)/shard_map/y_then_x/ppermute | solution.py:301
  38.8 15.1 %collective-permute-start.9 = (bf16[2,256,512]{2,1,0:T(8,128)(2,1)S(1)}, bf16[2,256,512]{2,1,0:T(8,128)(2,1)S(1)}, u32[]{:S(2)}, u32[]{:S(2)}) collective-permute-start(bf16[2,256,512]{2,1,0:T(8,128)(2,1)S(1)} %get-tuple-element.30), channel_id=1, source_target_pairs={{0,48},{8,24},{16,0},{24,40},{32,16},{40,56},{48,32},{56,8},{64,11... | collective-permute-start | bytes 1572872 | tf_op jit(solution)/shard_map/y_then_x/ppermute | solution.py:302
  41.2 21.5 %collective-permute-start.13 = (bf16[4,128,512]{2,1,0:T(8,128)(2,1)S(1)}, bf16[4,128,512]{2,1,0:T(8,128)(2,1)S(1)}, u32[]{:S(2)}, u32[]{:S(2)}) collective-permute-start(bf16[4,128,512]{2,1,0:T(8,128)(2,1)S(1)} %xl.1.refs_6_), channel_id=1, source_target_pairs={{0,64},{8,72},{16,80},{24,88},{32,96},{40,104},{48,112},{56,120},{... | collective-permute-start | bytes 1572872 | tf_op jit(solution)/shard_map/x_then_y_send/ppermute | solution.py:303
  43.5 24.9 %collective-permute-start.11 = (bf16[2,256,512]{2,1,0:T(8,128)(2,1)S(1)}, bf16[2,256,512]{2,1,0:T(8,128)(2,1)S(1)}, u32[]{:S(2)}, u32[]{:S(2)}) collective-permute-start(bf16[2,256,512]{2,1,0:T(8,128)(2,1)S(1)} %m3y.2.refs_4_), channel_id=1, source_target_pairs={{0,16},{8,56},{16,32},{24,8},{32,48},{40,24},{48,0},{56,40},{64,80... | collective-permute-start | bytes 1572872 | tf_op jit(solution)/shard_map/y_then_x/ppermute | solution.py:301
  55.8 14.6 %collective-permute-start.10 = (bf16[2,256,512]{2,1,0:T(8,128)(2,1)S(1)}, bf16[2,256,512]{2,1,0:T(8,128)(2,1)S(1)}, u32[]{:S(2)}, u32[]{:S(2)}) collective-permute-start(bf16[2,256,512]{2,1,0:T(8,128)(2,1)S(1)} %m3y.3.refs_6_), channel_id=1, source_target_pairs={{0,16},{8,56},{16,32},{24,8},{32,48},{40,24},{48,0},{56,40},{64,80... | collective-permute-start | bytes 1572872 | tf_op jit(solution)/shard_map/y_then_x/ppermute | solution.py:301
  56.1 23.0 %collective-permute-start.18 = (bf16[6,128,512]{2,1,0:T(8,128)(2,1)S(1)}, bf16[6,128,512]{2,1,0:T(8,128)(2,1)S(1)}, u32[]{:S(2)}, u32[]{:S(2)}) collective-permute-start(bf16[6,128,512]{2,1,0:T(8,128)(2,1)S(1)} %x3.1.refs_6_), channel_id=1, source_target_pairs={{0,64},{8,72},{16,80},{24,88},{32,96},{40,104},{48,112},{56,120},{... | collective-permute-start | bytes 2359304 | tf_op jit(solution)/shard_map/y_then_x/ppermute | solution.py:303
  65.5 13.5 %collective-permute-start.19 = (bf16[2,256,512]{2,1,0:T(8,128)(2,1)S(1)}, bf16[2,256,512]{2,1,0:T(8,128)(2,1)S(1)}, u32[]{:S(2)}, u32[]{:S(2)}) collective-permute-start(bf16[2,256,512]{2,1,0:T(8,128)(2,1)S(1)} %get-tuple-element.31.refs_7_), channel_id=1, source_target_pairs={{0,16},{8,56},{16,32},{24,8},{32,48},{40,24},{48,0},{56,40},{64,80... | collective-permute-start | bytes 1572872 | tf_op jit(solution)/shard_map/x_then_y/ppermute | solution.py:301
  72.4 1.6 %collective-permute-start.14 = (f32[1,128,512]{2,1,0:T(8,128)S(1)}, f32[1,128,512]{2,1,0:T(8,128)S(1)}, u32[]{:S(2)}, u32[]{:S(2)}) collective-permute-start(f32[1,128,512]{2,1,0:T(8,128)S(1)} %get-tuple-element.34), channel_id=1, source_target_pairs={{0,8},{8,0},{16,24},{24,16},{32,40},{40,32},{48,56},{56,48},{64,72... | collective-permute-start | bytes 786440 | tf_op jit(solution)/shard_map/last/ppermute | solution.py:288
  72.5 1.9 %collective-permute-start.15 = (f32[1,128,512]{2,1,0:T(8,128)S(1)}, f32[1,128,512]{2,1,0:T(8,128)S(1)}, u32[]{:S(2)}, u32[]{:S(2)}) collective-permute-start(f32[1,128,512]{2,1,0:T(8,128)S(1)} %get-tuple-element.35), channel_id=1, source_target_pairs={{0,8},{8,0},{16,24},{24,16},{32,40},{40,32},{48,56},{56,48},{64,72... | collective-permute-start | bytes 786440 | tf_op jit(solution)/shard_map/last/ppermute | solution.py:288
  73.0 11.3 %collective-permute-start.21 = (bf16[2,256,512]{2,1,0:T(8,128)(2,1)S(1)}, bf16[2,256,512]{2,1,0:T(8,128)(2,1)S(1)}, u32[]{:S(2)}, u32[]{:S(2)}) collective-permute-start(bf16[2,256,512]{2,1,0:T(8,128)(2,1)S(1)} %get-tuple-element.37), channel_id=1, source_target_pairs={{0,48},{8,24},{16,0},{24,40},{32,16},{40,56},{48,32},{56,8},{64,11... | collective-permute-start | bytes 1572872 | tf_op jit(solution)/shard_map/x_then_y/ppermute | solution.py:302
  79.1 3.6 %copy-start.4 = (s32[8,2]{0,1:T(2,128)S(1)}, s32[8,2]{0,1:T(2,128)}, u32[]{:S(2)}) copy-start(s32[8,2]{0,1:T(2,128)} %param.8) | copy-start | bytes 196
  79.1 3.6 %copy-start.2 = (f32[4096]{0:T(1024)S(1)}, f32[4096]{0:T(1024)}, u32[]{:S(2)}) copy-start(f32[4096]{0:T(1024)} %param.9) | copy-start | bytes 49156
  79.1 3.6 %copy-start.3 = (f32[4096]{0:T(1024)S(1)}, f32[4096]{0:T(1024)}, u32[]{:S(2)}) copy-start(f32[4096]{0:T(1024)} %param.10) | copy-start | bytes 49156
  81.1 8.4 %collective-permute-start.20 = (bf16[2,256,512]{2,1,0:T(8,128)(2,1)S(1)}, bf16[2,256,512]{2,1,0:T(8,128)(2,1)S(1)}, u32[]{:S(2)}, u32[]{:S(2)}) collective-permute-start(bf16[2,256,512]{2,1,0:T(8,128)(2,1)S(1)} %m3x.1.refs_8_), channel_id=1, source_target_pairs={{0,16},{8,56},{16,32},{24,8},{32,48},{40,24},{48,0},{56,40},{64,80... | collective-permute-start | bytes 1572872 | tf_op jit(solution)/shard_map/last/ppermute | solution.py:301
  83.0 10.8 %collective-permute-start.16 = (bf16[1,256,512]{2,1,0:T(8,128)(2,1)S(1)}, bf16[1,256,512]{2,1,0:T(8,128)(2,1)S(1)}, u32[]{:S(2)}, u32[]{:S(2)}) collective-permute-start(bf16[1,256,512]{2,1,0:T(8,128)(2,1)S(1)} %get-tuple-element.32.refs_7_), channel_id=1, source_target_pairs={{0,64},{8,72},{16,80},{24,88},{32,96},{40,104},{48,112},{56,120},{... | collective-permute-start | bytes 786440 | tf_op jit(solution)/shard_map/x_then_y/ppermute | solution.py:303
  84.3 11.5 %copy-start.1 = (s32[4,16]{1,0:T(4,128)S(1)}, s32[4,16]{1,0:T(4,128)}, u32[]{:S(2)}) copy-start(s32[4,16]{1,0:T(4,128)} %refs_0_.3) | copy-start | bytes 772
  84.3 11.4 %collective-permute-start.17 = (bf16[1,256,512]{2,1,0:T(8,128)(2,1)S(1)}, bf16[1,256,512]{2,1,0:T(8,128)(2,1)S(1)}, u32[]{:S(2)}, u32[]{:S(2)}) collective-permute-start(bf16[1,256,512]{2,1,0:T(8,128)(2,1)S(1)} %get-tuple-element.36), channel_id=1, source_target_pairs={{0,72},{8,64},{16,88},{24,80},{32,104},{40,96},{48,120},{56,112},{... | collective-permute-start | bytes 786440 | tf_op jit(solution)/shard_map/x_then_y/ppermute | solution.py:375
  91.5 5.1 %collective-permute-start.22 = (f32[1,128,512]{2,1,0:T(8,128)S(1)}, f32[1,128,512]{2,1,0:T(8,128)S(1)}, u32[]{:S(2)}, u32[]{:S(2)}) collective-permute-start(f32[1,128,512]{2,1,0:T(8,128)S(1)} %get-tuple-element.39), channel_id=1, source_target_pairs={{0,8},{8,0},{16,24},{24,16},{32,40},{40,32},{48,56},{56,48},{64,72... | collective-permute-start | bytes 786440 | tf_op jit(solution)/shard_map/last/ppermute | solution.py:288
  93.6 3.0 %collective-permute-start.23 = (f32[1,128,512]{2,1,0:T(8,128)S(1)}, f32[1,128,512]{2,1,0:T(8,128)S(1)}, u32[]{:S(2)}, u32[]{:S(2)}) collective-permute-start(f32[1,128,512]{2,1,0:T(8,128)S(1)} %get-tuple-element.40), channel_id=1, source_target_pairs={{0,8},{8,0},{16,24},{24,16},{32,40},{40,32},{48,56},{56,48},{64,72... | collective-permute-start | bytes 786440 | tf_op jit(solution)/shard_map/last/ppermute | solution.py:288

commit v4 on v3

--- a/solution.py
+++ b/solution.py
@@ -380,7 +380,7 @@
         )
         yr = [swap(a) for a in ys]
         m3x, = mmx(
-            "m3x", both(0, 0, False, 1, [((0, 1), (4, 0)), (2, 0)]), [(2, BF16, 0)], [xer, x3r, m1xr], after=(yo, *yr)
+            "m3x", both(0, 0, False, 1, [((0, 1), (4, 0)), (2, 0)]), [(2, BF16, 0)], [xer, x3r, m1xr], after=(yo, *yr, m2xr), weight=100
         )
         m3xr = ahead(m3x)
         window = 8 * N_COMP * N_PAIR

time: 100 us -> 101 us (1.010)
  starting transfers between devices: 35 us -> 36.3 us
    ppermute x6, starting transfers between devices: 12.9 us -> 14.5 us  [per_device(): ahead = lambda a: lax.ppermute(a, 'comp', AHEAD)]
    ppermute x1, waiting for transfers between devices: 1.93 us -> 0.66 us  [per_device(): fo, fr = (across(yf), lax.ppermute(yg, 'comp', XCROSS))]
  transfers between devices with their start and end apart: 24 -> 24, of which waited for: 10 -> 12; matrix products, arithmetic and copies ran while one was open for 0% -> 0% of each run, Pallas kernels for 30% -> 28%
where the time goes in v4:
time: 101 us; the launch traced here: 100 us
  starting transfers between devices  36.3 us (36%)
  Pallas kernels  35.2 us (35%)
  waiting for transfers between devices  27.4 us (27%)
    pallas_call x12, Pallas kernels, mm(): pl.pallas_call(body, in_specs=[VMEM] * len(panels) + [HBM] * 2 + [VMEM] *...  28.8 us
    ppermute x6, starting transfers between devices, per_device(): ahead = lambda a: lax.ppermute(a, 'comp', AHEAD)  14.5 us
    ppermute x3, starting transfers between devices, per_device(): zmove = lambda a: lax.ppermute(a, ('comp', 'pair'), ZSPLIT)  11.3 us
    ppermute x4, waiting for transfers between devices, per_device(): across = lambda a: lax.ppermute(a, 'comp', XSWAP)  11 us
    ppermute x6, waiting for transfers between devices, per_device(): ahead = lambda a: lax.ppermute(a, 'comp', AHEAD)  6.94 us
    ppermute x6, starting transfers between devices, per_device(): swap = lambda a: lax.ppermute(a, 'comp', CORE)  4.43 us
    ppermute x3, waiting for transfers between devices, per_device(): behind = lambda a: lax.ppermute(a, 'comp', BEHIND)  3.79 us
    pallas_call x2, Pallas kernels, assemble(): pl.pallas_call(body, in_specs=[pl.BlockSpec(memory_space=pltpu.SMEM)] + [...  3.77 us
  transfers between devices with their start and end apart: 24, of which 12 were waited for; matrix products, arithmetic and copies ran while one was open for 0% of the time, Pallas kernels for 28%

profile of v4, /device:TPU:1, one launch (start us, length us, event | category | flops | bytes accessed | tf_op | source)
XLA Modules:
  0.0 100.3 jit_solution(5199147256142991978)
XLA Ops:
  0.8 2.6 %pick.1.a_ref = bf16[1,128,512]{2,1,0:T(8,128)(2,1)S(1)} custom-call(bf16[512,8192]{1,0:T(8,128)(2,1)} %refs_2_.7, f32[64,128]{1,0:T(8,128)S(1)} %bitcast.5), custom_call_target="tpu_custom_call" | custom-call | tf_op jit(solution)/shard_map/panel/pick/pallas_call | solution.py:87
  3.3 1.5 %collective-permute-start = (bf16[1,128,512]{2,1,0:T(8,128)(2,1)S(1)}, bf16[1,128,512]{2,1,0:T(8,128)(2,1)S(1)}, u32[]{:S(2)}, u32[]{:S(2)}) collective-permute-start(bf16[1,128,512]{2,1,0:T(8,128)(2,1)S(1)} %pick.1.a_ref), channel_id=1, source_target_pairs={{0,8},{8,0},{16,24},{24,16},{32,40},{40,32},{48,56},{56,48},{64,72... | collective-permute-start | bytes 393224 | tf_op jit(solution)/shard_map/panel/ppermute | solution.py:288
  6.2 2.9 %collective-permute-start.1 = (bf16[2,128,512]{2,1,0:T(8,128)(2,1)S(1)}, bf16[2,128,512]{2,1,0:T(8,128)(2,1)S(1)}, u32[]{:S(2)}, u32[]{:S(2)}) collective-permute-start(bf16[2,128,512]{2,1,0:T(8,128)(2,1)S(1)} %get-tuple-element.25), channel_id=1, source_target_pairs={{0,1},{1,0},{2,3},{3,2},{4,5},{5,4},{6,7},{7,6},{8,9},{9,8},{10,11... | collective-permute-start | bytes 786440 | tf_op jit(solution)/shard_map/panel/ppermute | solution.py:296
  9.1 3.8 %collective-permute-start.2 = (bf16[2,128,512]{2,1,0:T(8,128)(2,1)S(1)}, bf16[2,128,512]{2,1,0:T(8,128)(2,1)S(1)}, u32[]{:S(2)}, u32[]{:S(2)}) collective-permute-start(bf16[2,128,512]{2,1,0:T(8,128)(2,1)S(1)} %get-tuple-element.24.refs_0_), channel_id=1, source_target_pairs={{0,2},{1,3},{2,4},{3,5},{4,6},{5,7},{6,0},{7,1},{8,14},{9,15},{10,... | collective-permute-start | bytes 786440 | tf_op jit(solution)/shard_map/panel/ppermute | solution.py:289
  12.9 2.7 %collective-permute-done.1.refs_1_ = bf16[2,128,512]{2,1,0:T(8,128)(2,1)S(1)} collective-permute-done((bf16[2,128,512]{2,1,0:T(8,128)(2,1)S(1)}, bf16[2,128,512]{2,1,0:T(8,128)(2,1)S(1)}, u32[]{:S(2)}, u32[]{:S(2)}) %collective-permute-start.1) | collective-permute-done | bytes 262176 | tf_op jit(solution)/shard_map/panel/ppermute | solution.py:296
  15.6 3.8 %collective-permute-start.4 = (bf16[2,128,512]{2,1,0:T(8,128)(2,1)S(1)}, bf16[2,128,512]{2,1,0:T(8,128)(2,1)S(1)}, u32[]{:S(2)}, u32[]{:S(2)}) collective-permute-start(bf16[2,128,512]{2,1,0:T(8,128)(2,1)S(1)} %collective-permute-done.1.refs_1_), channel_id=1, source_target_pairs={{0,2},{1,3},{2,4},{3,5},{4,6},{5,7},{6,0},{7,1},{8,14},{9,15},{10,... | collective-permute-start | bytes 786440 | tf_op jit(solution)/shard_map/panel/ppermute | solution.py:289
  19.4 2.9 %m12y.2 = (bf16[2,256,512]{2,1,0:T(8,128)(2,1)S(1)}, bf16[2,256,512]{2,1,0:T(8,128)(2,1)S(1)}) custom-call(bf16[2,128,512]{2,1,0:T(8,128)(2,1)S(1)} %get-tuple-element.24.refs_0_, bf16[2,128,512]{2,1,0:T(8,128)(2,1)S(1)} %collective-permute-done.1.refs_1_, bf16[2,128,512]{2,1,0:T(8,128)(2,1)S(1)} %collective-permute-done.2.refs_2_.zero, ...), custom_call_target="tpu_custom_call" | custom-call | flops 1073741824 | bytes 4194304 | tf_op jit(solution)/shard_map/y_then_x/m12y/pallas_call | solution.py:196
  22.3 2.8 %collective-permute-start.7 = (bf16[2,256,512]{2,1,0:T(8,128)(2,1)S(1)}, bf16[2,256,512]{2,1,0:T(8,128)(2,1)S(1)}, u32[]{:S(2)}, u32[]{:S(2)}) collective-permute-start(bf16[2,256,512]{2,1,0:T(8,128)(2,1)S(1)} %get-tuple-element.27.after), channel_id=1, source_target_pairs={{0,16},{8,56},{16,32},{24,8},{32,48},{40,24},{48,0},{56,40},{64,80... | collective-permute-start | bytes 1572872 | tf_op jit(solution)/shard_map/y_then_x/ppermute | solution.py:301
  25.1 3.7 %collective-permute-start.6 = (bf16[2,128,512]{2,1,0:T(8,128)(2,1)S(1)}, bf16[2,128,512]{2,1,0:T(8,128)(2,1)S(1)}, u32[]{:S(2)}, u32[]{:S(2)}) collective-permute-start(bf16[2,128,512]{2,1,0:T(8,128)(2,1)S(1)} %choose.1.refs_3_), channel_id=1, source_target_pairs={{0,2},{1,3},{2,4},{3,5},{4,6},{5,7},{6,0},{7,1},{8,14},{9,15},{10,... | collective-permute-start | bytes 786440 | tf_op jit(solution)/shard_map/x_then_y_send/ppermute | solution.py:289
  28.8 3.0 %xe.1.refs_5_ = bf16[6,128,512]{2,1,0:T(8,128)(2,1)S(1)} custom-call(bf16[2,128,512]{2,1,0:T(8,128)(2,1)S(1)} %collective-permute-done.4.one.refs_0_, bf16[512,8192]{1,0:T(8,128)(2,1)} %refs_2_.7, bf16[512,8192]{1,0:T(8,128)(2,1)S(1)} %collective-permute-done.3.refs_4_.refs_2_.refs_3_, bf16[2,128,512]{2,1,0:T(8,128)(2,1)S(1)} %choose.1.refs_3_), custom_call_target="tpu_custom_call" | custom-call | flops 805306368 | bytes 6291456 | tf_op jit(solution)/shard_map/x_then_y_send/xe/pallas_call | solution.py:196
  31.9 1.3 %collective-permute-start.12 = (bf16[6,128,512]{2,1,0:T(8,128)(2,1)S(1)}, bf16[6,128,512]{2,1,0:T(8,128)(2,1)S(1)}, u32[]{:S(2)}, u32[]{:S(2)}) collective-permute-start(bf16[6,128,512]{2,1,0:T(8,128)(2,1)S(1)} %xe.1.refs_5_), channel_id=1, source_target_pairs={{0,64},{8,72},{16,80},{24,88},{32,96},{40,104},{48,112},{56,120},{... | collective-permute-start | bytes 2359304 | tf_op jit(solution)/shard_map/x_then_y_send/ppermute | solution.py:303
  33.1 2.9 %m12y.3 = (bf16[2,256,512]{2,1,0:T(8,128)(2,1)S(1)}, bf16[2,256,512]{2,1,0:T(8,128)(2,1)S(1)}) custom-call(bf16[2,128,512]{2,1,0:T(8,128)(2,1)S(1)} %get-tuple-element.24.refs_0_, bf16[2,128,512]{2,1,0:T(8,128)(2,1)S(1)} %collective-permute-done.1.refs_1_, bf16[2,128,512]{2,1,0:T(8,128)(2,1)S(1)} %collective-permute-done.2.refs_2_.zero, ...), custom_call_target="tpu_custom_call" | custom-call | flops 1073741824 | bytes 4194304 | tf_op jit(solution)/shard_map/y_then_x/m12y/pallas_call | solution.py:196
  36.0 2.7 %collective-permute-start.5 = (bf16[2,256,512]{2,1,0:T(8,128)(2,1)S(1)}, bf16[2,256,512]{2,1,0:T(8,128)(2,1)S(1)}, u32[]{:S(2)}, u32[]{:S(2)}) collective-permute-start(bf16[2,256,512]{2,1,0:T(8,128)(2,1)S(1)} %get-tuple-element.28.refs_3_), channel_id=1, source_target_pairs={{0,16},{8,56},{16,32},{24,8},{32,48},{40,24},{48,0},{56,40},{64,80... | collective-permute-start | bytes 1572872 | tf_op jit(solution)/shard_map/y_then_x/ppermute | solution.py:301
  38.8 2.4 %xl.1.refs_6_ = bf16[4,128,512]{2,1,0:T(8,128)(2,1)S(1)} custom-call(bf16[2,128,512]{2,1,0:T(8,128)(2,1)S(1)} %collective-permute-done.6.refs_0_.refs_1_, bf16[512,8192]{1,0:T(8,128)(2,1)} %refs_2_.7, bf16[512,8192]{1,0:T(8,128)(2,1)S(1)} %collective-permute-done.3.refs_4_.refs_2_.refs_3_, bf16[2,256,512]{2,1,0:T(8,128)(2,1)S(1)} %get-tuple-element.28.refs_3_, ...), custom_call_target="tpu_custom_call" | custom-call | flops 53687091200 | bytes 4194304 | tf_op jit(solution)/shard_map/x_then_y_send/xl/pallas_call | solution.py:196
  41.6 2.0 %m3y.2.refs_4_ = bf16[2,256,512]{2,1,0:T(8,128)(2,1)S(1)} custom-call(bf16[2,128,512]{2,1,0:T(8,128)(2,1)S(1)} %get-tuple-element.24.refs_0_, bf16[2,128,512]{2,1,0:T(8,128)(2,1)S(1)} %collective-permute-done.1.refs_1_, bf16[2,128,512]{2,1,0:T(8,128)(2,1)S(1)} %collective-permute-done.2.refs_2_.zero, bf16[512,8192]{1,0:T(8,128)(2,1)} %refs_2_.7, ...), custom_call_target="tpu_custom_call" | custom-call | flops 536870912 | bytes 2097152 | tf_op jit(solution)/shard_map/y_then_x/m3y/pallas_call | solution.py:196
  43.5 2.7 %collective-permute-start.11 = (bf16[2,256,512]{2,1,0:T(8,128)(2,1)S(1)}, bf16[2,256,512]{2,1,0:T(8,128)(2,1)S(1)}, u32[]{:S(2)}, u32[]{:S(2)}) collective-permute-start(bf16[2,256,512]{2,1,0:T(8,128)(2,1)S(1)} %m3y.2.refs_4_), channel_id=1, source_target_pairs={{0,16},{8,56},{16,32},{24,8},{32,48},{40,24},{48,0},{56,40},{64,80... | collective-permute-start | bytes 1572872 | tf_op jit(solution)/shard_map/y_then_x/ppermute | solution.py:301
  46.2 2.9 %x3.1.refs_6_ = bf16[6,128,512]{2,1,0:T(8,128)(2,1)S(1)} custom-call(bf16[2,128,512]{2,1,0:T(8,128)(2,1)S(1)} %collective-permute-done.4.one.refs_0_, bf16[2,128,512]{2,1,0:T(8,128)(2,1)S(1)} %collective-permute-done.6.refs_0_.refs_1_, bf16[512,8192]{1,0:T(8,128)(2,1)} %refs_2_.7, bf16[512,8192]{1,0:T(8,128)(2,1)S(1)} %collective-permute-done.3.refs_4_.refs_2_.refs_3_, ...), custom_call_target="tpu_custom_call" | custom-call | flops 1073741824 | bytes 4194304 | tf_op jit(solution)/shard_map/y_then_x/x3/pallas_call | solution.py:196
  49.1 1.4 %collective-permute-done.5.refs_5_ = bf16[2,256,512]{2,1,0:T(8,128)(2,1)S(1)} collective-permute-done((bf16[2,256,512]{2,1,0:T(8,128)(2,1)S(1)}, bf16[2,256,512]{2,1,0:T(8,128)(2,1)S(1)}, u32[]{:S(2)}, u32[]{:S(2)}) %collective-permute-start.5) | collective-permute-done | bytes 524320 | tf_op jit(solution)/shard_map/y_then_x/ppermute | solution.py:301
  50.5 3.4 %collective-permute-done.9.refs_7_.refs_8_.refs_6_ = bf16[2,256,512]{2,1,0:T(8,128)(2,1)S(1)} collective-permute-done((bf16[2,256,512]{2,1,0:T(8,128)(2,1)S(1)}, bf16[2,256,512]{2,1,0:T(8,128)(2,1)S(1)}, u32[]{:S(2)}, u32[]{:S(2)}) %collective-permute-start.9) | collective-permute-done | bytes 524320 | tf_op jit(solution)/shard_map/y_then_x/ppermute | solution.py:302
  53.9 2.0 %m3y.3.refs_6_ = bf16[2,256,512]{2,1,0:T(8,128)(2,1)S(1)} custom-call(bf16[2,128,512]{2,1,0:T(8,128)(2,1)S(1)} %get-tuple-element.24.refs_0_, bf16[2,128,512]{2,1,0:T(8,128)(2,1)S(1)} %collective-permute-done.1.refs_1_, bf16[2,128,512]{2,1,0:T(8,128)(2,1)S(1)} %collective-permute-done.2.refs_2_.zero, bf16[512,8192]{1,0:T(8,128)(2,1)} %refs_2_.7, ...), custom_call_target="tpu_custom_call" | custom-call | flops 536870912 | bytes 2097152 | tf_op jit(solution)/shard_map/y_then_x/m3y/pallas_call | solution.py:196
  56.3 6.3 %collective-permute-done.13.refs_5_ = bf16[4,128,512]{2,1,0:T(8,128)(2,1)S(1)} collective-permute-done((bf16[4,128,512]{2,1,0:T(8,128)(2,1)S(1)}, bf16[4,128,512]{2,1,0:T(8,128)(2,1)S(1)}, u32[]{:S(2)}, u32[]{:S(2)}) %collective-permute-start.13) | collective-permute-done | bytes 524320 | tf_op jit(solution)/shard_map/x_then_y_send/ppermute | solution.py:303
  62.7 2.9 %m12x.1 = (bf16[2,256,512]{2,1,0:T(8,128)(2,1)S(1)}, bf16[2,256,512]{2,1,0:T(8,128)(2,1)S(1)}) custom-call(bf16[2,128,512]{2,1,0:T(8,128)(2,1)S(1)} %collective-permute-done.4.one.refs_0_, bf16[2,128,512]{2,1,0:T(8,128)(2,1)S(1)} %collective-permute-done.6.refs_0_.refs_1_, bf16[512,8192]{1,0:T(8,128)(2,1)} %refs_2_.7, ...), custom_call_target="tpu_custom_call" | custom-call | flops 1073741824 | bytes 4194304 | tf_op jit(solution)/shard_map/x_then_y/m12x/pallas_call | solution.py:196
  65.5 2.9 %collective-permute-start.19 = (bf16[2,256,512]{2,1,0:T(8,128)(2,1)S(1)}, bf16[2,256,512]{2,1,0:T(8,128)(2,1)S(1)}, u32[]{:S(2)}, u32[]{:S(2)}) collective-permute-start(bf16[2,256,512]{2,1,0:T(8,128)(2,1)S(1)} %get-tuple-element.31.refs_7_), channel_id=1, source_target_pairs={{0,16},{8,56},{16,32},{24,8},{32,48},{40,24},{48,0},{56,40},{64,80... | collective-permute-start | bytes 1572872 | tf_op jit(solution)/shard_map/x_then_y/ppermute | solution.py:301
  68.4 2.0 %yfg.1 = (bf16[1,256,512]{2,1,0:T(8,128)(2,1)S(1)}, bf16[1,256,512]{2,1,0:T(8,128)(2,1)S(1)}) custom-call(bf16[2,128,512]{2,1,0:T(8,128)(2,1)S(1)} %get-tuple-element.24.refs_0_, bf16[2,128,512]{2,1,0:T(8,128)(2,1)S(1)} %collective-permute-done.1.refs_1_, bf16[2,128,512]{2,1,0:T(8,128)(2,1)S(1)} %collective-permute-done.2.refs_2_.zero, ...), custom_call_target="tpu_custom_call" | custom-call | flops 536870912 | bytes 2097152 | tf_op jit(solution)/shard_map/x_then_y/yfg/pallas_call | solution.py:196
  70.4 2.0 %yos.1 = (f32[1,256,512]{2,1,0:T(8,128)S(1)}, f32[1,128,512]{2,1,0:T(8,128)S(1)}, f32[1,128,512]{2,1,0:T(8,128)S(1)}) custom-call(bf16[2,128,512]{2,1,0:T(8,128)(2,1)S(1)} %get-tuple-element.24.refs_0_, bf16[2,128,512]{2,1,0:T(8,128)(2,1)S(1)} %collective-permute-done.1.refs_1_, bf16[2,128,512]{2,1,0:T(8,128)(2,1)S(1)} %collective-permute-done.2.refs_2_.zero, ...), custom_call_target="tpu_custom_call" | custom-call | flops 536870912 | bytes 2097152 | tf_op jit(solution)/shard_map/last/yos/pallas_call | solution.py:196
  74.4 4.6 %collective-permute-done.18.refs_5_.refs_4_ = bf16[6,128,512]{2,1,0:T(8,128)(2,1)S(1)} collective-permute-done((bf16[6,128,512]{2,1,0:T(8,128)(2,1)S(1)}, bf16[6,128,512]{2,1,0:T(8,128)(2,1)S(1)}, u32[]{:S(2)}, u32[]{:S(2)}) %collective-permute-start.18) | collective-permute-done | bytes 786464 | tf_op jit(solution)/shard_map/y_then_x/ppermute | solution.py:303
  80.4 2.0 %m3x.1.refs_8_ = bf16[2,256,512]{2,1,0:T(8,128)(2,1)S(1)} custom-call(bf16[2,128,512]{2,1,0:T(8,128)(2,1)S(1)} %collective-permute-done.4.one.refs_0_, bf16[2,128,512]{2,1,0:T(8,128)(2,1)S(1)} %collective-permute-done.6.refs_0_.refs_1_, bf16[512,8192]{1,0:T(8,128)(2,1)} %refs_2_.7, bf16[512,8192]{1,0:T(8,128)(2,1)S(1)} %collective-permute-done.3.refs_4_.refs_2_.refs_3_, ...), custom_call_target="tpu_custom_call" | custom-call | flops 53687091200 | bytes 2097152 | tf_op jit(solution)/shard_map/last/m3x/pallas_call | solution.py:196
  82.5 3.1 %collective-permute-start.21 = (bf16[2,256,512]{2,1,0:T(8,128)(2,1)S(1)}, bf16[2,256,512]{2,1,0:T(8,128)(2,1)S(1)}, u32[]{:S(2)}, u32[]{:S(2)}) collective-permute-start(bf16[2,256,512]{2,1,0:T(8,128)(2,1)S(1)} %m3x.1.refs_8_), channel_id=1, source_target_pairs={{0,16},{8,56},{16,32},{24,8},{32,48},{40,24},{48,0},{56,40},{64,80... | collective-permute-start | bytes 1572872 | tf_op jit(solution)/shard_map/last/ppermute | solution.py:301
  87.1 4.6 %collective-permute-done.21.refs_5_ = bf16[2,256,512]{2,1,0:T(8,128)(2,1)S(1)} collective-permute-done((bf16[2,256,512]{2,1,0:T(8,128)(2,1)S(1)}, bf16[2,256,512]{2,1,0:T(8,128)(2,1)S(1)}, u32[]{:S(2)}, u32[]{:S(2)}) %collective-permute-start.21) | collective-permute-done | bytes 524320 | tf_op jit(solution)/shard_map/last/ppermute | solution.py:301
  91.7 2.0 %xos.1 = (f32[1,256,512]{2,1,0:T(8,128)S(1)}, f32[1,128,512]{2,1,0:T(8,128)S(1)}, f32[1,128,512]{2,1,0:T(8,128)S(1)}) custom-call(bf16[2,128,512]{2,1,0:T(8,128)(2,1)S(1)} %collective-permute-done.4.one.refs_0_, bf16[2,128,512]{2,1,0:T(8,128)(2,1)S(1)} %collective-permute-done.6.refs_0_.refs_1_, bf16[512,8192]{1,0:T(8,128)(2,1)} %refs_2_.7, ...), custom_call_target="tpu_custom_call" | custom-call | flops 536870912 | bytes 2097152 | tf_op jit(solution)/shard_map/last/xos/pallas_call | solution.py:196
  93.7 1.9 %collective-permute-start.22 = (f32[1,128,512]{2,1,0:T(8,128)S(1)}, f32[1,128,512]{2,1,0:T(8,128)S(1)}, u32[]{:S(2)}, u32[]{:S(2)}) collective-permute-start(f32[1,128,512]{2,1,0:T(8,128)S(1)} %get-tuple-element.39), channel_id=1, source_target_pairs={{0,8},{8,0},{16,24},{24,16},{32,40},{40,32},{48,56},{56,48},{64,72... | collective-permute-start | bytes 786440 | tf_op jit(solution)/shard_map/last/ppermute | solution.py:288
  97.4 2.9 %final.1 = f32[512,1024]{1,0:T(8,128)} custom-call(s32[4,16]{1,0:T(4,128)S(1)} %copy-done.1, f32[1024,512]{1,0:T(8,128)S(1)} %gather_y.1.refs_1_, f32[1,256,512]{2,1,0:T(8,128)S(1)} %get-tuple-element.38.refs_6_.refs_2_, f32[1,128,512]{2,1,0:T(8,128)S(1)} %collective-permute-done.22.refs_3_, f32[1,128,512]{2,1,0:T(8,128)S(1)} %collective-permute-done.23.refs_4_, ...), custom_call_target="tpu_custom_call" | custom-call | flops 1000000000 | bytes 2097152 | tf_op jit(solution)/shard_map/last/final/pallas_call | solution.py:263
  (47 shorter events, 9.7 us)
Async XLA Ops:
  0.0 0.8 copy-start
  3.3 2.5 %collective-permute-start = (bf16[1,128,512]{2,1,0:T(8,128)(2,1)S(1)}, bf16[1,128,512]{2,1,0:T(8,128)(2,1)S(1)}, u32[]{:S(2)}, u32[]{:S(2)}) collective-permute-start(bf16[1,128,512]{2,1,0:T(8,128)(2,1)S(1)} %pick.1.a_ref), channel_id=1, source_target_pairs={{0,8},{8,0},{16,24},{24,16},{32,40},{40,32},{48,56},{56,48},{64,72... | collective-permute-start | bytes 393224 | tf_op jit(solution)/shard_map/panel/ppermute | solution.py:288
  5.8 13.6 %collective-permute-start.3 = (bf16[512,8192]{1,0:T(8,128)(2,1)}, bf16[512,8192]{1,0:T(8,128)(2,1)S(1)}, u32[]{:S(2)}, u32[]{:S(2)}) collective-permute-start(bf16[512,8192]{1,0:T(8,128)(2,1)} %refs_2_.7), channel_id=1, source_target_pairs={{0,8},{8,0},{16,24},{24,16},{32,40},{40,32},{48,56},{56,48},{64,72... | collective-permute-start | bytes 25165832 | tf_op jit(solution)/shard_map/panel/ppermute | solution.py:288
  6.2 9.3 %collective-permute-start.1 = (bf16[2,128,512]{2,1,0:T(8,128)(2,1)S(1)}, bf16[2,128,512]{2,1,0:T(8,128)(2,1)S(1)}, u32[]{:S(2)}, u32[]{:S(2)}) collective-permute-start(bf16[2,128,512]{2,1,0:T(8,128)(2,1)S(1)} %get-tuple-element.25), channel_id=1, source_target_pairs={{0,1},{1,0},{2,3},{3,2},{4,5},{5,4},{6,7},{7,6},{8,9},{9,8},{10,11... | collective-permute-start | bytes 786440 | tf_op jit(solution)/shard_map/panel/ppermute | solution.py:296
  9.1 10.3 %collective-permute-start.2 = (bf16[2,128,512]{2,1,0:T(8,128)(2,1)S(1)}, bf16[2,128,512]{2,1,0:T(8,128)(2,1)S(1)}, u32[]{:S(2)}, u32[]{:S(2)}) collective-permute-start(bf16[2,128,512]{2,1,0:T(8,128)(2,1)S(1)} %get-tuple-element.24.refs_0_), channel_id=1, source_target_pairs={{0,2},{1,3},{2,4},{3,5},{4,6},{5,7},{6,0},{7,1},{8,14},{9,15},{10,... | collective-permute-start | bytes 786440 | tf_op jit(solution)/shard_map/panel/ppermute | solution.py:289
  15.6 9.5 %collective-permute-start.4 = (bf16[2,128,512]{2,1,0:T(8,128)(2,1)S(1)}, bf16[2,128,512]{2,1,0:T(8,128)(2,1)S(1)}, u32[]{:S(2)}, u32[]{:S(2)}) collective-permute-start(bf16[2,128,512]{2,1,0:T(8,128)(2,1)S(1)} %collective-permute-done.1.refs_1_), channel_id=1, source_target_pairs={{0,2},{1,3},{2,4},{3,5},{4,6},{5,7},{6,0},{7,1},{8,14},{9,15},{10,... | collective-permute-start | bytes 786440 | tf_op jit(solution)/shard_map/panel/ppermute | solution.py:289
  22.3 16.5 %collective-permute-start.7 = (bf16[2,256,512]{2,1,0:T(8,128)(2,1)S(1)}, bf16[2,256,512]{2,1,0:T(8,128)(2,1)S(1)}, u32[]{:S(2)}, u32[]{:S(2)}) collective-permute-start(bf16[2,256,512]{2,1,0:T(8,128)(2,1)S(1)} %get-tuple-element.27.after), channel_id=1, source_target_pairs={{0,16},{8,56},{16,32},{24,8},{32,48},{40,24},{48,0},{56,40},{64,80... | collective-permute-start | bytes 1572872 | tf_op jit(solution)/shard_map/y_then_x/ppermute | solution.py:301
  25.1 13.7 %collective-permute-start.8 = (bf16[2,256,512]{2,1,0:T(8,128)(2,1)S(1)}, bf16[2,256,512]{2,1,0:T(8,128)(2,1)S(1)}, u32[]{:S(2)}, u32[]{:S(2)}) collective-permute-start(bf16[2,256,512]{2,1,0:T(8,128)(2,1)S(1)} %get-tuple-element.29), channel_id=1, source_target_pairs={{0,48},{8,24},{16,0},{24,40},{32,16},{40,56},{48,32},{56,8},{64,11... | collective-permute-start | bytes 1572872 | tf_op jit(solution)/shard_map/y_then_x/ppermute | solution.py:302
  25.1 13.6 %collective-permute-start.6 = (bf16[2,128,512]{2,1,0:T(8,128)(2,1)S(1)}, bf16[2,128,512]{2,1,0:T(8,128)(2,1)S(1)}, u32[]{:S(2)}, u32[]{:S(2)}) collective-permute-start(bf16[2,128,512]{2,1,0:T(8,128)(2,1)S(1)} %choose.1.refs_3_), channel_id=1, source_target_pairs={{0,2},{1,3},{2,4},{3,5},{4,6},{5,7},{6,0},{7,1},{8,14},{9,15},{10,... | collective-permute-start | bytes 786440 | tf_op jit(solution)/shard_map/x_then_y_send/ppermute | solution.py:289
  31.9 24.5 %collective-permute-start.12 = (bf16[6,128,512]{2,1,0:T(8,128)(2,1)S(1)}, bf16[6,128,512]{2,1,0:T(8,128)(2,1)S(1)}, u32[]{:S(2)}, u32[]{:S(2)}) collective-permute-start(bf16[6,128,512]{2,1,0:T(8,128)(2,1)S(1)} %xe.1.refs_5_), channel_id=1, source_target_pairs={{0,64},{8,72},{16,80},{24,88},{32,96},{40,104},{48,112},{56,120},{... | collective-permute-start | bytes 2359304 | tf_op jit(solution)/shard_map/x_then_y_send/ppermute | solution.py:303
  36.0 14.4 %collective-permute-start.5 = (bf16[2,256,512]{2,1,0:T(8,128)(2,1)S(1)}, bf16[2,256,512]{2,1,0:T(8,128)(2,1)S(1)}, u32[]{:S(2)}, u32[]{:S(2)}) collective-permute-start(bf16[2,256,512]{2,1,0:T(8,128)(2,1)S(1)} %get-tuple-element.28.refs_3_), channel_id=1, source_target_pairs={{0,16},{8,56},{16,32},{24,8},{32,48},{40,24},{48,0},{56,40},{64,80... | collective-permute-start | bytes 1572872 | tf_op jit(solution)/shard_map/y_then_x/ppermute | solution.py:301
  38.8 15.1 %collective-permute-start.9 = (bf16[2,256,512]{2,1,0:T(8,128)(2,1)S(1)}, bf16[2,256,512]{2,1,0:T(8,128)(2,1)S(1)}, u32[]{:S(2)}, u32[]{:S(2)}) collective-permute-start(bf16[2,256,512]{2,1,0:T(8,128)(2,1)S(1)} %get-tuple-element.30), channel_id=1, source_target_pairs={{0,48},{8,24},{16,0},{24,40},{32,16},{40,56},{48,32},{56,8},{64,11... | collective-permute-start | bytes 1572872 | tf_op jit(solution)/shard_map/y_then_x/ppermute | solution.py:302
  41.2 21.5 %collective-permute-start.13 = (bf16[4,128,512]{2,1,0:T(8,128)(2,1)S(1)}, bf16[4,128,512]{2,1,0:T(8,128)(2,1)S(1)}, u32[]{:S(2)}, u32[]{:S(2)}) collective-permute-start(bf16[4,128,512]{2,1,0:T(8,128)(2,1)S(1)} %xl.1.refs_6_), channel_id=1, source_target_pairs={{0,64},{8,72},{16,80},{24,88},{32,96},{40,104},{48,112},{56,120},{... | collective-permute-start | bytes 1572872 | tf_op jit(solution)/shard_map/x_then_y_send/ppermute | solution.py:303
  43.5 24.9 %collective-permute-start.11 = (bf16[2,256,512]{2,1,0:T(8,128)(2,1)S(1)}, bf16[2,256,512]{2,1,0:T(8,128)(2,1)S(1)}, u32[]{:S(2)}, u32[]{:S(2)}) collective-permute-start(bf16[2,256,512]{2,1,0:T(8,128)(2,1)S(1)} %m3y.2.refs_4_), channel_id=1, source_target_pairs={{0,16},{8,56},{16,32},{24,8},{32,48},{40,24},{48,0},{56,40},{64,80... | collective-permute-start | bytes 1572872 | tf_op jit(solution)/shard_map/y_then_x/ppermute | solution.py:301
  55.8 14.6 %collective-permute-start.10 = (bf16[2,256,512]{2,1,0:T(8,128)(2,1)S(1)}, bf16[2,256,512]{2,1,0:T(8,128)(2,1)S(1)}, u32[]{:S(2)}, u32[]{:S(2)}) collective-permute-start(bf16[2,256,512]{2,1,0:T(8,128)(2,1)S(1)} %m3y.3.refs_6_), channel_id=1, source_target_pairs={{0,16},{8,56},{16,32},{24,8},{32,48},{40,24},{48,0},{56,40},{64,80... | collective-permute-start | bytes 1572872 | tf_op jit(solution)/shard_map/y_then_x/ppermute | solution.py:301
  56.1 23.0 %collective-permute-start.18 = (bf16[6,128,512]{2,1,0:T(8,128)(2,1)S(1)}, bf16[6,128,512]{2,1,0:T(8,128)(2,1)S(1)}, u32[]{:S(2)}, u32[]{:S(2)}) collective-permute-start(bf16[6,128,512]{2,1,0:T(8,128)(2,1)S(1)} %x3.1.refs_6_), channel_id=1, source_target_pairs={{0,64},{8,72},{16,80},{24,88},{32,96},{40,104},{48,112},{56,120},{... | collective-permute-start | bytes 2359304 | tf_op jit(solution)/shard_map/y_then_x/ppermute | solution.py:303
  65.5 14.5 %collective-permute-start.19 = (bf16[2,256,512]{2,1,0:T(8,128)(2,1)S(1)}, bf16[2,256,512]{2,1,0:T(8,128)(2,1)S(1)}, u32[]{:S(2)}, u32[]{:S(2)}) collective-permute-start(bf16[2,256,512]{2,1,0:T(8,128)(2,1)S(1)} %get-tuple-element.31.refs_7_), channel_id=1, source_target_pairs={{0,16},{8,56},{16,32},{24,8},{32,48},{40,24},{48,0},{56,40},{64,80... | collective-permute-start | bytes 1572872 | tf_op jit(solution)/shard_map/x_then_y/ppermute | solution.py:301
  68.4 12.0 %collective-permute-start.20 = (bf16[2,256,512]{2,1,0:T(8,128)(2,1)S(1)}, bf16[2,256,512]{2,1,0:T(8,128)(2,1)S(1)}, u32[]{:S(2)}, u32[]{:S(2)}) collective-permute-start(bf16[2,256,512]{2,1,0:T(8,128)(2,1)S(1)} %get-tuple-element.37), channel_id=1, source_target_pairs={{0,48},{8,24},{16,0},{24,40},{32,16},{40,56},{48,32},{56,8},{64,11... | collective-permute-start | bytes 1572872 | tf_op jit(solution)/shard_map/x_then_y/ppermute | solution.py:302
  72.4 1.6 %collective-permute-start.14 = (f32[1,128,512]{2,1,0:T(8,128)S(1)}, f32[1,128,512]{2,1,0:T(8,128)S(1)}, u32[]{:S(2)}, u32[]{:S(2)}) collective-permute-start(f32[1,128,512]{2,1,0:T(8,128)S(1)} %get-tuple-element.34), channel_id=1, source_target_pairs={{0,8},{8,0},{16,24},{24,16},{32,40},{40,32},{48,56},{56,48},{64,72... | collective-permute-start | bytes 786440 | tf_op jit(solution)/shard_map/last/ppermute | solution.py:288
  72.5 1.9 %collective-permute-start.15 = (f32[1,128,512]{2,1,0:T(8,128)S(1)}, f32[1,128,512]{2,1,0:T(8,128)S(1)}, u32[]{:S(2)}, u32[]{:S(2)}) collective-permute-start(f32[1,128,512]{2,1,0:T(8,128)S(1)} %get-tuple-element.35), channel_id=1, source_target_pairs={{0,8},{8,0},{16,24},{24,16},{32,40},{40,32},{48,56},{56,48},{64,72... | collective-permute-start | bytes 786440 | tf_op jit(solution)/shard_map/last/ppermute | solution.py:288
  80.4 5.2 %copy-start.4 = (s32[8,2]{0,1:T(2,128)S(1)}, s32[8,2]{0,1:T(2,128)}, u32[]{:S(2)}) copy-start(s32[8,2]{0,1:T(2,128)} %param.8) | copy-start | bytes 196
  80.4 5.2 %copy-start.2 = (f32[4096]{0:T(1024)S(1)}, f32[4096]{0:T(1024)}, u32[]{:S(2)}) copy-start(f32[4096]{0:T(1024)} %param.9) | copy-start | bytes 49156
  80.4 5.2 %copy-start.3 = (f32[4096]{0:T(1024)S(1)}, f32[4096]{0:T(1024)}, u32[]{:S(2)}) copy-start(f32[4096]{0:T(1024)} %param.10) | copy-start | bytes 49156
  82.5 9.2 %collective-permute-start.21 = (bf16[2,256,512]{2,1,0:T(8,128)(2,1)S(1)}, bf16[2,256,512]{2,1,0:T(8,128)(2,1)S(1)}, u32[]{:S(2)}, u32[]{:S(2)}) collective-permute-start(bf16[2,256,512]{2,1,0:T(8,128)(2,1)S(1)} %m3x.1.refs_8_), channel_id=1, source_target_pairs={{0,16},{8,56},{16,32},{24,8},{32,48},{40,24},{48,0},{56,40},{64,80... | collective-permute-start | bytes 1572872 | tf_op jit(solution)/shard_map/last/ppermute | solution.py:301
  85.9 9.9 %collective-permute-start.16 = (bf16[1,256,512]{2,1,0:T(8,128)(2,1)S(1)}, bf16[1,256,512]{2,1,0:T(8,128)(2,1)S(1)}, u32[]{:S(2)}, u32[]{:S(2)}) collective-permute-start(bf16[1,256,512]{2,1,0:T(8,128)(2,1)S(1)} %get-tuple-element.32.refs_7_), channel_id=1, source_target_pairs={{0,64},{8,72},{16,80},{24,88},{32,96},{40,104},{48,112},{56,120},{... | collective-permute-start | bytes 786440 | tf_op jit(solution)/shard_map/x_then_y/ppermute | solution.py:303
  87.1 9.3 %copy-start.1 = (s32[4,16]{1,0:T(4,128)S(1)}, s32[4,16]{1,0:T(4,128)}, u32[]{:S(2)}) copy-start(s32[4,16]{1,0:T(4,128)} %refs_0_.3) | copy-start | bytes 772
  87.1 9.3 %collective-permute-start.17 = (bf16[1,256,512]{2,1,0:T(8,128)(2,1)S(1)}, bf16[1,256,512]{2,1,0:T(8,128)(2,1)S(1)}, u32[]{:S(2)}, u32[]{:S(2)}) collective-permute-start(bf16[1,256,512]{2,1,0:T(8,128)(2,1)S(1)} %get-tuple-element.36), channel_id=1, source_target_pairs={{0,72},{8,64},{16,88},{24,80},{32,104},{40,96},{48,120},{56,112},{... | collective-permute-start | bytes 786440 | tf_op jit(solution)/shard_map/x_then_y/ppermute | solution.py:375
  93.7 3.6 %collective-permute-start.22 = (f32[1,128,512]{2,1,0:T(8,128)S(1)}, f32[1,128,512]{2,1,0:T(8,128)S(1)}, u32[]{:S(2)}, u32[]{:S(2)}) collective-permute-start(f32[1,128,512]{2,1,0:T(8,128)S(1)} %get-tuple-element.39), channel_id=1, source_target_pairs={{0,8},{8,0},{16,24},{24,16},{32,40},{40,32},{48,56},{56,48},{64,72... | collective-permute-start | bytes 786440 | tf_op jit(solution)/shard_map/last/ppermute | solution.py:288
  95.6 1.8 %collective-permute-start.23 = (f32[1,128,512]{2,1,0:T(8,128)S(1)}, f32[1,128,512]{2,1,0:T(8,128)S(1)}, u32[]{:S(2)}, u32[]{:S(2)}) collective-permute-start(f32[1,128,512]{2,1,0:T(8,128)S(1)} %get-tuple-element.40), channel_id=1, source_target_pairs={{0,8},{8,0},{16,24},{24,16},{32,40},{40,32},{48,56},{56,48},{64,72... | collective-permute-start | bytes 786440 | tf_op jit(solution)/shard_map/last/ppermute | solution.py:288
